TPU v7x, 128 devices: a whole 4x4x4 slice. The times are simulated.
128 devices in a mesh: lat: 8 (over y_hi, z), lon: 16 (over x, y_lo, core).
Axes of the slice: x: 4, y: 4 (y_hi: 2, y_lo: 2; y = y_hi * 2 + y_lo), z: 4, core: 2. Of those that a mesh axis runs over, the one named last changes fastest.
Arguments:
- tokens: bfloat16 [192, 768, 512], P('lat', 'lon'), may hold values from -8 to 8
- lat_band: int32 [192], replicated, may hold values from 0 to 15, as said below
- gain_attn: float32 [512], replicated, may hold values from 0.1 to 1.9
- w_qkv: bfloat16 [512, 1536], replicated, may hold values from -1.5 to 1.5
- w_out: bfloat16 [512, 512], replicated, may hold values from -0.25 to 0.25
- gain_merge: float32 [2048], replicated, may hold values from 0.1 to 1.9
- w_merge: bfloat16 [2048, 1024], replicated, may hold values from -0.125 to 0.125
- grad_merged: bfloat16 [96, 384, 1024], P('lat', 'lon'), may hold values from -6 to 6
Outputs:
- merged: bfloat16 [96, 384, 1024], P('lat', 'lon')
- grad_tokens: float32 [192, 768, 512], P('lat', 'lon')
- grad_gain_attn: float32 [512], replicated
- grad_w_qkv: float32 [512, 1536], replicated
- grad_w_out: float32 [512, 512], replicated
- grad_gain_merge: float32 [2048], replicated
- grad_w_merge: float32 [2048, 1024], replicated
Inputs may be any that keep to these rules, and one draw needn't show every extreme that they name: `lat_band`: band number of each latitude row; it never falls from one row to the next, and every band holds at least one row.
All inputs are finite; a program needn't handle non-finite values.
Results may differ from a plain program's by a relative error of at most 0.025.
Values may be sent and summed in bfloat16 or wider, within the bound.
A program may use at most 192 MiB of HBM per device.

v0:
```python
import jax
import jax.numpy as jnp
from jax import lax
from jax.sharding import PartitionSpec as P

HEADS = 8
WLAT = 6
WLON = 12


EPSILON = 1e-05


def shifted_2(value, axis, steps):
    count = lax.axis_size(axis)
    pairs = [(source, (source + steps) % count) for source in range(count)]
    return lax.ppermute(value, axis, pairs)


def as_sent(shard):
    return jax.tree.map(lambda a: a.astype(jnp.bfloat16) if a.dtype == jnp.float32 else a, shard)


def normalize(values, gain_vec):
    average = jnp.mean(values, axis=-1, keepdims=True)
    centered = values - average
    variance = jnp.mean(centered * centered, axis=-1, keepdims=True)
    return centered * lax.rsqrt(variance + EPSILON) * gain_vec


def windows_attend(qkv_grid, band_rows, head_count):
    grid_rows, grid_cols, triple = qkv_grid.shape
    features = triple // 3
    head_size = features // head_count
    count_a = grid_rows // WLAT
    count_b = grid_cols // WLON
    window_size = WLAT * WLON
    blocks = qkv_grid.reshape(count_a, WLAT, count_b, WLON, triple).transpose(0, 2, 1, 3, 4)
    blocks = blocks.reshape(count_a, count_b, window_size, triple)
    queries = blocks[:, :, :, :features].reshape(
        count_a, count_b, window_size, head_count, head_size
    )
    key_rows = blocks[:, :, :, features : 2 * features].reshape(
        count_a, count_b, window_size, head_count, head_size
    )
    value_rows = blocks[:, :, :, 2 * features :].reshape(
        count_a, count_b, window_size, head_count, head_size
    )
    scores = jnp.einsum("abqhd,abkhd->abhqk", queries, key_rows, preferred_element_type=jnp.float32)
    scores = scores * head_size ** (-0.5)
    labels = jnp.repeat(band_rows.reshape(count_a, WLAT), WLON, axis=1)
    allowed = labels[:, :, None] == labels[:, None, :]
    scores = jnp.where(allowed[:, None, None, :, :], scores, -1e30)
    attn_weights = jax.nn.softmax(scores, axis=-1).astype(jnp.bfloat16)
    attn_out = jnp.einsum(
        "abhqk,abkhd->abqhd", attn_weights, value_rows, preferred_element_type=jnp.float32
    )
    attn_out = attn_out.astype(jnp.bfloat16).reshape(count_a, count_b, WLAT, WLON, features)
    return attn_out.transpose(0, 2, 1, 3, 4).reshape(grid_rows, grid_cols, features)


def merge_groups(mixed_tokens):
    grid_rows, grid_cols, features = mixed_tokens.shape
    grouped = mixed_tokens.reshape(grid_rows // 2, 2, grid_cols // 2, 2, features).transpose(
        0, 2, 3, 1, 4
    )
    return grouped.reshape(grid_rows // 2, grid_cols // 2, 4 * features)


def on_device(tokens, lat_band, gain_attn, w_qkv, w_out, gain_merge, w_merge, grad_merged):
    tile_rows, tile_cols, features = tokens.shape
    half_lat = WLAT // 2
    half_lon = WLON // 2
    west_cols = shifted_2(tokens[:, tile_cols - half_lon :], "lon", 1)
    shifted = jnp.concatenate([west_cols, tokens[:, : tile_cols - half_lon]], axis=1)
    south_rows = shifted_2(shifted[tile_rows - half_lat :], "lat", 1)
    shifted = jnp.concatenate([south_rows, shifted[: tile_rows - half_lat]], axis=0)
    band_count = lat_band.shape[0]
    extended = jnp.concatenate([lat_band[band_count - half_lat :], lat_band])
    band_rows = lax.dynamic_slice_in_dim(extended, lax.axis_index("lat") * tile_rows, tile_rows)

    def section_one(values, gain_vec):
        return normalize(values, gain_vec).astype(jnp.bfloat16)

    normed, first_back = jax.vjp(section_one, shifted.astype(jnp.float32), gain_attn)
    flat_normed = normed.reshape(-1, features)
    qkv_grid = jnp.dot(flat_normed, w_qkv, preferred_element_type=jnp.float32).astype(jnp.bfloat16)
    qkv_grid = qkv_grid.reshape(tile_rows, tile_cols, 3 * features)

    def section_two(values):
        return windows_attend(values, band_rows, HEADS)

    attended, second_back = jax.vjp(section_two, qkv_grid)
    north_rows = shifted_2(attended[:half_lat], "lat", -1)
    back_frame = jnp.concatenate([attended[half_lat:], north_rows], axis=0)
    east_cols = shifted_2(back_frame[:, :half_lon], "lon", -1)
    own_att = jnp.concatenate([back_frame[:, half_lon:], east_cols], axis=1)
    flat_att = own_att.reshape(-1, features)
    projected = jnp.dot(flat_att, w_out, preferred_element_type=jnp.float32).reshape(
        tile_rows, tile_cols, features
    )
    mixed_tokens = (tokens.astype(jnp.float32) + projected).astype(jnp.bfloat16)

    def section_three(values, gain_vec):
        return normalize(merge_groups(values).astype(jnp.float32), gain_vec).astype(jnp.bfloat16)

    merged_in, third_back = jax.vjp(section_three, mixed_tokens, gain_merge)
    flat_in = merged_in.reshape(-1, 4 * features)
    flat_grad = grad_merged.reshape(-1, grad_merged.shape[2])
    merged = (
        jnp.dot(flat_in, w_merge, preferred_element_type=jnp.float32)
        .astype(jnp.bfloat16)
        .reshape(grad_merged.shape)
    )
    grad_w_merge = jnp.dot(flat_in.T, flat_grad, preferred_element_type=jnp.float32)
    grad_in = (
        jnp.dot(flat_grad, w_merge.T, preferred_element_type=jnp.float32)
        .astype(jnp.bfloat16)
        .reshape(merged_in.shape)
    )
    grad_mixed, grad_gain_merge = third_back(grad_in)
    flat_mixed = grad_mixed.reshape(-1, features)
    grad_w_out = jnp.dot(flat_att.T, flat_mixed, preferred_element_type=jnp.float32)
    grad_att = jnp.dot(flat_mixed, w_out.T, preferred_element_type=jnp.float32).astype(jnp.bfloat16)
    grad_att = grad_att.reshape(tile_rows, tile_cols, features)
    to_east = shifted_2(grad_att[:, tile_cols - half_lon :], "lon", 1)
    grad_back = jnp.concatenate([to_east, grad_att[:, : tile_cols - half_lon]], axis=1)
    to_north = shifted_2(grad_back[tile_rows - half_lat :], "lat", 1)
    grad_shifted = jnp.concatenate([to_north, grad_back[: tile_rows - half_lat]], axis=0)
    (grad_qkv,) = second_back(grad_shifted)
    flat_qkv = grad_qkv.reshape(-1, 3 * features)
    grad_w_qkv = jnp.dot(flat_normed.T, flat_qkv, preferred_element_type=jnp.float32)
    grad_normed = jnp.dot(flat_qkv, w_qkv.T, preferred_element_type=jnp.float32).astype(
        jnp.bfloat16
    )
    grad_inputs, grad_gain_attn = first_back(grad_normed.reshape(tile_rows, tile_cols, features))
    upper_rows = shifted_2(grad_inputs[:half_lat].astype(jnp.bfloat16), "lat", -1).astype(
        jnp.float32
    )
    own_frame = jnp.concatenate([grad_inputs[half_lat:], upper_rows], axis=0)
    right_cols = shifted_2(as_sent(own_frame[:, :half_lon]), "lon", -1)
    own_frame = jnp.concatenate([own_frame[:, half_lon:], right_cols], axis=1)
    grad_tokens = own_frame + grad_mixed.astype(jnp.float32)
    grad_gain_attn, grad_w_qkv, grad_w_out, grad_gain_merge, grad_w_merge = lax.psum(
        (grad_gain_attn, grad_w_qkv, grad_w_out, grad_gain_merge, grad_w_merge), ("lat", "lon")
    )
    return (
        merged,
        grad_tokens,
        grad_gain_attn,
        grad_w_qkv,
        grad_w_out,
        grad_gain_merge,
        grad_w_merge,
    )


def solution(mesh):
    return jax.shard_map(
        on_device,
        mesh=mesh,
        in_specs=(P("lat", "lon", None), P(), P(), P(), P(), P(), P(), P("lat", "lon", None)),
        out_specs=(P("lat", "lon", None), P("lat", "lon", None), P(), P(), P(), P(), P()),
        check_vma=False,
    )
```

profile of v0, /device:TPU:1, one launch (start us, length us, event | category | flops | bytes accessed | tf_op | source)
XLA Modules:
  0.0 426.9 jit_solution(17404584500663782681)
XLA Ops:
  16.5 6.9 %collective-permute-done.1 = bf16[3,48,512]{2,1,0:T(8,128)(2,1)S(1)} collective-permute-done((bf16[3,48,512]{2,1,0:T(8,128)(2,1)S(1)}, bf16[3,48,512]{2,1,0:T(8,128)(2,1)S(1)}, u32[]{:S(2)}, u32[]{:S(2)}) %collective-permute-start.1) | collective-permute-done | bytes 147488 | tf_op jit(solution)/shard_map/ppermute | solution.py:17
  28.9 6.6 %reshape_reshape.3 = bf16[4,6,4,12,1536]{4,3,2,1,0:T(8,128)(2,1)} reshape(bf16[1152,1536]{1,0:T(8,128)(2,1)} %convolution_convert_fusion) | data formatting | bytes 7077888 | tf_op jit(solution)/shard_map/jvp()/reshape;reshape | solution.py:38
  35.4 5.5 %copy.128 = bf16[4,4,6,12,1536]{4,1,3,2,0:T(4,128)(2,1)S(1)} copy(bf16[4,4,6,12,1536]{4,3,1,2,0:T(8,128)(2,1)} %bitcast.103) | data formatting | bytes 7077888 | tf_op jit(solution)/shard_map/jvp()/transpose | solution.py:38
  43.7 4.1 copy.131
  47.7 4.1 copy.130
  51.8 4.1 copy.129
  55.9 6.5 %fusion.49 = (f32[4,4,8,72]{3,2,1,0:T(8,128)S(1)}, f32[4,4,8,72,72]{3,4,2,1,0:T(8,128)}) fusion(pred[4,72,72]{1,2,0:T(8,128)(4,1)S(1)} %broadcast_compare_fusion, bf16[4,4,72,8,64]{2,4,3,1,0:T(8,128)(2,1)} %bitcast.120, bf16[4,4,72,8,64]{2,4,3,1,0:T(8,128)(2,1)} %bitcast.122), kind=kOutput, calls=%fused_computation.101 | convolution fusion | flops 87588936 | bytes 5071104 | tf_op jit(solution)/shard_map/jvp()/sub | solution.py:54
  62.4 5.1 %convert_bitcast_fusion = bf16[4,4,72,8,64]{2,4,3,1,0:T(8,128)(2,1)} fusion(bf16[4,4,72,8,64]{2,4,3,1,0:T(8,128)(2,1)} %bitcast.110, f32[4,4,8,72,72]{3,4,2,1,0:T(8,128)} %get-tuple-element.30, f32[4,4,8,72]{3,2,1,0:T(8,128)S(1)} %get-tuple-element.29), kind=kOutput, calls=%fused_computation.53 | convolution fusion | flops 86851584 | bytes 5050368 | tf_op jit(solution)/shard_map/jvp(abhqk,abkhd->abqhd)/dot_general | solution.py:55
  67.5 5.5 %copy.133 = bf16[4,4,72,8,64]{4,3,1,2,0:T(8,128)(2,1)} copy(bf16[4,4,72,8,64]{2,4,3,1,0:T(8,128)(2,1)} %convert_bitcast_fusion) | data formatting | bytes 2359296 | tf_op jit(solution)/shard_map/jvp()/convert_element_type | solution.py:58
  73.1 4.4 %reshape.312 = bf16[4,4,6,12,512]{4,1,3,2,0:T(4,128)(2,1)} reshape(bf16[4,4,72,8,64]{4,3,1,2,0:T(8,128)(2,1)} %copy.133) | data formatting | bytes 2359296 | tf_op jit(solution)/shard_map/jvp()/reshape | solution.py:58
  86.3 5.2 %fusion.9 = f32[288,2048]{1,0:T(8,128)} fusion(bf16[288,1024]{1,0:T(8,128)(2,1)} %bitcast.130, bf16[2048,1024]{1,0:T(8,128)(2,1)} %param.14), kind=kOutput, calls=%fused_computation.24 | convolution fusion | flops 1209139200 | bytes 7143424 | tf_op jit(solution)/shard_map/dot_general | solution.py:117
  91.5 4.2 reshape.328
  97.1 5.2 %collective-permute-start.3 = (bf16[24,6,512]{2,1,0:T(8,128)(2,1)S(1)}, bf16[24,6,512]{2,1,0:T(8,128)(2,1)S(1)}, u32[]{:S(2)}, u32[]{:S(2)}) collective-permute-start(bf16[24,6,512]{2,1,0:T(8,128)(2,1)S(1)} %pad_maximum_fusion.4), channel_id=1, source_target_pairs={{0,15},{1,0},{2,1},{3,2},{4,3},{5,4},{6,5},{7,6},{8,7},{9,8},{10,9... | collective-permute-start | bytes 442376 | tf_op jit(solution)/shard_map/ppermute | solution.py:17
  124.7 4.2 reshape.327
  128.9 4.2 reshape.331
  149.6 6.0 %convolution_bitcast_fusion = f32[2048,1024]{1,0:T(8,128)} fusion(bf16[12,24,1024]{2,1,0:T(8,128)(2,1)S(1)} %copy-done.33, f32[12,24,2048]{2,1,0:T(8,128)S(1)} %copy-done.12, f32[2048]{0:T(1024)S(1)} %copy-done.24, f32[12,24]{1,0:T(8,128)S(1)} %fusion.42, f32[12,24]{1,0:T(8,128)S(1)} %broadcast_multiply_fusion.1), kind=kOutput, calls=%fused_computation.13 | convolution fusion | flops 1210318848 | bytes 11348224 | tf_op jit(solution)/shard_map/dot_general | solution.py:115
  157.6 5.7 %collective-permute-done.5 = bf16[3,48,512]{2,1,0:T(8,128)(2,1)S(1)} collective-permute-done((bf16[3,48,512]{2,1,0:T(8,128)(2,1)S(1)}, bf16[3,48,512]{2,1,0:T(8,128)(2,1)S(1)}, u32[]{:S(2)}, u32[]{:S(2)}) %collective-permute-start.5) | collective-permute-done | bytes 147488 | tf_op jit(solution)/shard_map/ppermute | solution.py:17
  171.5 4.1 reshape.319
  175.7 5.0 %copy.141 = bf16[4,4,72,8,64]{2,4,3,1,0:T(8,128)(2,1)} copy(bf16[4,4,72,8,64]{4,3,1,2,0:T(8,128)(2,1)} %reshape.319) | data formatting | bytes 2359296 | tf_op jit(solution)/shard_map/transpose(jvp())/reshape | solution.py:58
  180.7 5.3 %fusion.6 = (f32[4,4,8,72]{3,2,1,0:T(8,128)S(1)}, bf16[4,4,8,72,72]{3,4,2,1,0:T(8,128)(2,1)S(1)}) fusion(f32[4,4,8,72,72]{3,4,2,1,0:T(8,128)} %get-tuple-element.30, f32[4,4,8,72]{3,2,1,0:T(8,128)S(1)} %multiply_divide_fusion, bf16[4,4,72,8,64]{2,4,3,1,0:T(8,128)(2,1)} %bitcast.111, bf16[4,4,72,8,64]{2,4,3,1,0:T(8,128)(2,1)} %copy.141), kind=kOutput, calls=%fused_computation.9 | convolution fusion | flops 88243200 | bytes 6414336 | tf_op jit(solution)/shard_map/transpose(jvp(abhqk,abkhd->abqhd))/dot_general | solution.py:55
  194.5 4.1 copy.143
  198.6 4.1 copy.145
  202.7 4.1 copy.147
  213.7 6.8 %reshape.324 = bf16[1152,1536]{1,0:T(8,128)(2,1)} reshape(bf16[4,6,4,12,1536]{4,3,2,1,0:T(8,128)(2,1)} %copy.148) | data formatting | bytes 7077888 | tf_op jit(solution)/shard_map/reshape;transpose(jvp())/reshape | solution.py:131
  220.4 5.6 %multiply_reduce_fusion.2 = (f32[1152]{0:T(1024)S(1)}, f32[1152,512]{1,0:T(8,128)}) fusion(bf16[24,48,512]{2,1,0:T(8,128)(2,1)S(1)} %get-tuple-element.17, f32[512]{0:T(512)S(1)} %copy-done.28, f32[1152]{0:T(1024)S(1)} %div.77, bf16[1152,1536]{1,0:T(8,128)(2,1)} %reshape.324, bf16[512,1536]{1,0:T(8,128)(2,1)S(1)} %copy-done), kind=kOutput, calls=%fused_computation.38 | convolution fusion | flops 1816066944 | bytes 8662016 | tf_op jit(solution)/shard_map/dot_general | solution.py:133
  232.5 3.9 fusion.52
  237.5 5.2 %convolution_convert_fusion.6 = bf16[288,1024]{1,0:T(8,128)(2,1)} fusion(bf16[2048,1024]{1,0:T(8,128)(2,1)} %param.14, f32[288,2048]{1,0:T(8,128)} %reshape.327, f32[2048]{0:T(1024)S(1)} %copy-done.25, f32[288]{0:T(512)S(1)} %copy-done.32, f32[288]{0:T(512)S(1)} %copy-done.30), kind=kOutput, calls=%fused_computation.60 | convolution fusion | flops 1210613760 | bytes 7153920 | tf_op jit(solution)/shard_map/dot_general | solution.py:111
  245.1 4.3 %reshape.330 = f32[24,48,512]{2,1,0:T(8,128)} reshape(f32[12,2,24,2,512]{4,3,2,1,0:T(2,128)} %copy.149) | data formatting | bytes 4718592 | tf_op jit(solution)/shard_map/convert_element_type | solution.py:143
  252.6 67.9 %all-reduce.3 = (f32[512]{0:T(512)}, f32[2048]{0:T(1024)}) all-reduce(f32[512]{0:T(512)S(1)} %get-tuple-element.9, f32[2048]{0:T(1024)S(1)} %bitcast.128), channel_id=1, replica_groups=mesh['lat'=8,'lon'=16] {'lat','lon'}, use_global_device_ids=true, to_apply=%region_12.13 | all-reduce | flops 2560 | bytes 20480 | tf_op jit(solution)/shard_map/psum | solution.py:144
  322.8 4.0 collective-permute-done.7
  328.9 77.6 %all-reduce.7.cloned.1.call-done = (f32[512,1536]{1,0:T(8,128)}, f32[512,512]{1,0:T(8,128)}, f32[2048,1024]{1,0:T(8,128)}) async-done(((f32[512,1536]{1,0:T(8,128)}, f32[512,512]{1,0:T(8,128)}, f32[2048,1024]{1,0:T(8,128)}), (f32[512,1536]{1,0:T(8,128)}, f32[512,512]{1,0:T(8,128)}, f32[2048,1024]{1,0:T(8,128)})) %all-reduce.7.cloned.1.call-update) | async-done | bytes 12582928 | tf_op jit(solution)/shard_map/psum | solution.py:144
  411.4 8.4 %copy.187 = f32[2048,1024]{1,0:T(8,128)} copy(f32[2048,1024]{1,0:T(8,128)} %get-tuple-element.41) | data formatting | bytes 16777216
  (168 shorter events, 114.1 us)
Async XLA Ops:
  7.2 17.9 %copy-start = (bf16[512,1536]{1,0:T(8,128)(2,1)S(1)}, bf16[512,1536]{1,0:T(8,128)(2,1)}, u32[]{:S(2)}) copy-start(bf16[512,1536]{1,0:T(8,128)(2,1)} %param.11) | copy-start | bytes 4718596
  7.2 399.4 %all-reduce.7.cloned.1.call-start = ((), (), s32[]{:S(2)}) async-start(), calls=%async_computation | async-start | bytes 25165824 | tf_op jit(solution)/shard_map/psum | solution.py:144
  8.3 5.4 %collective-permute-start = (bf16[24,6,512]{2,1,0:T(8,128)(2,1)S(1)}, bf16[24,6,512]{2,1,0:T(8,128)(2,1)S(1)}, u32[]{:S(2)}, u32[]{:S(2)}) collective-permute-start(bf16[24,6,512]{2,1,0:T(8,128)(2,1)S(1)} %slice.62), channel_id=1, source_target_pairs={{0,1},{1,2},{2,3},{3,4},{4,5},{5,6},{6,7},{7,8},{8,9},{9,10},{10,1... | collective-permute-start | bytes 442376 | tf_op jit(solution)/shard_map/ppermute | solution.py:17
  12.9 10.5 %copy-start.3 = (bf16[24,48,512]{2,1,0:T(8,128)(2,1)S(1)}, bf16[24,48,512]{2,1,0:T(8,128)(2,1)}, u32[]{:S(2)}) copy-start(bf16[24,48,512]{2,1,0:T(8,128)(2,1)} %param.8) | copy-start | bytes 3538948
  14.6 10.0 %copy-start.27 = (f32[512]{0:T(512)S(1)}, f32[512]{0:T(512)}, u32[]{:S(2)}) copy-start(f32[512]{0:T(512)} %param.10) | copy-start | bytes 6148
  14.7 8.7 %collective-permute-start.1 = (bf16[3,48,512]{2,1,0:T(8,128)(2,1)S(1)}, bf16[3,48,512]{2,1,0:T(8,128)(2,1)S(1)}, u32[]{:S(2)}, u32[]{:S(2)}) collective-permute-start(bf16[3,48,512]{2,1,0:T(8,128)(2,1)S(1)} %pad_maximum_fusion.6), channel_id=1, source_target_pairs={{0,16},{16,32},{32,48},{48,64},{64,80},{80,96},{96,112},{112,0},{1... | collective-permute-start | bytes 442376 | tf_op jit(solution)/shard_map/ppermute | solution.py:17
  16.5 39.5 %copy-start.20 = (pred[4,72,72]{1,2,0:T(8,128)(4,1)}, pred[4,72,72]{1,2,0:T(8,128)(4,1)S(1)}, u32[]{:S(2)}) copy-start(pred[4,72,72]{1,2,0:T(8,128)(4,1)S(1)} %broadcast_compare_fusion) | copy-start | bytes 62212
  62.4 39.9 %copy-start.18 = (f32[4,4,8,72]{3,2,1,0:T(8,128)}, f32[4,4,8,72]{3,2,1,0:T(8,128)S(1)}, u32[]{:S(2)}) copy-start(f32[4,4,8,72]{3,2,1,0:T(8,128)S(1)} %get-tuple-element.29) | copy-start | bytes 110596
  84.3 12.7 %collective-permute-start.2 = (bf16[3,48,512]{2,1,0:T(8,128)(2,1)S(1)}, bf16[3,48,512]{2,1,0:T(8,128)(2,1)S(1)}, u32[]{:S(2)}, u32[]{:S(2)}) collective-permute-start(bf16[3,48,512]{2,1,0:T(8,128)(2,1)S(1)} %slice.86), channel_id=1, source_target_pairs={{0,112},{16,0},{32,16},{48,32},{64,48},{80,64},{96,80},{112,96},{1... | collective-permute-start | bytes 442376 | tf_op jit(solution)/shard_map/ppermute | solution.py:17
  86.3 5.2 %copy-start.22 = (f32[2048]{0:T(1024)S(1)}, f32[2048]{0:T(1024)}, u32[]{:S(2)}) copy-start(f32[2048]{0:T(1024)} %param.13) | copy-start | bytes 24580
  97.1 6.7 %collective-permute-start.3 = (bf16[24,6,512]{2,1,0:T(8,128)(2,1)S(1)}, bf16[24,6,512]{2,1,0:T(8,128)(2,1)S(1)}, u32[]{:S(2)}, u32[]{:S(2)}) collective-permute-start(bf16[24,6,512]{2,1,0:T(8,128)(2,1)S(1)} %pad_maximum_fusion.4), channel_id=1, source_target_pairs={{0,15},{1,0},{2,1},{3,2},{4,3},{5,4},{6,5},{7,6},{8,7},{9,8},{10,9... | collective-permute-start | bytes 442376 | tf_op jit(solution)/shard_map/ppermute | solution.py:17
  113.2 20.1 %copy-start.29 = (f32[288]{0:T(512)}, f32[288]{0:T(512)S(1)}, u32[]{:S(2)}) copy-start(f32[288]{0:T(512)S(1)} %div.82) | copy-start | bytes 3460
  128.9 4.3 %copy-start.23 = (f32[2048]{0:T(1024)S(1)}, f32[2048]{0:T(1024)}, u32[]{:S(2)}) copy-start(f32[2048]{0:T(1024)} %param.13) | copy-start | bytes 24580
  133.3 3.1 copy-start.31
  149.5 6.3 %copy-start.10 = (bf16[24,48,512]{2,1,0:T(8,128)(2,1)S(1)}, bf16[24,48,512]{2,1,0:T(8,128)(2,1)}, u32[]{:S(2)}) copy-start(bf16[24,48,512]{2,1,0:T(8,128)(2,1)} %copy-done.9) | copy-start | bytes 3538948
  149.5 6.3 %copy-start.15 = (bf16[1152,512]{1,0:T(8,128)(2,1)S(1)}, bf16[1152,512]{1,0:T(8,128)(2,1)}, u32[]{:S(2)}) copy-start(bf16[1152,512]{1,0:T(8,128)(2,1)} %reshape.316) | copy-start | bytes 3538948
  149.5 6.1 %collective-permute-start.4 = (bf16[24,6,512]{2,1,0:T(8,128)(2,1)S(1)}, bf16[24,6,512]{2,1,0:T(8,128)(2,1)S(1)}, u32[]{:S(2)}, u32[]{:S(2)}) collective-permute-start(bf16[24,6,512]{2,1,0:T(8,128)(2,1)S(1)} %slice.89), channel_id=1, source_target_pairs={{0,1},{1,2},{2,3},{3,4},{4,5},{5,6},{6,7},{7,8},{8,9},{9,10},{10,1... | collective-permute-start | bytes 442376 | tf_op jit(solution)/shard_map/ppermute | solution.py:17
  155.7 7.7 %collective-permute-start.5 = (bf16[3,48,512]{2,1,0:T(8,128)(2,1)S(1)}, bf16[3,48,512]{2,1,0:T(8,128)(2,1)S(1)}, u32[]{:S(2)}, u32[]{:S(2)}) collective-permute-start(bf16[3,48,512]{2,1,0:T(8,128)(2,1)S(1)} %pad_maximum_fusion.5), channel_id=1, source_target_pairs={{0,16},{16,32},{32,48},{48,64},{64,80},{80,96},{96,112},{112,0},{1... | collective-permute-start | bytes 442376 | tf_op jit(solution)/shard_map/ppermute | solution.py:17
  175.7 10.3 %slice-start = ((s8[4718592]{0:T(1024)(128)(4,1)}), s8[524288]{0:T(1024)(128)(4,1)S(1)}, s32[]{:S(2)}) async-start(s8[4718592]{0:T(1024)(128)(4,1)} %bitcast.118), calls=%async_computation.1 | async-start | bytes 1048576
  180.7 5.3 %slice-start.1 = ((s8[4718592]{0:T(1024)(128)(4,1)}), s8[4194304]{0:T(1024)(128)(4,1)S(1)}, s32[]{:S(2)}) async-start(s8[4718592]{0:T(1024)(128)(4,1)} %bitcast.118), calls=%async_computation.2 | async-start | bytes 8388608
  180.7 5.5 %copy-start.14 = (bf16[4,4,72,512]{2,3,1,0:T(8,128)(2,1)S(1)}, bf16[4,4,72,512]{2,3,1,0:T(8,128)(2,1)}, u32[]{:S(2)}) copy-start(bf16[4,4,72,512]{2,3,1,0:T(8,128)(2,1)} %copy.131) | copy-start | bytes 3538948
  180.7 5.5 %copy-start.19 = (f32[4,4,8,72]{3,2,1,0:T(8,128)S(1)}, f32[4,4,8,72]{3,2,1,0:T(8,128)}, u32[]{:S(2)}) copy-start(f32[4,4,8,72]{3,2,1,0:T(8,128)} %copy-done.18) | copy-start | bytes 110596
  180.7 5.5 %copy-start.21 = (pred[4,72,72]{1,2,0:T(8,128)(4,1)S(1)}, pred[4,72,72]{1,2,0:T(8,128)(4,1)}, u32[]{:S(2)}) copy-start(pred[4,72,72]{1,2,0:T(8,128)(4,1)} %copy-done.20) | copy-start | bytes 62212
  186.1 2.9 copy-start.13
  189.0 2.8 copy-start.8
  213.7 6.8 %copy-start.28 = (f32[512]{0:T(512)S(1)}, f32[512]{0:T(512)}, u32[]{:S(2)}) copy-start(f32[512]{0:T(512)} %param.10) | copy-start | bytes 6148
  229.0 3.5 copy-start.11
  237.4 5.3 %copy-start.6 = (bf16[12,2,24,2,512]{4,2,3,1,0:T(8,128)(2,1)S(1)}, bf16[12,2,24,2,512]{4,2,3,1,0:T(8,128)(2,1)}, u32[]{:S(2)}) copy-start(bf16[12,2,24,2,512]{4,2,3,1,0:T(8,128)(2,1)} %copy-done.5) | copy-start | bytes 3538948
  237.4 83.1 %collective-permute-start.6 = (bf16[3,48,512]{2,1,0:T(8,128)(2,1)S(1)}, bf16[3,48,512]{2,1,0:T(8,128)(2,1)S(1)}, u32[]{:S(2)}, u32[]{:S(2)}) collective-permute-start(bf16[3,48,512]{2,1,0:T(8,128)(2,1)S(1)} %slice.100), channel_id=1, source_target_pairs={{0,112},{16,0},{32,16},{48,32},{64,48},{80,64},{96,80},{112,96},{1... | collective-permute-start | bytes 442376 | tf_op jit(solution)/shard_map/ppermute | solution.py:17
  321.7 5.2 %copy-start.7 = (f32[24,48,512]{2,1,0:T(8,128)S(1)}, f32[24,48,512]{2,1,0:T(8,128)}, u32[]{:S(2)}) copy-start(f32[24,48,512]{2,1,0:T(8,128)} %reshape.330) | copy-start | bytes 7077892
  321.7 5.2 %collective-permute-start.7 = (bf16[24,6,512]{2,1,0:T(8,128)(2,1)S(1)}, bf16[24,6,512]{2,1,0:T(8,128)(2,1)S(1)}, u32[]{:S(2)}, u32[]{:S(2)}) collective-permute-start(bf16[24,6,512]{2,1,0:T(8,128)(2,1)S(1)} %fusion.39), channel_id=1, source_target_pairs={{0,15},{1,0},{2,1},{3,2},{4,3},{5,4},{6,5},{7,6},{8,7},{9,8},{10,9... | collective-permute-start | bytes 442376 | tf_op jit(solution)/shard_map/ppermute | solution.py:17
  406.5 3.8 copy-start.16
  (13 other events, 24.5 us)
Sparse Core Ops, SparseCore 0:
  236.5 169.9 all-reduce.6
where the time goes:
time: 432 us; the launch traced here: 427 us
  local copies, waits for them, and re-layouts  141 us (33%)
  waiting for transfers between devices  96.2 us (22%)
  blocking collectives  67.9 us (16%)
  matrix products  61.2 us (14%)
  other arithmetic  33.7 us (8%)
  between operations  14.8 us (3%)
  starting transfers between devices  12.5 us (3%)
    psum x1, waiting for transfers between devices, on_device(): lax.psum((grad_gain_attn, grad_w_qkv, grad_w_out, grad_gain_merge, grad_w...  77.6 us
    psum x1, blocking collectives, on_device(): lax.psum((grad_gain_attn, grad_w_qkv, grad_w_out, grad_gain_merge, grad_w...  67.9 us
    ppermute x8, waiting for transfers between devices, shifted_2(): return lax.ppermute(value, axis, pairs)  18.6 us
    convert_element_type x5, local copies, waits for them, and re-layouts, section_three(): merge_groups(values).astype(jnp.float32)  17.6 us
    unnamed x76, local copies, waits for them, and re-layouts  15.6 us
    reshape x3, local copies, waits for them, and re-layouts, windows_attend(): attn_out.astype(jnp.bfloat16)  13.5 us
    dot_general x3, matrix products, windows_attend(): jnp.einsum('abhqk,abkhd->abqhd', attn_weights, value_rows, preferred_elem...  13.1 us
    ppermute x8, starting transfers between devices, shifted_2(): return lax.ppermute(value, axis, pairs)  12.5 us
  transfers between devices with their start and end apart: 9, of which 6 were waited for; matrix products, arithmetic and copies ran while one was open for 10% of the time, Pallas kernels for 0%

commit v1 on v0

v1 whole, which is shorter than its diff:
```python
import functools
import jax
import jax.numpy as jnp
from jax import lax
from jax.experimental import pallas as pl
from jax.experimental.pallas import tpu as pltpu
from jax.sharding import PartitionSpec as P

HEADS = 8
WLAT = 6
WLON = 12
EPSILON = 1e-05
F32 = jnp.float32
BF = jnp.bfloat16
ROWS = 24
COLS = 48
C = 512
WIN = 72
NW = COLS // WLON
PAIRS = HEADS // 2
MIB = 1 << 20


def dot(a, b, ca, cb):
    return lax.dot_general(a, b, (((ca,), (cb,)), ((), ())), preferred_element_type=F32)


def head_masks(scale):
    lane = lax.broadcasted_iota(jnp.int32, (1, 128), 1)
    low = jnp.where(lane < 64, scale, 0.0).astype(F32)
    high = jnp.where(lane < 64, 0.0, scale).astype(F32)
    return low, high


def stacked(value, masks):
    return jnp.concatenate([value * masks[0], value * masks[1]], axis=0).astype(BF)


def merged_heads(value):
    lane = lax.broadcasted_iota(jnp.int32, (WIN, 128), 1)
    return jnp.where(lane < 64, value[:WIN], value[WIN:])


def to_windows(src, dst):
    for v in range(NW):
        for r in range(WLAT):
            dst[v, WLON * r : WLON * (r + 1), :] = src[r, WLON * v : WLON * (v + 1), :]


def to_grid(src, dst):
    for v in range(NW):
        for r in range(WLAT):
            dst[r, WLON * v : WLON * (v + 1), :] = src[v, WLON * r : WLON * (r + 1), :]


def moments(x):
    mean = jnp.mean(x, axis=-1, keepdims=True)
    centered = x - mean
    var = jnp.mean(centered * centered, axis=-1, keepdims=True)
    rstd = lax.rsqrt(var + EPSILON)
    return centered * rstd, rstd


def attend_fwd(tok_ref, bias_ref, gain_ref, w_ref, att_ref, qkv_ref, prob_ref, normed_ref, s1, s2, qf):
    xhat, _ = moments(tok_ref[...].astype(F32))
    s1[...] = xhat * gain_ref[...].reshape(1, 1, C)
    to_windows(s1, s2)
    normed = s2[...].reshape(NW * WIN, C).astype(BF)
    normed_ref[...] = normed
    for t in range(3):
        part = dot(normed, w_ref[:, C * t : C * (t + 1)], 1, 0).reshape(NW, WIN, C)
        if t == 0:
            qf[...] = part
        qkv_ref[:, :, C * t : C * (t + 1)] = part.astype(BF)
    bias = bias_ref[0]

    def window(v, carry):
        masks = head_masks(0.125)
        for p in range(PAIRS):
            lanes = slice(128 * p, 128 * (p + 1))
            qs = stacked(qf[v, :, lanes].astype(BF).astype(F32), masks)
            k = qkv_ref[v, :, C + 128 * p : C + 128 * (p + 1)]
            val = qkv_ref[v, :, 2 * C + 128 * p : 2 * C + 128 * (p + 1)]
            s = dot(k, qs, 1, 1) + bias
            e = jnp.exp(s - jnp.max(s, axis=0, keepdims=True))
            prob = (e * (1.0 / jnp.sum(e, axis=0, keepdims=True))).astype(BF)
            prob_ref[v, p] = prob
            s2[v, :, lanes] = merged_heads(dot(prob, val, 0, 0))
        return carry

    lax.fori_loop(0, NW, window, 0)
    to_grid(s2, s1)
    att_ref[...] = s1[...].astype(BF)


def attention_forward(tokens, bias, gain, w_qkv):
    steps = ROWS // WLAT
    return pl.pallas_call(
        attend_fwd,
        grid=(steps,),
        in_specs=[
            pl.BlockSpec((WLAT, COLS, C), lambda i: (i, 0, 0)),
            pl.BlockSpec((1, WIN, 2 * WIN), lambda i: (i, 0, 0)),
            pl.BlockSpec((1, C), lambda i: (0, 0)),
            pl.BlockSpec((C, 3 * C), lambda i: (0, 0)),
        ],
        out_specs=[
            pl.BlockSpec((WLAT, COLS, C), lambda i: (i, 0, 0)),
            pl.BlockSpec((NW, WIN, 3 * C), lambda i: (i, 0, 0)),
            pl.BlockSpec((NW, PAIRS, WIN, 2 * WIN), lambda i: (i, 0, 0, 0)),
            pl.BlockSpec((NW * WIN, C), lambda i: (i, 0)),
        ],
        out_shape=[
            jax.ShapeDtypeStruct((ROWS, COLS, C), BF),
            jax.ShapeDtypeStruct((steps * NW, WIN, 3 * C), BF),
            jax.ShapeDtypeStruct((steps * NW, PAIRS, WIN, 2 * WIN), BF),
            jax.ShapeDtypeStruct((ROWS * COLS, C), BF),
        ],
        scratch_shapes=[
            pltpu.VMEM((WLAT, COLS, C), F32),
            pltpu.VMEM((NW, WIN, C), F32),
            pltpu.VMEM((NW, WIN, C), F32),
        ],
        compiler_params=pltpu.CompilerParams(vmem_limit_bytes=40 * MIB),
        name="attend_fwd",
    )(tokens, bias, gain, w_qkv)


def attend_bwd(tok_ref, gatt_ref, qkv_ref, prob_ref, normed_ref, gain_ref, w_ref,
               gin_ref, gw_ref, ggain_ref, s1, s2, dq, dall):
    step = pl.program_id(0)
    s1[...] = gatt_ref[...].astype(F32)
    to_windows(s1, s2)

    def window(v, carry):
        masks = head_masks(1.0)
        scaled = head_masks(0.125)
        for p in range(PAIRS):
            lanes = slice(128 * p, 128 * (p + 1))
            q = qkv_ref[v, :, lanes].astype(F32)
            k = qkv_ref[v, :, C + 128 * p : C + 128 * (p + 1)]
            val = qkv_ref[v, :, 2 * C + 128 * p : 2 * C + 128 * (p + 1)]
            qs = stacked(q, scaled)
            gs = stacked(s2[v, :, lanes], masks)
            prob = prob_ref[v, p]
            pf = prob.astype(F32)
            dp = dot(val, gs, 1, 1)
            delta = jnp.sum(pf * dp, axis=0, keepdims=True)
            ds = (pf * (dp - delta)).astype(BF)
            dq[v, :, lanes] = merged_heads(dot(ds, k, 0, 0)) * 0.125
            dq[v, :, C + 128 * p : C + 128 * (p + 1)] = dot(ds, qs, 1, 0)
            dq[v, :, 2 * C + 128 * p : 2 * C + 128 * (p + 1)] = dot(prob, gs, 1, 0)
        return carry

    lax.fori_loop(0, NW, window, 0)
    dqkv = dq[...].reshape(NW * WIN, 3 * C).astype(BF)
    dall[pl.ds(pl.multiple_of(step * (NW * WIN), NW * WIN), NW * WIN), :] = dqkv
    s2[...] = dot(dqkv, w_ref[...], 1, 1).astype(BF).astype(F32).reshape(NW, WIN, C)
    to_grid(s2, s1)
    xhat, rstd = moments(tok_ref[...].astype(F32))
    g = s1[...]
    part = jnp.sum(g * xhat, axis=(0, 1)).reshape(1, C)

    @pl.when(step == 0)
    def _():
        ggain_ref[...] = part

    @pl.when(step > 0)
    def _():
        ggain_ref[...] += part

    dx = g * gain_ref[...].reshape(1, 1, C)
    m1 = jnp.mean(dx, axis=-1, keepdims=True)
    m2 = jnp.mean(dx * xhat, axis=-1, keepdims=True)
    gin_ref[...] = rstd * (dx - m1 - xhat * m2)

    @pl.when(step == pl.num_programs(0) - 1)
    def _():
        for t in range(6):
            cols = slice(256 * t, 256 * (t + 1))
            gw_ref[:, cols] = dot(normed_ref[...], dall[:, cols], 0, 0).astype(BF)


def attention_backward(tokens, grad_att, qkv, prob, normed, gain, w_qkv):
    steps = ROWS // WLAT
    return pl.pallas_call(
        attend_bwd,
        grid=(steps,),
        in_specs=[
            pl.BlockSpec((WLAT, COLS, C), lambda i: (i, 0, 0)),
            pl.BlockSpec((WLAT, COLS, C), lambda i: (i, 0, 0)),
            pl.BlockSpec((NW, WIN, 3 * C), lambda i: (i, 0, 0)),
            pl.BlockSpec((NW, PAIRS, WIN, 2 * WIN), lambda i: (i, 0, 0, 0)),
            pl.BlockSpec((ROWS * COLS, C), lambda i: (0, 0)),
            pl.BlockSpec((1, C), lambda i: (0, 0)),
            pl.BlockSpec((C, 3 * C), lambda i: (0, 0)),
        ],
        out_specs=[
            pl.BlockSpec((WLAT, COLS, C), lambda i: (i, 0, 0)),
            pl.BlockSpec((C, 3 * C), lambda i: (0, 0)),
            pl.BlockSpec((1, C), lambda i: (0, 0)),
        ],
        out_shape=[
            jax.ShapeDtypeStruct((ROWS, COLS, C), F32),
            jax.ShapeDtypeStruct((C, 3 * C), BF),
            jax.ShapeDtypeStruct((1, C), F32),
        ],
        scratch_shapes=[
            pltpu.VMEM((WLAT, COLS, C), F32),
            pltpu.VMEM((NW, WIN, C), F32),
            pltpu.VMEM((NW, WIN, 3 * C), F32),
            pltpu.VMEM((ROWS * COLS, 3 * C), BF),
        ],
        compiler_params=pltpu.CompilerParams(vmem_limit_bytes=48 * MIB),
        name="attend_bwd",
    )(tokens, grad_att, qkv, prob, normed, gain, w_qkv)


CH = 4
NCH = ROWS // CH
MT = (CH // 2) * (COLS // 2)
MALL = NCH * MT
C4 = 4 * C
C2 = 1024


def merge_body(att_ref, tok_ref, gm_ref, wout_ref, wm_hbm, gain_ref,
               merged_ref, gatt_ref, gmix_ref, gwm_ref, gwo_ref, ggain_ref,
               wm_ref, sem, s1, xh, rs, mi, gi):
    load = pltpu.make_async_copy(wm_hbm, wm_ref, sem)
    load.start()
    gain = gain_ref[...]

    def forward(c, carry):
        rows = pl.ds(c * CH, CH)
        att = att_ref[rows].reshape(CH * COLS, C)
        proj = dot(att, wout_ref[...], 1, 0).reshape(CH, COLS, C)
        mixed = (tok_ref[rows].astype(F32) + proj).astype(BF).astype(F32)
        for q in range(4):
            s1[q] = mixed[:, :, 128 * q : 128 * (q + 1)]
        parts = []
        for b in range(2):
            for a in range(2):
                for q in range(4):
                    piece = [s1[q, 2 * i + a, pl.ds(b, COLS // 2, stride=2), :] for i in range(CH // 2)]
                    parts.append(jnp.concatenate(piece, axis=0))
        x = jnp.concatenate(parts, axis=1)
        xhat, rstd = moments(x)
        here = pl.ds(pl.multiple_of(c * MT, MT), MT)
        xh[here, :] = xhat
        rs[here, :] = rstd
        mi[here, :] = (xhat * gain).astype(BF)
        return carry

    lax.fori_loop(0, NCH, forward, 0)
    load.wait()
    gm = gm_ref[...].astype(F32).reshape(MALL, C2).astype(BF)

    def merged_tile(n, carry):
        cols = pl.ds(pl.multiple_of(n * 256, 256), 256)
        merged_ref[:, :, cols] = dot(mi[...], wm_ref[:, cols], 1, 0).reshape(ROWS // 2, COLS // 2, 256).astype(BF)
        return carry

    lax.fori_loop(0, C2 // 256, merged_tile, 0)

    def wide_tile(n, carry):
        cols = pl.ds(pl.multiple_of(n * 256, 256), 256)
        gwm_ref[cols, :] = dot(mi[:, cols], gm, 0, 0).astype(BF)
        gi[:, cols] = dot(gm, wm_ref[cols, :], 1, 1).astype(BF)
        return carry

    lax.fori_loop(0, C4 // 256, wide_tile, 0)
    ggain_ref[...] = jnp.zeros_like(ggain_ref)

    def backward(c, carry):
        rows = pl.ds(c * CH, CH)
        here = pl.ds(pl.multiple_of(c * MT, MT), MT)
        xhat = xh[here, :]
        g = gi[here, :].astype(F32)
        ggain_ref[...] += jnp.sum(g * xhat, axis=0, keepdims=True)
        dx = g * gain
        m1 = jnp.mean(dx, axis=-1, keepdims=True)
        m2 = jnp.mean(dx * xhat, axis=-1, keepdims=True)
        dx = rs[here, :] * (dx - m1 - xhat * m2)
        for b in range(2):
            for a in range(2):
                for q in range(4):
                    start = C * (2 * b + a) + 128 * q
                    for i in range(CH // 2):
                        s1[q, 2 * i + a, pl.ds(b, COLS // 2, stride=2), :] = dx[
                            (COLS // 2) * i : (COLS // 2) * (i + 1), start : start + 128
                        ]
        mixed = jnp.concatenate([s1[q] for q in range(4)], axis=-1).astype(BF)
        gmix_ref[rows] = mixed
        gatt_ref[rows] = dot(mixed.reshape(CH * COLS, C), wout_ref[...], 1, 1).reshape(CH, COLS, C).astype(BF)
        return carry

    lax.fori_loop(0, NCH, backward, 0)
    gmix = gmix_ref[...].reshape(ROWS * COLS, C)
    att = att_ref[...].reshape(ROWS * COLS, C)
    for t in range(2):
        cols = slice(256 * t, 256 * (t + 1))
        gwo_ref[cols, :] = dot(att[:, cols], gmix, 0, 0).astype(BF)


def merge_block(att, tokens, grad_merged, w_out, w_merge, gain):
    vmem = pl.BlockSpec(memory_space=pltpu.VMEM)
    return pl.pallas_call(
        merge_body,
        in_specs=[vmem] * 4 + [pl.BlockSpec(memory_space=pl.ANY), vmem],
        out_specs=[vmem] * 6,
        out_shape=[
            jax.ShapeDtypeStruct((ROWS // 2, COLS // 2, C2), BF),
            jax.ShapeDtypeStruct((ROWS, COLS, C), BF),
            jax.ShapeDtypeStruct((ROWS, COLS, C), BF),
            jax.ShapeDtypeStruct((C4, C2), BF),
            jax.ShapeDtypeStruct((C, C), BF),
            jax.ShapeDtypeStruct((1, C4), F32),
        ],
        scratch_shapes=[
            pltpu.VMEM((C4, C2), BF),
            pltpu.SemaphoreType.DMA(()),
            pltpu.VMEM((4, CH, COLS, 128), F32),
            pltpu.VMEM((MALL, C4), F32),
            pltpu.VMEM((MALL, 1), F32),
            pltpu.VMEM((MALL, C4), BF),
            pltpu.VMEM((MALL, C4), BF),
        ],
        compiler_params=pltpu.CompilerParams(vmem_limit_bytes=52 * MIB),
        name="merge_block",
    )(att, tokens, grad_merged, w_out, w_merge, gain)


def shifted_2(value, axis, steps):
    count = lax.axis_size(axis)
    pairs = [(source, (source + steps) % count) for source in range(count)]
    return lax.ppermute(value, axis, pairs)


def on_device(tokens, lat_band, gain_attn, w_qkv, w_out, gain_merge, w_merge, grad_merged):
    tile_rows, tile_cols, features = tokens.shape
    half_lat = WLAT // 2
    half_lon = WLON // 2
    west_cols = shifted_2(tokens[:, tile_cols - half_lon :], "lon", 1)
    shifted = jnp.concatenate([west_cols, tokens[:, : tile_cols - half_lon]], axis=1)
    south_rows = shifted_2(shifted[tile_rows - half_lat :], "lat", 1)
    shifted = jnp.concatenate([south_rows, shifted[: tile_rows - half_lat]], axis=0)
    band_count = lat_band.shape[0]
    extended = jnp.concatenate([lat_band[band_count - half_lat :], lat_band])
    band_rows = lax.dynamic_slice_in_dim(extended, lax.axis_index("lat") * tile_rows, tile_rows)
    labels = jnp.repeat(band_rows.reshape(-1, WLAT), WLON, axis=1)
    bias = jnp.where(labels[:, :, None] == jnp.tile(labels, (1, 2))[:, None, :], 0.0, -1e30).astype(F32)
    gain_a = gain_attn.reshape(1, C)
    attended, qkv, prob, normed = attention_forward(shifted, bias, gain_a, w_qkv)
    north_rows = shifted_2(attended[:half_lat], "lat", -1)
    back_frame = jnp.concatenate([attended[half_lat:], north_rows], axis=0)
    east_cols = shifted_2(back_frame[:, :half_lon], "lon", -1)
    own_att = jnp.concatenate([back_frame[:, half_lon:], east_cols], axis=1)
    merged, grad_att, grad_mixed, gw_merge, gw_out, gg_merge = merge_block(
        own_att, tokens, grad_merged, w_out, w_merge, gain_merge.reshape(1, C4)
    )
    to_east = shifted_2(grad_att[:, tile_cols - half_lon :], "lon", 1)
    grad_back = jnp.concatenate([to_east, grad_att[:, : tile_cols - half_lon]], axis=1)
    to_north = shifted_2(grad_back[tile_rows - half_lat :], "lat", 1)
    grad_shifted = jnp.concatenate([to_north, grad_back[: tile_rows - half_lat]], axis=0)
    grad_inputs, gw_qkv, gg_attn = attention_backward(
        shifted, grad_shifted, qkv, prob, normed, gain_a, w_qkv
    )
    upper_rows = shifted_2(grad_inputs[:half_lat].astype(BF), "lat", -1).astype(F32)
    own_frame = jnp.concatenate([grad_inputs[half_lat:], upper_rows], axis=0)
    right_cols = shifted_2(own_frame[:, :half_lon].astype(BF), "lon", -1).astype(F32)
    own_frame = jnp.concatenate([own_frame[:, half_lon:], right_cols], axis=1)
    grad_tokens = own_frame + grad_mixed.astype(F32)
    gg_attn, gg_merge, gw_qkv, gw_out, gw_merge = lax.psum(
        (gg_attn, gg_merge, gw_qkv, gw_out, gw_merge), ("lat", "lon")
    )
    return (
        merged,
        grad_tokens,
        gg_attn.reshape(C),
        gw_qkv.astype(F32),
        gw_out.astype(F32),
        gg_merge.reshape(C4),
        gw_merge.astype(F32),
    )


def solution(mesh):
    return jax.shard_map(
        on_device,
        mesh=mesh,
        in_specs=(P("lat", "lon", None), P(), P(), P(), P(), P(), P(), P("lat", "lon", None)),
        out_specs=(P("lat", "lon", None), P("lat", "lon", None), P(), P(), P(), P(), P()),
        check_vma=False,
    )
```

time: 432 us -> 288 us (0.67); the launches traced: 427 us -> 288 us
  local copies, waits for them, and re-layouts: 141 us -> 7.43 us
  matrix products: 61.2 us -> 0 us
  Pallas kernels: 0 us -> 60.1 us
  other arithmetic: 33.7 us -> 16.4 us
  waiting for transfers between devices: 96.2 us -> 105 us
    pallas_call x0 -> x3, Pallas kernels: none -> 60.1 us  [the longest x1 26.7 us: attention_backward(): pl.pallas_call(attend_bwd, grid=(steps,), in_specs=[pl.BlockSpec((WLAT, C...]
    dot_general x14 -> x0, matrix products: 54.7 us -> none  [the longest x3 13.1 us: windows_attend(): jnp.einsum('abhqk,abkhd->abqhd', attn_weights, value_rows, preferred_elem...]
    reshape x11 -> x1, local copies, waits for them, and re-layouts: 42.9 us -> 0.08 us  [on_device(): labels = jnp.repeat(band_rows.reshape(-1, WLAT), WLON, axis=1)]
    convert_element_type x9 -> x0, local copies, waits for them, and re-layouts: 34.1 us -> none  [the longest x5 17.6 us: section_three(): merge_groups(values).astype(jnp.float32)]
    transpose x5 -> x0, local copies, waits for them, and re-layouts: 17.3 us -> none  [the longest x2 8.83 us: windows_attend(): qkv_grid.reshape(count_a, WLAT, count_b, WLON, triple)]
    reduce_sum x7 -> x0, other arithmetic: 15 us -> none  [the longest x2 6.45 us: normalize(): return centered * lax.rsqrt(variance + EPSILON) * gain_vec]
    slice x5 -> x1, local copies, waits for them, and re-layouts: 16 us -> 0.98 us  [on_device(): grad_inputs[:half_lat].astype(BF)]
    unnamed x76 -> x24, local copies, waits for them, and re-layouts: 15.6 us -> 1.31 us
  transfers between devices with their start and end apart: 9 -> 9, of which waited for: 6 -> 8; matrix products, arithmetic and copies ran while one was open for 10% -> 3% of each run, Pallas kernels for 0% -> 0%
where the time goes in v1:
time: 288 us
  waiting for transfers between devices  105 us (36%)
  blocking collectives  69.9 us (24%)
  Pallas kernels  60.1 us (21%)
  other arithmetic  16.4 us (6%)
  starting transfers between devices  14.7 us (5%)
  between operations  14.3 us (5%)
  local copies, waits for them, and re-layouts  7.43 us (3%)
    psum x1, waiting for transfers between devices, on_device(): lax.psum((gg_attn, gg_merge, gw_qkv, gw_out, gw_merge), ('lat', 'lon'))  78.8 us
    psum x1, blocking collectives, on_device(): lax.psum((gg_attn, gg_merge, gw_qkv, gw_out, gw_merge), ('lat', 'lon'))  69.9 us
    pallas_call x1, Pallas kernels, attention_backward(): pl.pallas_call(attend_bwd, grid=(steps,), in_specs=[pl.BlockSpec((WLAT, C...  26.7 us
    ppermute x8, waiting for transfers between devices, shifted_2(): return lax.ppermute(value, axis, pairs)  26.4 us
    pallas_call x1, Pallas kernels, merge_block(): pl.pallas_call(merge_body, in_specs=[vmem] * 4 + [pl.BlockSpec(memory_spa...  17.4 us
    pallas_call x1, Pallas kernels, attention_forward(): pl.pallas_call(attend_fwd, grid=(steps,), in_specs=[pl.BlockSpec((WLAT, C...  16 us
    ppermute x8, starting transfers between devices, shifted_2(): return lax.ppermute(value, axis, pairs)  14.7 us
  transfers between devices with their start and end apart: 9, of which 8 were waited for; matrix products, arithmetic and copies ran while one was open for 3% of the time, Pallas kernels for 0%

profile of v1, /device:TPU:1, one launch (start us, length us, event | category | flops | bytes accessed | tf_op | source)
XLA Modules:
  0.0 288.0 jit_solution(11421798297181710240)
XLA Ops:
  7.2 1.1 slice.53
  8.3 2.8 collective-permute-start
  11.0 0.7 slice.57
  11.8 0.8 pad_add_fusion
  13.0 0.7 collective-permute-done
  13.7 1.1 pad_maximum_fusion.6
  14.7 1.7 collective-permute-start.1
  16.6 6.9 %collective-permute-done.1 = bf16[3,48,512]{2,1,0:T(8,128)(2,1)S(1)} collective-permute-done((bf16[3,48,512]{2,1,0:T(8,128)(2,1)S(1)}, bf16[3,48,512]{2,1,0:T(8,128)(2,1)S(1)}, u32[]{:S(2)}, u32[]{:S(2)}) %collective-permute-start.1) | collective-permute-done | bytes 147488 | tf_op jit(solution)/shard_map/ppermute | solution.py:337
  23.9 16.0 %attend_fwd.1 = (bf16[24,48,512]{2,1,0:T(8,128)(2,1)S(1)}, bf16[16,72,1536]{2,1,0:T(8,128)(2,1)S(1)}, bf16[16,4,72,144]{3,2,1,0:T(8,128)(2,1)S(1)}, bf16[1152,512]{1,0:T(8,128)(2,1)S(1)}) custom-call(bf16[24,48,512]{2,1,0:T(8,128)(2,1)S(1)} %fusion.1.tok_ref, f32[4,72,144]{2,1,0:T(8,128)S(1)} %compare_select_fusion.bias_ref, f32[1,512]{1,0:T(1,128)S(1)} %bitcast.8, ...), custom_call_target="tpu_custom_call" | custom-call | tf_op jit(solution)/shard_map/attend_fwd/pallas_call | solution.py:98
  40.0 1.5 collective-permute-start.2
  41.6 2.5 collective-permute-done.2
  44.1 5.8 %collective-permute-start.3 = (bf16[24,6,512]{2,1,0:T(8,128)(2,1)S(1)}, bf16[24,6,512]{2,1,0:T(8,128)(2,1)S(1)}, u32[]{:S(2)}, u32[]{:S(2)}) collective-permute-start(bf16[24,6,512]{2,1,0:T(8,128)(2,1)S(1)} %pad_maximum_fusion.4), channel_id=1, source_target_pairs={{0,15},{1,0},{2,1},{3,2},{4,3},{5,4},{6,5},{7,6},{8,7},{9,8},{10,9... | collective-permute-start | bytes 442376 | tf_op jit(solution)/shard_map/ppermute | solution.py:337
  50.2 1.4 collective-permute-done.3
  51.6 1.2 pad_maximum_fusion.2.att_ref
  52.7 17.4 %merge_block.1 = (bf16[12,24,1024]{2,1,0:T(8,128)(2,1)}, bf16[24,48,512]{2,1,0:T(8,128)(2,1)}, bf16[24,48,512]{2,1,0:T(8,128)(2,1)}, bf16[2048,1024]{1,0:T(8,128...) custom-call(bf16[24,48,512]{2,1,0:T(8,128)(2,1)} %pad_maximum_fusion.2.att_ref, bf16[24,48,512]{2,1,0:T(8,128)(2,1)} %tok_ref.1, ...), custom_call_target="tpu_custom_call" | custom-call | tf_op jit(solution)/shard_map/merge_block/pallas_call | solution.py:308
  70.1 1.1 slice.62
  71.3 2.6 collective-permute-done.4
  73.9 1.0 pad_maximum_fusion.5
  74.9 8.3 %collective-permute-done.5 = bf16[3,48,512]{2,1,0:T(8,128)(2,1)S(1)} collective-permute-done((bf16[3,48,512]{2,1,0:T(8,128)(2,1)S(1)}, bf16[3,48,512]{2,1,0:T(8,128)(2,1)S(1)}, u32[]{:S(2)}, u32[]{:S(2)}) %collective-permute-start.5) | collective-permute-done | bytes 147488 | tf_op jit(solution)/shard_map/ppermute | solution.py:337
  83.7 26.7 %attend_bwd.1 = (f32[24,48,512]{2,1,0:T(8,128)}, bf16[512,1536]{1,0:T(8,128)(2,1)}, f32[1,512]{1,0:T(1,128)S(1)}) custom-call(bf16[24,48,512]{2,1,0:T(8,128)(2,1)S(1)} %fusion.1.tok_ref, bf16[24,48,512]{2,1,0:T(8,128)(2,1)S(1)} %fusion.gatt_ref, bf16[16,72,1536]{2,1,0:T(8,128)(2,1)} %copy-done.1, bf16[16,4,72,144]{3,2,1,0:T(8,128)(2,1)} %copy-done.2, ...), custom_call_target="tpu_custom_call" | custom-call | tf_op jit(solution)/shard_map/attend_bwd/pallas_call | solution.py:186
  110.5 1.0 slice.80
  111.4 2.0 collective-permute-start.6
  113.5 1.8 slice.66
  115.2 69.9 %all-reduce = (f32[512]{0:T(512)}, f32[2048]{0:T(1024)}) all-reduce(f32[512]{0:T(512)S(1)} %bitcast.10, f32[2048]{0:T(1024)S(1)} %bitcast.7), channel_id=1, replica_groups=mesh['lat'=8,'lon'=16] {'lat','lon'}, use_global_device_ids=true, to_apply=%region_0.1 | all-reduce | flops 2560 | bytes 20480 | tf_op jit(solution)/shard_map/psum | solution.py:374
  185.2 0.7 collective-permute-start.7
  186.3 4.1 %collective-permute-done.7 = bf16[24,6,512]{2,1,0:T(8,128)(2,1)S(1)} collective-permute-done((bf16[24,6,512]{2,1,0:T(8,128)(2,1)S(1)}, bf16[24,6,512]{2,1,0:T(8,128)(2,1)S(1)}, u32[]{:S(2)}, u32[]{:S(2)}) %collective-permute-start.7) | collective-permute-done | bytes 147488 | tf_op jit(solution)/shard_map/ppermute | solution.py:337
  190.5 1.9 maximum_add_fusion
  192.3 78.8 %all-reduce.4.cloned.1.call-done = (bf16[512,1536]{1,0:T(8,128)(2,1)}, bf16[512,512]{1,0:T(8,128)(2,1)}, bf16[2048,1024]{1,0:T(8,128)(2,1)}) async-done(((bf16[512,1536]{1,0:T(8,128)(2,1)}, bf16[512,512]{1,0:T(8,128)(2,1)}, bf16[2048,1024]{1,0:T(8,128)(2,1)}), (bf16[512,1536]{1,0:T(8,128)(2,1)}, bf16[512,512]{1,0:T(8,128)(2,1)}, bf16[2048,1024]{1,0:T(8,128)(2,1)})) %all-reduce.4.cloned.1.call-update) | async-done | bytes 6291472 | tf_op jit(solution)/shard_map/psum | solution.py:374
  271.2 2.3 convert_element_type.24
  273.4 2.1 convert_element_type.23
  275.5 1.3 copy-done.9
  276.8 4.4 %convert_element_type.25 = f32[2048,1024]{1,0:T(8,128)} convert(bf16[2048,1024]{1,0:T(8,128)(2,1)S(1)} %copy-done.9) | non-fusion elementwise | flops 2097152 | bytes 12582912 | tf_op jit(solution)/shard_map/convert_element_type | solution.py:384
  (45 shorter events, 2.6 us)
Async XLA Ops:
  7.2 16.3 %copy-start.7 = (bf16[24,48,512]{2,1,0:T(8,128)(2,1)S(1)}, bf16[24,48,512]{2,1,0:T(8,128)(2,1)}, u32[]{:S(2)}) copy-start(bf16[24,48,512]{2,1,0:T(8,128)(2,1)} %tok_ref.1) | copy-start | bytes 3538948
  7.2 264.0 %all-reduce.4.cloned.1.call-start = ((), (), s32[]{:S(2)}) async-start(), calls=%async_computation | async-start | bytes 12582912 | tf_op jit(solution)/shard_map/psum | solution.py:374
  8.3 5.4 %collective-permute-start = (bf16[24,6,512]{2,1,0:T(8,128)(2,1)S(1)}, bf16[24,6,512]{2,1,0:T(8,128)(2,1)S(1)}, u32[]{:S(2)}, u32[]{:S(2)}) collective-permute-start(bf16[24,6,512]{2,1,0:T(8,128)(2,1)S(1)} %slice.53), channel_id=1, source_target_pairs={{0,1},{1,2},{2,3},{3,4},{4,5},{5,6},{6,7},{7,8},{8,9},{9,10},{10,1... | collective-permute-start | bytes 442376 | tf_op jit(solution)/shard_map/ppermute | solution.py:337
  13.7 10.3 %copy-start = (bf16[512,1536]{1,0:T(8,128)(2,1)S(1)}, bf16[512,1536]{1,0:T(8,128)(2,1)}, u32[]{:S(2)}) copy-start(bf16[512,1536]{1,0:T(8,128)(2,1)} %w_ref.3) | copy-start | bytes 4718596
  13.7 10.3 %copy-start.6 = (f32[512]{0:T(512)S(1)}, f32[512]{0:T(512)}, u32[]{:S(2)}) copy-start(f32[512]{0:T(512)} %param.10) | copy-start | bytes 6148
  14.7 8.7 %collective-permute-start.1 = (bf16[3,48,512]{2,1,0:T(8,128)(2,1)S(1)}, bf16[3,48,512]{2,1,0:T(8,128)(2,1)S(1)}, u32[]{:S(2)}, u32[]{:S(2)}) collective-permute-start(bf16[3,48,512]{2,1,0:T(8,128)(2,1)S(1)} %pad_maximum_fusion.6), channel_id=1, source_target_pairs={{0,16},{16,32},{32,48},{48,64},{64,80},{80,96},{96,112},{112,0},{1... | collective-permute-start | bytes 442376 | tf_op jit(solution)/shard_map/ppermute | solution.py:337
  39.9 10.3 %copy-start.1 = (bf16[16,72,1536]{2,1,0:T(8,128)(2,1)}, bf16[16,72,1536]{2,1,0:T(8,128)(2,1)S(1)}, u32[]{:S(2)}) copy-start(bf16[16,72,1536]{2,1,0:T(8,128)(2,1)S(1)} %get-tuple-element.23.qkv_ref) | copy-start | bytes 10616836
  39.9 10.3 %copy-start.2 = (bf16[16,4,72,144]{3,2,1,0:T(8,128)(2,1)}, bf16[16,4,72,144]{3,2,1,0:T(8,128)(2,1)S(1)}, u32[]{:S(2)}) copy-start(bf16[16,4,72,144]{3,2,1,0:T(8,128)(2,1)S(1)} %get-tuple-element.24.prob_ref) | copy-start | bytes 3981316
  40.0 4.1 %collective-permute-start.2 = (bf16[3,48,512]{2,1,0:T(8,128)(2,1)S(1)}, bf16[3,48,512]{2,1,0:T(8,128)(2,1)S(1)}, u32[]{:S(2)}, u32[]{:S(2)}) collective-permute-start(bf16[3,48,512]{2,1,0:T(8,128)(2,1)S(1)} %slice.59), channel_id=1, source_target_pairs={{0,112},{16,0},{32,16},{48,32},{64,48},{80,64},{96,80},{112,96},{1... | collective-permute-start | bytes 442376 | tf_op jit(solution)/shard_map/ppermute | solution.py:337
  44.0 8.7 %copy-start.3 = (bf16[12,24,1024]{2,1,0:T(8,128)(2,1)S(1)}, bf16[12,24,1024]{2,1,0:T(8,128)(2,1)}, u32[]{:S(2)}) copy-start(bf16[12,24,1024]{2,1,0:T(8,128)(2,1)} %gm_ref.1) | copy-start | bytes 1769476
  44.0 8.7 %copy-start.4 = (bf16[512,512]{1,0:T(8,128)(2,1)S(1)}, bf16[512,512]{1,0:T(8,128)(2,1)}, u32[]{:S(2)}) copy-start(bf16[512,512]{1,0:T(8,128)(2,1)} %wout_ref.1) | copy-start | bytes 1572868
  44.1 8.7 %copy-start.5 = (f32[2048]{0:T(1024)S(1)}, f32[2048]{0:T(1024)}, u32[]{:S(2)}) copy-start(f32[2048]{0:T(1024)} %param.13) | copy-start | bytes 24580
  44.1 7.5 %collective-permute-start.3 = (bf16[24,6,512]{2,1,0:T(8,128)(2,1)S(1)}, bf16[24,6,512]{2,1,0:T(8,128)(2,1)S(1)}, u32[]{:S(2)}, u32[]{:S(2)}) collective-permute-start(bf16[24,6,512]{2,1,0:T(8,128)(2,1)S(1)} %pad_maximum_fusion.4), channel_id=1, source_target_pairs={{0,15},{1,0},{2,1},{3,2},{4,3},{5,4},{6,5},{7,6},{8,7},{9,8},{10,9... | collective-permute-start | bytes 442376 | tf_op jit(solution)/shard_map/ppermute | solution.py:337
  70.1 13.1 %copy-start.8 = (bf16[24,48,512]{2,1,0:T(8,128)(2,1)S(1)}, bf16[24,48,512]{2,1,0:T(8,128)(2,1)}, u32[]{:S(2)}) copy-start(bf16[24,48,512]{2,1,0:T(8,128)(2,1)} %get-tuple-element.22) | copy-start | bytes 3538948
  71.2 2.7 collective-permute-start.4
  74.8 8.4 %collective-permute-start.5 = (bf16[3,48,512]{2,1,0:T(8,128)(2,1)S(1)}, bf16[3,48,512]{2,1,0:T(8,128)(2,1)S(1)}, u32[]{:S(2)}, u32[]{:S(2)}) collective-permute-start(bf16[3,48,512]{2,1,0:T(8,128)(2,1)S(1)} %pad_maximum_fusion.5), channel_id=1, source_target_pairs={{0,16},{16,32},{32,48},{48,64},{64,80},{80,96},{96,112},{112,0},{1... | collective-permute-start | bytes 442376 | tf_op jit(solution)/shard_map/ppermute | solution.py:337
  111.4 73.7 %collective-permute-start.6 = (bf16[3,48,512]{2,1,0:T(8,128)(2,1)S(1)}, bf16[3,48,512]{2,1,0:T(8,128)(2,1)S(1)}, u32[]{:S(2)}, u32[]{:S(2)}) collective-permute-start(bf16[3,48,512]{2,1,0:T(8,128)(2,1)S(1)} %slice.80), channel_id=1, source_target_pairs={{0,112},{16,0},{32,16},{48,32},{64,48},{80,64},{96,80},{112,96},{1... | collective-permute-start | bytes 442376 | tf_op jit(solution)/shard_map/ppermute | solution.py:337
  185.2 5.2 %copy-start.11 = (bf16[24,48,512]{2,1,0:T(8,128)(2,1)S(1)}, bf16[24,48,512]{2,1,0:T(8,128)(2,1)}, u32[]{:S(2)}) copy-start(bf16[24,48,512]{2,1,0:T(8,128)(2,1)} %get-tuple-element.27) | copy-start | bytes 3538948
  185.2 5.2 %collective-permute-start.7 = (bf16[24,6,512]{2,1,0:T(8,128)(2,1)S(1)}, bf16[24,6,512]{2,1,0:T(8,128)(2,1)S(1)}, u32[]{:S(2)}, u32[]{:S(2)}) collective-permute-start(bf16[24,6,512]{2,1,0:T(8,128)(2,1)S(1)} %fusion.2), channel_id=1, source_target_pairs={{0,15},{1,0},{2,1},{3,2},{4,3},{5,4},{6,5},{7,6},{8,7},{9,8},{10,9... | collective-permute-start | bytes 442376 | tf_op jit(solution)/shard_map/ppermute | solution.py:337
  271.2 2.3 copy-start.10
  273.4 3.3 %copy-start.9 = (bf16[2048,1024]{1,0:T(8,128)(2,1)S(1)}, bf16[2048,1024]{1,0:T(8,128)(2,1)}, u32[]{:S(2)}) copy-start(bf16[2048,1024]{1,0:T(8,128)(2,1)} %get-tuple-element.37) | copy-start | bytes 12582916
Sparse Core Ops, SparseCore 0:
  110.6 160.5 all-reduce.3

commit v2 on v1

--- a/solution.py
+++ b/solution.py
@@ -329,6 +329,261 @@
         compiler_params=pltpu.CompilerParams(vmem_limit_bytes=52 * MIB),
         name="merge_block",
     )(att, tokens, grad_merged, w_out, w_merge, gain)
+
+
+AXES = ("x", "y", "z")
+
+
+def coordinates():
+    lat = lax.axis_index("lat")
+    lon = lax.axis_index("lon")
+    return {"x": lon // 4, "y": (lat // 4) * 2 + (lon // 2) % 2, "z": lat % 4, "core": lon % 2}
+
+
+def device(at):
+    return ((at["y"] // 2) * 4 + at["z"], at["x"] * 4 + (at["y"] % 2) * 2 + at["core"])
+
+
+def peer(at, axis, step):
+    size = 2 if axis == "core" else 4
+    return device({**at, axis: (at[axis] + step) % size})
+
+
+def remote(src, dst, send, recv, target):
+    return pltpu.make_async_remote_copy(
+        src_ref=src, dst_ref=dst, send_sem=send, recv_sem=recv,
+        device_id=target, device_id_type=pl.DeviceIdType.MESH,
+    )
+
+
+def greet(at):
+    barrier = pltpu.get_barrier_semaphore()
+    for axis, count in (("core", 2), ("x", 4), ("y", 4), ("z", 4)):
+        for step in range(1, count):
+            pl.semaphore_signal(
+                barrier, inc=1, device_id=peer(at, axis, step), device_id_type=pl.DeviceIdType.MESH
+            )
+    pl.semaphore_wait(barrier, 10)
+
+
+def add_rows(dst, terms, rows, chunk):
+    chunk = min(rows, chunk)
+
+    def body(i, carry):
+        total = None
+        for ref, first in terms:
+            piece = ref[pl.ds(pl.multiple_of(first + i * chunk, 16), chunk), :].astype(F32)
+            total = piece if total is None else total + piece
+        dst[pl.ds(pl.multiple_of(i * chunk, 16), chunk), :] = total.astype(dst.dtype)
+        return carry
+
+    if rows == chunk:
+        body(0, 0)
+    else:
+        lax.fori_loop(0, rows // chunk, body, 0)
+
+
+class Sum:
+    def __init__(self, at, src, out, order, bufs, send, recv):
+        self.at, self.src, self.out, self.order = at, src, out, order
+        self.recv0, self.acc0, self.recvs, self.accs = bufs
+        self.send, self.recv = send, recv
+        self.rows = src.shape[0]
+        self.sent = []
+
+    def start(self, src, dst, index, target):
+        copy = remote(src, dst, self.send.at[index], self.recv.at[index], target)
+        copy.start()
+        self.sent.append(copy)
+        return copy
+
+    def begin(self):
+        half = self.rows // 2
+        theirs = pl.ds(pl.multiple_of((1 - self.at["core"]) * half, 16), half)
+        self.last = [self.start(self.src.at[theirs, :], self.recv0, 0, peer(self.at, "core", 1))]
+
+    def core_sum(self):
+        half = self.rows // 2
+        self.last[0].wait_recv()
+        add_rows(self.acc0, [(self.src, self.at["core"] * half), (self.recv0, 0)], half, 64)
+        self.scatter(0, self.acc0)
+
+    def scatter(self, level, acc):
+        axis = self.order[level]
+        block = self.rows // 2 // 4 ** (level + 1)
+        self.last = []
+        for step in range(1, 4):
+            first = pl.multiple_of((self.at[axis] + step) % 4 * block, 16)
+            self.last.append(
+                self.start(
+                    acc.at[pl.ds(first, block), :], self.recvs[level].at[step - 1],
+                    1 + 3 * level + step - 1, peer(self.at, axis, step),
+                )
+            )
+
+    def combine(self, level):
+        axis = self.order[level]
+        block = self.rows // 2 // 4 ** (level + 1)
+        for copy in self.last:
+            copy.wait_recv()
+        acc = self.acc0 if level == 0 else self.accs[level - 1]
+        terms = [(acc, self.at[axis] * block)] + [(self.recvs[level].at[s], 0) for s in range(3)]
+        if level < 2:
+            add_rows(self.accs[level], terms, block, 64)
+            self.scatter(level + 1, self.accs[level])
+        else:
+            add_rows(self.out.at[pl.ds(self.first(3), block), :], terms, block, 64)
+            self.gather(2)
+
+    def first(self, levels):
+        first = self.at["core"] * (self.rows // 2)
+        for level in range(levels):
+            first = first + self.at[self.order[level]] * (self.rows // 2 // 4 ** (level + 1))
+        return pl.multiple_of(first, 16)
+
+    def gather(self, level):
+        axis = self.order[level]
+        block = self.rows // 2 // 4 ** (level + 1)
+        mine = self.out.at[pl.ds(self.first(level + 1), block), :]
+        self.last = [
+            self.start(mine, mine, 10 + 3 * level + step - 1, peer(self.at, axis, step)) for step in range(1, 4)
+        ]
+
+    def gathered(self, level):
+        for copy in self.last:
+            copy.wait_recv()
+        if level:
+            self.gather(level - 1)
+        else:
+            mine = self.out.at[pl.ds(self.first(0), self.rows // 2), :]
+            self.last = [self.start(mine, mine, 19, peer(self.at, "core", 1))]
+
+    def finish(self):
+        self.last[0].wait_recv()
+        for copy in self.sent:
+            copy.wait_send()
+
+    def steps(self):
+        return [
+            self.begin,
+            self.core_sum,
+            lambda: self.combine(0),
+            lambda: self.combine(1),
+            lambda: self.combine(2),
+            lambda: self.gathered(2),
+            lambda: self.gathered(1),
+            lambda: self.gathered(0),
+            self.finish,
+        ]
+
+
+SUM_COPIES = 20
+
+
+def sum_scratch(rows, lanes):
+    half = rows // 2
+    return [
+        pltpu.VMEM((half, lanes), BF),
+        pltpu.VMEM((half, lanes), BF),
+        pltpu.VMEM((3, half // 4, lanes), BF),
+        pltpu.VMEM((3, half // 16, lanes), BF),
+        pltpu.VMEM((3, half // 64, lanes), BF),
+        pltpu.VMEM((half // 4, lanes), BF),
+        pltpu.VMEM((half // 16, lanes), BF),
+    ]
+
+
+def pack_scratch(refs):
+    return refs[0], refs[1], refs[2:5], refs[5:7]
+
+
+class SmallSum:
+    def __init__(self, at, block, slots, send, recv):
+        self.at, self.block, self.slots, self.send, self.recv = at, block, slots, send, recv
+        self.sent = []
+
+    def begin(self, level):
+        axis, count = (("core", 2), ("x", 4), ("y", 4), ("z", 4))[level]
+        base = 0 if level == 0 else 3 * level - 2
+        self.last = []
+        for step in range(1, count):
+            i = base + step - 1
+            copy = remote(self.block.at[level], self.slots.at[i], self.send.at[i], self.recv.at[i],
+                          peer(self.at, axis, step))
+            copy.start()
+            self.last.append((copy, i))
+            self.sent.append(copy)
+
+    def end(self, level):
+        total = self.block[level]
+        for copy, i in self.last:
+            copy.wait_recv()
+            total = total + self.slots[i]
+        self.block[level + 1] = total
+
+    def finish(self):
+        for copy in self.sent:
+            copy.wait_send()
+
+
+def sum_body(gwm_ref, gwq_ref, gwo_ref, ga_ref, gg_ref, outm_ref, outq_ref, outs_ref, *scratch):
+    qo, small, slots, send, recv, ssend, srecv = scratch[:7]
+    at = coordinates()
+    greet(at)
+    for t in range(3):
+        qo[C * t : C * (t + 1), :] = gwq_ref[:, C * t : C * (t + 1)]
+    qo[3 * C : 4 * C, :] = gwo_ref[...]
+    small[0] = jnp.zeros_like(small[0])
+    small[0, 0:1, :] = ga_ref[...]
+    for t in range(4):
+        small[0, 1 + t : 2 + t, :] = gg_ref[:, C * t : C * (t + 1)]
+    pieces = [
+        (gwm_ref.at[:, 0:C], outm_ref.at[:, 0:C]),
+        (gwm_ref.at[:, C : 2 * C], outm_ref.at[:, C : 2 * C]),
+        (qo, outq_ref),
+    ]
+    sums = []
+    for t, (src, out) in enumerate(pieces):
+        order = AXES[t:] + AXES[:t]
+        bufs = pack_scratch(scratch[7 + 7 * t : 14 + 7 * t])
+        sums.append(Sum(at, src, out, order, bufs, send.at[t], recv.at[t]).steps())
+    gains = SmallSum(at, small, slots, ssend, srecv)
+    for n in range(len(sums[0])):
+        for steps in sums:
+            steps[n]()
+        if n < 4:
+            gains.begin(n)
+            gains.end(n)
+    gains.finish()
+    outs_ref[...] = small[4]
+
+
+def sum_all(gw_merge, gw_qkv, gw_out, gg_attn, gg_merge):
+    vmem = pl.BlockSpec(memory_space=pltpu.VMEM)
+    return pl.pallas_call(
+        sum_body,
+        in_specs=[vmem] * 5,
+        out_specs=[vmem] * 3,
+        out_shape=[
+            jax.ShapeDtypeStruct((C4, C2), BF),
+            jax.ShapeDtypeStruct((4 * C, C), BF),
+            jax.ShapeDtypeStruct((8, C), F32),
+        ],
+        scratch_shapes=[
+            pltpu.VMEM((4 * C, C), BF),
+            pltpu.VMEM((5, 8, C), F32),
+            pltpu.VMEM((10, 8, C), F32),
+            pltpu.SemaphoreType.DMA((3, SUM_COPIES)),
+            pltpu.SemaphoreType.DMA((3, SUM_COPIES)),
+            pltpu.SemaphoreType.DMA((10,)),
+            pltpu.SemaphoreType.DMA((10,)),
+        ]
+        + sum_scratch(4 * C, C) * 3,
+        compiler_params=pltpu.CompilerParams(
+            vmem_limit_bytes=52 * MIB, collective_id=0, has_side_effects=True
+        ),
+        name="sum_all",
+    )(gw_merge, gw_qkv, gw_out, gg_attn, gg_merge)
 
 
 def shifted_2(value, axis, steps):
@@ -371,17 +626,16 @@
     right_cols = shifted_2(own_frame[:, :half_lon].astype(BF), "lon", -1).astype(F32)
     own_frame = jnp.concatenate([own_frame[:, half_lon:], right_cols], axis=1)
     grad_tokens = own_frame + grad_mixed.astype(F32)
-    gg_attn, gg_merge, gw_qkv, gw_out, gw_merge = lax.psum(
-        (gg_attn, gg_merge, gw_qkv, gw_out, gw_merge), ("lat", "lon")
-    )
+    sum_merge, sum_qo, sum_gain = sum_all(gw_merge, gw_qkv, gw_out, gg_attn, gg_merge)
+    gw_qkv = jnp.concatenate([sum_qo[C * t : C * (t + 1)] for t in range(3)], axis=1)
     return (
         merged,
         grad_tokens,
-        gg_attn.reshape(C),
+        sum_gain[0],
         gw_qkv.astype(F32),
-        gw_out.astype(F32),
-        gg_merge.reshape(C4),
-        gw_merge.astype(F32),
+        sum_qo[3 * C :].astype(F32),
+        sum_gain[1:5].reshape(C4),
+        sum_merge.astype(F32),
     )
 
 

time: 288 us -> 197 us (0.68)
  waiting for transfers between devices: 105 us -> 26.7 us
  Pallas kernels: 60.1 us -> 130 us
  blocking collectives: 69.9 us -> 0 us
  between operations: 14.3 us -> 0.89 us
    psum x1 -> x0, waiting for transfers between devices: 78.8 us -> none  [on_device(): lax.psum((gg_attn, gg_merge, gw_qkv, gw_out, gw_merge), ('lat', 'lon'))]
    pallas_call x0 -> x1, Pallas kernels: none -> 70.7 us  [sum_all(): pl.pallas_call(sum_body, in_specs=[vmem] * 5, out_specs=[vmem] * 3, out_s...]
    psum x1 -> x0, blocking collectives: 69.9 us -> none  [on_device(): lax.psum((gg_attn, gg_merge, gw_qkv, gw_out, gw_merge), ('lat', 'lon'))]
  transfers between devices with their start and end apart: 9 -> 8, of which waited for: 8 -> 7; matrix products, arithmetic and copies ran while one was open for 3% -> 6% of each run, Pallas kernels for 0% -> 0%
where the time goes in v2:
time: 197 us
  Pallas kernels  130 us (66%)
  waiting for transfers between devices  26.7 us (14%)
  other arithmetic  16.9 us (9%)
  starting transfers between devices  14 us (7%)
  local copies, waits for them, and re-layouts  8.25 us (4%)
    pallas_call x1, Pallas kernels, sum_all(): pl.pallas_call(sum_body, in_specs=[vmem] * 5, out_specs=[vmem] * 3, out_s...  70.7 us
    ppermute x8, waiting for transfers between devices, shifted_2(): return lax.ppermute(value, axis, pairs)  26.7 us
    pallas_call x1, Pallas kernels, attention_backward(): pl.pallas_call(attend_bwd, grid=(steps,), in_specs=[pl.BlockSpec((WLAT, C...  26.1 us
    pallas_call x1, Pallas kernels, merge_block(): pl.pallas_call(merge_body, in_specs=[vmem] * 4 + [pl.BlockSpec(memory_spa...  17.3 us
    pallas_call x1, Pallas kernels, attention_forward(): pl.pallas_call(attend_fwd, grid=(steps,), in_specs=[pl.BlockSpec((WLAT, C...  15.9 us
    ppermute x8, starting transfers between devices, shifted_2(): return lax.ppermute(value, axis, pairs)  14 us
    convert_element_type x1, other arithmetic, on_device(): sum_merge.astype(F32)  4.43 us
  transfers between devices with their start and end apart: 8, of which 7 were waited for; matrix products, arithmetic and copies ran while one was open for 6% of the time, Pallas kernels for 0%

profile of v2, /device:TPU:1, one launch (start us, length us, event | category | flops | bytes accessed | tf_op | source)
XLA Modules:
  0.0 196.8 jit_solution(5146015540547689212)
XLA Ops:
  0.6 1.1 slice.71
  1.7 2.8 %collective-permute-start = (bf16[24,6,512]{2,1,0:T(8,128)(2,1)S(1)}, bf16[24,6,512]{2,1,0:T(8,128)(2,1)S(1)}, u32[]{:S(2)}, u32[]{:S(2)}) collective-permute-start(bf16[24,6,512]{2,1,0:T(8,128)(2,1)S(1)} %slice.71), channel_id=1, source_target_pairs={{0,1},{1,2},{2,3},{3,4},{4,5},{5,6},{6,7},{7,8},{8,9},{9,10},{10,1... | collective-permute-start | bytes 442376 | tf_op jit(solution)/shard_map/ppermute | solution.py:592
  4.5 0.7 slice.75
  5.2 0.8 pad_add_fusion
  6.4 0.7 collective-permute-done
  7.1 1.1 pad_maximum_fusion.6
  8.2 1.7 collective-permute-start.1
  10.0 6.9 %collective-permute-done.1 = bf16[3,48,512]{2,1,0:T(8,128)(2,1)S(1)} collective-permute-done((bf16[3,48,512]{2,1,0:T(8,128)(2,1)S(1)}, bf16[3,48,512]{2,1,0:T(8,128)(2,1)S(1)}, u32[]{:S(2)}, u32[]{:S(2)}) %collective-permute-start.1) | collective-permute-done | bytes 147488 | tf_op jit(solution)/shard_map/ppermute | solution.py:592
  17.4 15.9 %attend_fwd.1 = (bf16[24,48,512]{2,1,0:T(8,128)(2,1)S(1)}, bf16[16,72,1536]{2,1,0:T(8,128)(2,1)S(1)}, bf16[16,4,72,144]{3,2,1,0:T(8,128)(2,1)S(1)}, bf16[1152,512]{1,0:T(8,128)(2,1)S(1)}) custom-call(bf16[24,48,512]{2,1,0:T(8,128)(2,1)S(1)} %fusion.1.tok_ref, f32[4,72,144]{2,1,0:T(8,128)S(1)} %compare_select_fusion.bias_ref, f32[1,512]{1,0:T(1,128)S(1)} %bitcast.9, ...), custom_call_target="tpu_custom_call" | custom-call | tf_op jit(solution)/shard_map/attend_fwd/pallas_call | solution.py:98
  33.3 1.5 collective-permute-start.2
  34.9 2.5 %collective-permute-done.2 = bf16[3,48,512]{2,1,0:T(8,128)(2,1)S(1)} collective-permute-done((bf16[3,48,512]{2,1,0:T(8,128)(2,1)S(1)}, bf16[3,48,512]{2,1,0:T(8,128)(2,1)S(1)}, u32[]{:S(2)}, u32[]{:S(2)}) %collective-permute-start.2) | collective-permute-done | bytes 147488 | tf_op jit(solution)/shard_map/ppermute | solution.py:592
  37.4 5.8 %collective-permute-start.3 = (bf16[24,6,512]{2,1,0:T(8,128)(2,1)S(1)}, bf16[24,6,512]{2,1,0:T(8,128)(2,1)S(1)}, u32[]{:S(2)}, u32[]{:S(2)}) collective-permute-start(bf16[24,6,512]{2,1,0:T(8,128)(2,1)S(1)} %pad_maximum_fusion.4), channel_id=1, source_target_pairs={{0,15},{1,0},{2,1},{3,2},{4,3},{5,4},{6,5},{7,6},{8,7},{9,8},{10,9... | collective-permute-start | bytes 442376 | tf_op jit(solution)/shard_map/ppermute | solution.py:592
  43.6 1.4 collective-permute-done.3
  45.0 1.2 pad_maximum_fusion.2.att_ref
  46.1 17.3 %merge_block.1 = (bf16[12,24,1024]{2,1,0:T(8,128)(2,1)}, bf16[24,48,512]{2,1,0:T(8,128)(2,1)}, bf16[24,48,512]{2,1,0:T(8,128)(2,1)}, bf16[2048,1024]{1,0:T(8,128...) custom-call(bf16[24,48,512]{2,1,0:T(8,128)(2,1)} %pad_maximum_fusion.2.att_ref, ...), custom_call_target="tpu_custom_call" | custom-call | tf_op jit(solution)/shard_map/merge_block/pallas_call | solution.py:308
  63.5 1.1 slice.80
  64.6 2.6 %collective-permute-done.4 = bf16[24,6,512]{2,1,0:T(8,128)(2,1)S(1)} collective-permute-done((bf16[24,6,512]{2,1,0:T(8,128)(2,1)S(1)}, bf16[24,6,512]{2,1,0:T(8,128)(2,1)S(1)}, u32[]{:S(2)}, u32[]{:S(2)}) %collective-permute-start.4) | collective-permute-done | bytes 147488 | tf_op jit(solution)/shard_map/ppermute | solution.py:592
  67.2 1.0 pad_maximum_fusion.5
  68.4 8.3 %collective-permute-done.5 = bf16[3,48,512]{2,1,0:T(8,128)(2,1)S(1)} collective-permute-done((bf16[3,48,512]{2,1,0:T(8,128)(2,1)S(1)}, bf16[3,48,512]{2,1,0:T(8,128)(2,1)S(1)}, u32[]{:S(2)}, u32[]{:S(2)}) %collective-permute-start.5) | collective-permute-done | bytes 147488 | tf_op jit(solution)/shard_map/ppermute | solution.py:592
  77.2 26.1 %attend_bwd.1 = (f32[24,48,512]{2,1,0:T(8,128)}, bf16[512,1536]{1,0:T(8,128)(2,1)S(1)}, f32[1,512]{1,0:T(1,128)S(1)}) custom-call(bf16[24,48,512]{2,1,0:T(8,128)(2,1)S(1)} %fusion.1.tok_ref, bf16[24,48,512]{2,1,0:T(8,128)(2,1)S(1)} %fusion.gatt_ref, bf16[16,72,1536]{2,1,0:T(8,128)(2,1)} %copy-done.1, bf16[16,4,72,144]{3,2,1,0:T(8,128)(2,1)} %copy-done.2, ...), custom_call_target="tpu_custom_call" | custom-call | tf_op jit(solution)/shard_map/attend_bwd/pallas_call | solution.py:186
  103.3 1.2 slice.106
  104.5 1.8 slice.84
  106.4 70.7 %sum_all.1 = (bf16[2048,1024]{1,0:T(8,128)(2,1)}, bf16[2048,512]{1,0:T(8,128)(2,1)}, f32[8,512]{1,0:T(8,128)S(1)}) custom-call(bf16[2048,1024]{1,0:T(8,128)(2,1)} %get-tuple-element.31.gwm_ref, bf16[512,1536]{1,0:T(8,128)(2,1)} %copy-done.3, bf16[512,512]{1,0:T(8,128)(2,1)S(1)} %get-tuple-element.33.gwo_ref, f32[1,512]{1,0:T(1,128)S(1)} %get-tuple-element.34.ga_ref, ...), custom_call_target="tpu_custom_call" | custom-call | tf_op jit(solution)/shard_map/sum_all/pallas_call | solution.py:563
  177.1 0.6 slice.88
  177.7 1.4 collective-permute-start.6
  179.1 2.8 %slice_convert_fusion = (f32[512,512]{1,0:T(8,128)}, bf16[512,512]{1,0:T(8,128)(2,1)S(1)}, bf16[512,512]{1,0:T(8,128)(2,1)S(1)}, bf16[512,512]{1,0:T(8,128)(2,1)S(1)}) fusion(bf16[2048,512]{1,0:T(8,128)(2,1)} %get-tuple-element.37), kind=kLoop, calls=%fused_computation.9 | loop fusion | flops 262144 | bytes 4718592 | tf_op jit(solution)/shard_map/convert_element_type | solution.py:636
  181.9 2.1 %maximum_convert_fusion = f32[512,1536]{1,0:T(8,128)} fusion(bf16[512,512]{1,0:T(8,128)(2,1)S(1)} %get-tuple-element.40, bf16[512,512]{1,0:T(8,128)(2,1)S(1)} %get-tuple-element.41, bf16[512,512]{1,0:T(8,128)(2,1)S(1)} %get-tuple-element.42), kind=kLoop, calls=%fused_computation.2 | loop fusion | flops 4718592 | bytes 4718592 | tf_op jit(solution)/shard_map/convert_element_type | solution.py:635
  184.0 0.6 copy.15
  184.6 0.6 copy-done.10
  185.2 4.4 %convert_element_type.25 = f32[2048,1024]{1,0:T(8,128)} convert(bf16[2048,1024]{1,0:T(8,128)(2,1)S(1)} %copy-done.10) | non-fusion elementwise | flops 2097152 | bytes 12582912 | tf_op jit(solution)/shard_map/convert_element_type | solution.py:638
  190.5 4.4 %collective-permute-done.7 = bf16[24,6,512]{2,1,0:T(8,128)(2,1)S(1)} collective-permute-done((bf16[24,6,512]{2,1,0:T(8,128)(2,1)S(1)}, bf16[24,6,512]{2,1,0:T(8,128)(2,1)S(1)}, u32[]{:S(2)}, u32[]{:S(2)}) %collective-permute-start.7) | collective-permute-done | bytes 147488 | tf_op jit(solution)/shard_map/ppermute | solution.py:592
  194.9 1.9 maximum_add_fusion
  (45 shorter events, 3.1 us)
Async XLA Ops:
  0.6 16.2 %copy-start.8 = (bf16[24,48,512]{2,1,0:T(8,128)(2,1)S(1)}, bf16[24,48,512]{2,1,0:T(8,128)(2,1)}, u32[]{:S(2)}) copy-start(bf16[24,48,512]{2,1,0:T(8,128)(2,1)} %tok_ref.1) | copy-start | bytes 3538948
  1.7 5.4 %collective-permute-start = (bf16[24,6,512]{2,1,0:T(8,128)(2,1)S(1)}, bf16[24,6,512]{2,1,0:T(8,128)(2,1)S(1)}, u32[]{:S(2)}, u32[]{:S(2)}) collective-permute-start(bf16[24,6,512]{2,1,0:T(8,128)(2,1)S(1)} %slice.71), channel_id=1, source_target_pairs={{0,1},{1,2},{2,3},{3,4},{4,5},{5,6},{6,7},{7,8},{8,9},{9,10},{10,1... | collective-permute-start | bytes 442376 | tf_op jit(solution)/shard_map/ppermute | solution.py:592
  7.1 10.3 %copy-start = (bf16[512,1536]{1,0:T(8,128)(2,1)S(1)}, bf16[512,1536]{1,0:T(8,128)(2,1)}, u32[]{:S(2)}) copy-start(bf16[512,1536]{1,0:T(8,128)(2,1)} %w_ref.3) | copy-start | bytes 4718596
  7.1 10.3 %copy-start.7 = (f32[512]{0:T(512)S(1)}, f32[512]{0:T(512)}, u32[]{:S(2)}) copy-start(f32[512]{0:T(512)} %param.10) | copy-start | bytes 6148
  8.2 8.7 %collective-permute-start.1 = (bf16[3,48,512]{2,1,0:T(8,128)(2,1)S(1)}, bf16[3,48,512]{2,1,0:T(8,128)(2,1)S(1)}, u32[]{:S(2)}, u32[]{:S(2)}) collective-permute-start(bf16[3,48,512]{2,1,0:T(8,128)(2,1)S(1)} %pad_maximum_fusion.6), channel_id=1, source_target_pairs={{0,16},{16,32},{32,48},{48,64},{64,80},{80,96},{96,112},{112,0},{1... | collective-permute-start | bytes 442376 | tf_op jit(solution)/shard_map/ppermute | solution.py:592
  33.3 10.3 %copy-start.1 = (bf16[16,72,1536]{2,1,0:T(8,128)(2,1)}, bf16[16,72,1536]{2,1,0:T(8,128)(2,1)S(1)}, u32[]{:S(2)}) copy-start(bf16[16,72,1536]{2,1,0:T(8,128)(2,1)S(1)} %get-tuple-element.26.qkv_ref) | copy-start | bytes 10616836
  33.3 10.3 %copy-start.2 = (bf16[16,4,72,144]{3,2,1,0:T(8,128)(2,1)}, bf16[16,4,72,144]{3,2,1,0:T(8,128)(2,1)S(1)}, u32[]{:S(2)}) copy-start(bf16[16,4,72,144]{3,2,1,0:T(8,128)(2,1)S(1)} %get-tuple-element.27.prob_ref) | copy-start | bytes 3981316
  33.3 4.1 %collective-permute-start.2 = (bf16[3,48,512]{2,1,0:T(8,128)(2,1)S(1)}, bf16[3,48,512]{2,1,0:T(8,128)(2,1)S(1)}, u32[]{:S(2)}, u32[]{:S(2)}) collective-permute-start(bf16[3,48,512]{2,1,0:T(8,128)(2,1)S(1)} %slice.77), channel_id=1, source_target_pairs={{0,112},{16,0},{32,16},{48,32},{64,48},{80,64},{96,80},{112,96},{1... | collective-permute-start | bytes 442376 | tf_op jit(solution)/shard_map/ppermute | solution.py:592
  37.4 8.7 %copy-start.4 = (bf16[12,24,1024]{2,1,0:T(8,128)(2,1)S(1)}, bf16[12,24,1024]{2,1,0:T(8,128)(2,1)}, u32[]{:S(2)}) copy-start(bf16[12,24,1024]{2,1,0:T(8,128)(2,1)} %gm_ref.1) | copy-start | bytes 1769476
  37.4 8.7 %copy-start.5 = (bf16[512,512]{1,0:T(8,128)(2,1)S(1)}, bf16[512,512]{1,0:T(8,128)(2,1)}, u32[]{:S(2)}) copy-start(bf16[512,512]{1,0:T(8,128)(2,1)} %wout_ref.1) | copy-start | bytes 1572868
  37.4 8.7 %copy-start.6 = (f32[2048]{0:T(1024)S(1)}, f32[2048]{0:T(1024)}, u32[]{:S(2)}) copy-start(f32[2048]{0:T(1024)} %param.13) | copy-start | bytes 24580
  37.4 7.5 %collective-permute-start.3 = (bf16[24,6,512]{2,1,0:T(8,128)(2,1)S(1)}, bf16[24,6,512]{2,1,0:T(8,128)(2,1)S(1)}, u32[]{:S(2)}, u32[]{:S(2)}) collective-permute-start(bf16[24,6,512]{2,1,0:T(8,128)(2,1)S(1)} %pad_maximum_fusion.4), channel_id=1, source_target_pairs={{0,15},{1,0},{2,1},{3,2},{4,3},{5,4},{6,5},{7,6},{8,7},{9,8},{10,9... | collective-permute-start | bytes 442376 | tf_op jit(solution)/shard_map/ppermute | solution.py:592
  63.4 13.3 %copy-start.9 = (bf16[24,48,512]{2,1,0:T(8,128)(2,1)S(1)}, bf16[24,48,512]{2,1,0:T(8,128)(2,1)}, u32[]{:S(2)}) copy-start(bf16[24,48,512]{2,1,0:T(8,128)(2,1)} %get-tuple-element.25) | copy-start | bytes 3538948
  64.5 2.7 %collective-permute-start.4 = (bf16[24,6,512]{2,1,0:T(8,128)(2,1)S(1)}, bf16[24,6,512]{2,1,0:T(8,128)(2,1)S(1)}, u32[]{:S(2)}, u32[]{:S(2)}) collective-permute-start(bf16[24,6,512]{2,1,0:T(8,128)(2,1)S(1)} %slice.80), channel_id=1, source_target_pairs={{0,1},{1,2},{2,3},{3,4},{4,5},{5,6},{6,7},{7,8},{8,9},{9,10},{10,1... | collective-permute-start | bytes 442376 | tf_op jit(solution)/shard_map/ppermute | solution.py:592
  68.2 8.5 %collective-permute-start.5 = (bf16[3,48,512]{2,1,0:T(8,128)(2,1)S(1)}, bf16[3,48,512]{2,1,0:T(8,128)(2,1)S(1)}, u32[]{:S(2)}, u32[]{:S(2)}) collective-permute-start(bf16[3,48,512]{2,1,0:T(8,128)(2,1)S(1)} %pad_maximum_fusion.5), channel_id=1, source_target_pairs={{0,16},{16,32},{32,48},{48,64},{64,80},{80,96},{96,112},{112,0},{1... | collective-permute-start | bytes 442376 | tf_op jit(solution)/shard_map/ppermute | solution.py:592
  103.3 3.0 %copy-start.3 = (bf16[512,1536]{1,0:T(8,128)(2,1)}, bf16[512,1536]{1,0:T(8,128)(2,1)S(1)}, u32[]{:S(2)}) copy-start(bf16[512,1536]{1,0:T(8,128)(2,1)S(1)} %get-tuple-element.32.gwq_ref) | copy-start | bytes 4718596
  177.7 12.0 %collective-permute-start.6 = (bf16[3,48,512]{2,1,0:T(8,128)(2,1)S(1)}, bf16[3,48,512]{2,1,0:T(8,128)(2,1)S(1)}, u32[]{:S(2)}, u32[]{:S(2)}) collective-permute-start(bf16[3,48,512]{2,1,0:T(8,128)(2,1)S(1)} %slice.106), channel_id=1, source_target_pairs={{0,112},{16,0},{32,16},{48,32},{64,48},{80,64},{96,80},{112,96},{1... | collective-permute-start | bytes 442376 | tf_op jit(solution)/shard_map/ppermute | solution.py:592
  181.9 3.3 %copy-start.10 = (bf16[2048,1024]{1,0:T(8,128)(2,1)S(1)}, bf16[2048,1024]{1,0:T(8,128)(2,1)}, u32[]{:S(2)}) copy-start(bf16[2048,1024]{1,0:T(8,128)(2,1)} %get-tuple-element.38) | copy-start | bytes 12582916
  189.7 5.2 %copy-start.11 = (bf16[24,48,512]{2,1,0:T(8,128)(2,1)S(1)}, bf16[24,48,512]{2,1,0:T(8,128)(2,1)}, u32[]{:S(2)}) copy-start(bf16[24,48,512]{2,1,0:T(8,128)(2,1)} %get-tuple-element.30) | copy-start | bytes 3538948
  189.7 5.2 %collective-permute-start.7 = (bf16[24,6,512]{2,1,0:T(8,128)(2,1)S(1)}, bf16[24,6,512]{2,1,0:T(8,128)(2,1)S(1)}, u32[]{:S(2)}, u32[]{:S(2)}) collective-permute-start(bf16[24,6,512]{2,1,0:T(8,128)(2,1)S(1)} %fusion.2), channel_id=1, source_target_pairs={{0,15},{1,0},{2,1},{3,2},{4,3},{5,4},{6,5},{7,6},{8,7},{9,8},{10,9... | collective-permute-start | bytes 442376 | tf_op jit(solution)/shard_map/ppermute | solution.py:592

commit v3 on v0

v3 whole, which is shorter than its diff:
```python
import functools
import jax
import jax.numpy as jnp
from jax import lax
from jax.experimental import pallas as pl
from jax.experimental.pallas import tpu as pltpu
from jax.sharding import PartitionSpec as P

HEADS = 8
WLAT = 6
WLON = 12
EPSILON = 1e-05
F32 = jnp.float32
BF = jnp.bfloat16
ROWS = 24
COLS = 48
C = 512
WIN = 72
NW = COLS // WLON
PAIRS = HEADS // 2
MIB = 1 << 20


def dot(a, b, ca, cb):
    return lax.dot_general(a, b, (((ca,), (cb,)), ((), ())), preferred_element_type=F32)


def head_masks(scale):
    lane = lax.broadcasted_iota(jnp.int32, (1, 128), 1)
    low = jnp.where(lane < 64, scale, 0.0).astype(F32)
    high = jnp.where(lane < 64, 0.0, scale).astype(F32)
    return low, high


def stacked(value, masks):
    return jnp.concatenate([value * masks[0], value * masks[1]], axis=0).astype(BF)


def merged_heads(value):
    lane = lax.broadcasted_iota(jnp.int32, (WIN, 128), 1)
    return jnp.where(lane < 64, value[:WIN], value[WIN:])


def moments(x):
    mean = jnp.mean(x, axis=-1, keepdims=True)
    centered = x - mean
    var = jnp.mean(centered * centered, axis=-1, keepdims=True)
    rstd = lax.rsqrt(var + EPSILON)
    return centered * rstd, rstd


AXES = ("x", "y", "z")


def coordinates():
    lat = lax.axis_index("lat")
    lon = lax.axis_index("lon")
    return {"x": lon // 4, "y": (lat // 4) * 2 + (lon // 2) % 2, "z": lat % 4, "core": lon % 2}


def device(at):
    return ((at["y"] // 2) * 4 + at["z"], at["x"] * 4 + (at["y"] % 2) * 2 + at["core"])


def peer(at, axis, step):
    size = 2 if axis == "core" else 4
    return device({**at, axis: (at[axis] + step) % size})


def remote(src, dst, send, recv, target):
    return pltpu.make_async_remote_copy(
        src_ref=src, dst_ref=dst, send_sem=send, recv_sem=recv,
        device_id=target, device_id_type=pl.DeviceIdType.MESH,
    )


def neighbour(rows, cols):
    lat = lax.axis_index("lat")
    lon = lax.axis_index("lon")
    return ((lat + rows) % 8, (lon + cols) % 16)


EDGES = ((0, 1), (1, 0), (1, 1))


def greet(at):
    barrier = pltpu.get_barrier_semaphore()
    targets = [
        peer(at, axis, step)
        for axis, count in (("core", 2), ("x", 4), ("y", 4), ("z", 4))
        for step in range(1, count)
    ]
    targets += [neighbour(sign * r, sign * c) for sign in (1, -1) for r, c in EDGES]
    for target in targets:
        pl.semaphore_signal(barrier, inc=1, device_id=target, device_id_type=pl.DeviceIdType.MESH)
    pl.semaphore_wait(barrier, len(targets))


def add_rows(dst, start, terms, rows):
    chunk = min(rows, 64)

    def body(i, carry):
        total = None
        for ref, first in terms:
            piece = ref[pl.ds(pl.multiple_of(first + i * chunk, 16), chunk), :].astype(F32)
            total = piece if total is None else total + piece
        dst[pl.ds(pl.multiple_of(start + i * chunk, 16), chunk), :] = total.astype(dst.dtype)
        return carry

    lax.fori_loop(0, rows // chunk, body, 0)


class Sum:
    def __init__(self, at, src, out, order, recvs, send, recv):
        self.at, self.src, self.out, self.order = at, src, out, order
        self.recvs, self.send, self.recv = recvs, send, recv
        self.rows = src.shape[0]
        self.sent = []

    def start(self, src, dst, index, target):
        copy = remote(src, dst, self.send.at[index], self.recv.at[index], target)
        copy.start()
        self.sent.append(copy)
        return copy

    def block(self, level):
        return self.rows // 2 // 4**level

    def first(self, levels):
        first = self.at["core"] * (self.rows // 2)
        for level in range(levels):
            first = first + self.at[self.order[level]] * self.block(level + 1)
        return pl.multiple_of(first, 16)

    def begin(self):
        half = self.rows // 2
        theirs = pl.ds(pl.multiple_of((1 - self.at["core"]) * half, 16), half)
        self.last = [self.start(self.src.at[theirs, :], self.recvs[0].at[0], 0, peer(self.at, "core", 1))]

    def combine(self, level):
        for copy in self.last:
            copy.wait_recv()
        count = self.block(level)
        first = self.first(level)
        terms = [(self.src, first)] + [(self.recvs[level].at[s], 0) for s in range(1 if level == 0 else 3)]
        if level == 3:
            add_rows(self.out, first, terms, count)
            self.gather(3)
            return
        add_rows(self.src, first, terms, count)
        axis = self.order[level]
        block = self.block(level + 1)
        self.last = []
        for step in range(1, 4):
            there = pl.multiple_of(first + (self.at[axis] + step) % 4 * block, 16)
            self.last.append(
                self.start(
                    self.src.at[pl.ds(there, block), :], self.recvs[level + 1].at[step - 1],
                    3 * level + step, peer(self.at, axis, step),
                )
            )

    def gather(self, level):
        mine = self.out.at[pl.ds(self.first(level), self.block(level)), :]
        if level == 0:
            self.last = [self.start(mine, mine, 19, peer(self.at, "core", 1))]
            return
        axis = self.order[level - 1]
        self.last = [
            self.start(mine, mine, 10 + 3 * (level - 1) + step - 1, peer(self.at, axis, step)) for step in range(1, 4)
        ]

    def gathered(self, level):
        for copy in self.last:
            copy.wait_recv()
        self.gather(level - 1)

    def finish(self):
        self.last[0].wait_recv()
        for copy in self.sent:
            copy.wait_send()

    def step(self, n):
        if n == 0:
            self.begin()
        elif n < 5:
            self.combine(n - 1)
        elif n < 8:
            self.gathered(8 - n)
        else:
            self.finish()


SUM_COPIES = 20


def sum_scratch(rows, lanes):
    half = rows // 2
    return [pltpu.VMEM((1, half, lanes), BF)] + [pltpu.VMEM((3, half // 4**n, lanes), BF) for n in (1, 2, 3)]


class SmallSum:
    def __init__(self, at, block, slots, send, recv):
        self.at, self.block, self.slots, self.send, self.recv = at, block, slots, send, recv
        self.sent = []

    def begin(self, level):
        axis, count = (("core", 2), ("x", 4), ("y", 4), ("z", 4))[level]
        base = 0 if level == 0 else 3 * level - 2
        self.last = []
        for step in range(1, count):
            i = base + step - 1
            copy = remote(self.block.at[level], self.slots.at[i], self.send.at[i], self.recv.at[i],
                          peer(self.at, axis, step))
            copy.start()
            self.last.append((copy, i))
            self.sent.append(copy)

    def end(self, level):
        total = self.block[level]
        for copy, i in self.last:
            copy.wait_recv()
            total = total + self.slots[i]
        self.block[level + 1] = total

    def finish(self):
        for copy in self.sent:
            copy.wait_send()

CH = 4
NCH = ROWS // CH
MT = (CH // 2) * (COLS // 2)
MALL = NCH * MT
C4 = 4 * C
C2 = 1024
WROWS = ROWS // WLAT
NWT = NW * WIN
FR = COLS + 8
TALL = 4 * C


class Halo:
    def __init__(self, sign, send, recv):
        self.sign, self.send, self.recv = sign, send, recv

    def start(self, sources, targets):
        self.copies = []
        for n, (r, c) in enumerate(EDGES):
            copy = remote(sources[n], targets[n], self.send.at[n], self.recv.at[n],
                          neighbour(self.sign * r, self.sign * c))
            copy.start()
            self.copies.append(copy)

    def arrived(self):
        for copy in self.copies:
            copy.wait_recv()

    def left(self):
        for copy in self.copies:
            copy.wait_send()


def pair_half(ref, pair, half):
    return ref[pair].astype(F32)[8 * half : 8 * half + 8]


def load_frame(fr, w, rows_ref, edge_ref):
    for r in range(WLAT):
        fr[r, 8:FR, :] = rows_ref[WLAT * w + r].astype(F32)
        fr[r, 0:8, :] = pair_half(edge_ref, 3 * w + (r + 1) // 2, (r + 1) % 2)


def to_windows(fr, dst):
    for v in range(NW):
        for r in range(WLAT):
            dst[v, WLON * r : WLON * (r + 1), :] = fr[r, WLON * v + 2 : WLON * v + 14, :]


def to_frame(src, fr):
    for v in range(NW):
        for r in range(WLAT):
            fr[r, WLON * v + 2 : WLON * v + 14, :] = src[v, WLON * r : WLON * (r + 1), :]


def pack_rows(fr, edge_ref, w):
    for r in range(0, WLAT, 2):
        edge_ref[3 * w + r // 2] = jnp.concatenate([fr[r, 0:8, :], fr[r + 1, 0:8, :]], axis=0).astype(BF)


def step_body(tok_hbm, bias_ref, ga_ref, wq_hbm, wo_hbm, gm_hbm, wm_hbm, gmg_ref,
              merged_ref, gtok_ref, outm_ref, outq_ref, outs_ref,
              text, hw, pk, wq, wo, gmb, wm, qkv, prob, nrm, qf, s2, fr, attx, he, bw,
              s1, xh, rs, mi, gwm, qo, gmix, gext, gw, pkg, dq, dall, bn2, bw2, hs2, he2,
              small, slots, ggm, gga, lsem, hsend, hrecv, send, recv, ssend, srecv, *sums):
    loads = [
        pltpu.make_async_copy(src, dst, lsem.at[n])
        for n, (src, dst) in enumerate(
            [(tok_hbm, text.at[pl.ds(3, ROWS)]), (wq_hbm, wq), (wo_hbm, wo), (gm_hbm, gmb), (wm_hbm, wm)]
        )
    ]
    for load in loads:
        load.start()
    at = coordinates()
    greet(at)
    halos = [Halo(sign, hsend.at[n], hrecv.at[n]) for n, sign in enumerate((1, -1, 1, -1))]

    loads[0].wait()
    for m in range(ROWS // 2):
        pk[m] = jnp.concatenate(
            [text[3 + 2 * m + k, 32:48, :].astype(F32)[8:16] for k in range(2)], axis=0
        ).astype(BF)
    halos[0].start(
        [pk, text.at[pl.ds(24, 3)], pk.at[pl.ds(10, 2)]],
        [hw.at[pl.ds(2, 12)], text.at[pl.ds(0, 3)], hw.at[pl.ds(0, 2)]],
    )
    loads[1].wait()
    halos[0].arrived()

    def forward_row(w, carry):
        load_frame(fr, w, text, hw)
        xhat, _ = moments(fr[...])
        fr[...] = xhat * ga_ref[...].reshape(1, 1, C)
        to_windows(fr, s2)
        normed = s2[...].reshape(NWT, C).astype(BF)
        nrm[pl.ds(pl.multiple_of(w * NWT, NWT), NWT), :] = normed
        for t in range(3):
            part = dot(normed, wq[:, C * t : C * (t + 1)], 1, 0).reshape(NW, WIN, C)
            if t == 0:
                qf[...] = part
            qkv[pl.ds(NW * w, NW), :, C * t : C * (t + 1)] = part.astype(BF)
        bias = bias_ref[w]

        def window(v, carry):
            masks = head_masks(0.125)
            n = NW * w + v
            for p in range(PAIRS):
                lanes = slice(128 * p, 128 * (p + 1))
                qs = stacked(qf[v, :, lanes].astype(BF).astype(F32), masks)
                k = qkv[n, :, C + 128 * p : C + 128 * (p + 1)]
                val = qkv[n, :, 2 * C + 128 * p : 2 * C + 128 * (p + 1)]
                s = dot(k, qs, 1, 1) + bias
                e = jnp.exp(s - jnp.max(s, axis=0, keepdims=True))
                pr = (e * (1.0 / jnp.sum(e, axis=0, keepdims=True))).astype(BF)
                prob[n, p] = pr
                s2[v, :, lanes] = merged_heads(dot(pr, val, 0, 0))
            return carry

        lax.fori_loop(0, NW, window, 0)
        to_frame(s2, fr)
        pack_rows(fr, bw, w)
        for r in range(WLAT):
            attx[WLAT * w + r] = fr[r, 8:FR, :].astype(BF)
        return carry

    lax.fori_loop(0, WROWS, forward_row, 0)

    halos[1].start(
        [bw, attx.at[pl.ds(0, 3)], bw.at[pl.ds(0, 2)]],
        [he.at[pl.ds(0, 12)], attx.at[pl.ds(24, 3)], he.at[pl.ds(12, 2)]],
    )
    for load in loads[2:]:
        load.wait()
    halos[1].arrived()
    gain = gmg_ref[...]
    lower = lax.broadcasted_iota(jnp.int32, (8, C), 0) < 2

    def merge_forward(c, carry):
        pieces = []
        for i in range(CH):
            row = attx[CH * c + 3 + i].astype(F32)
            edge = pair_half(he, 2 * c + (3 + i) // 2, (3 + i) % 2)
            pieces.append(jnp.concatenate([row[:40], jnp.where(lower, row[40:], edge)], axis=0))
        att = jnp.concatenate(pieces, axis=0).astype(BF)
        attx[pl.ds(CH * c + 3, CH)] = att.reshape(CH, COLS, C)
        proj = dot(att, wo[...], 1, 0).reshape(CH, COLS, C)
        mixed = (text[pl.ds(CH * c + 3, CH)].astype(F32) + proj).astype(BF).astype(F32)
        for q in range(4):
            s1[q] = mixed[:, :, 128 * q : 128 * (q + 1)]
        parts = []
        for b in range(2):
            for a in range(2):
                for q in range(4):
                    piece = [s1[q, 2 * i + a, pl.ds(b, COLS // 2, stride=2), :] for i in range(CH // 2)]
                    parts.append(jnp.concatenate(piece, axis=0))
        xhat, rstd = moments(jnp.concatenate(parts, axis=1))
        here = pl.ds(pl.multiple_of(c * MT, MT), MT)
        xh[here, :] = xhat
        rs[here, :] = rstd
        mi[here, :] = (xhat * gain).astype(BF)
        return carry

    lax.fori_loop(0, NCH, merge_forward, 0)
    gm = gmb[...].astype(F32).reshape(MALL, C2).astype(BF)

    def merged_tile(n, carry):
        cols = pl.ds(pl.multiple_of(n * 256, 256), 256)
        tile = dot(mi[...], wm[:, cols], 1, 0).reshape(ROWS // 2, COLS // 2, 256)
        merged_ref[:, :, cols] = tile.astype(BF)
        return carry

    lax.fori_loop(0, C2 // 256, merged_tile, 0)

    def wide_tile(n, carry):
        cols = pl.ds(pl.multiple_of(n * 256, 256), 256)
        gwm[cols, :] = dot(mi[:, cols], gm, 0, 0).astype(BF)
        mi[:, cols] = dot(gm, wm[cols, :], 1, 1).astype(BF)
        return carry

    lax.fori_loop(0, C4 // 256, wide_tile, 0)

    def summed(src, out, turn, n):
        order = AXES[turn:] + AXES[:turn]
        return Sum(at, src, out, order, sums[4 * n : 4 * n + 4], send.at[n], recv.at[n])

    wide = [
        summed(gwm.at[:, 0:384], outm_ref.at[:, 0:384], 0, 0),
        summed(gwm.at[:, 384:768], outm_ref.at[:, 384:768], 1, 1),
        summed(gwm.at[:, 768:1024], outm_ref.at[:, 768:1024], 2, 2),
    ]
    early = wide + [summed(qo.at[:, 0:128], outq_ref.at[:, 0:128], 2, 3)]
    late = [
        summed(qo.at[:, 128 * (t + 1) : 128 * (t + 2)], outq_ref.at[:, 128 * (t + 1) : 128 * (t + 2)], t, 4 + t)
        for t in range(3)
    ]

    def advance(group, n):
        for part in group:
            part.step(n)

    advance(wide, 0)
    ggm[...] = jnp.zeros_like(ggm)

    def merge_backward(c, carry):
        here = pl.ds(pl.multiple_of(c * MT, MT), MT)
        xhat = xh[here, :]
        g = mi[here, :].astype(F32)
        ggm[...] += jnp.sum(g * xhat, axis=0, keepdims=True)
        dx = g * gain
        m1 = jnp.mean(dx, axis=-1, keepdims=True)
        m2 = jnp.mean(dx * xhat, axis=-1, keepdims=True)
        dx = rs[here, :] * (dx - m1 - xhat * m2)
        for b in range(2):
            for a in range(2):
                for q in range(4):
                    start = C * (2 * b + a) + 128 * q
                    for i in range(CH // 2):
                        s1[q, 2 * i + a, pl.ds(b, COLS // 2, stride=2), :] = dx[
                            (COLS // 2) * i : (COLS // 2) * (i + 1), start : start + 128
                        ]
        mixed = jnp.concatenate([s1[q] for q in range(4)], axis=-1).astype(BF)
        gmix[pl.ds(c * CH, CH)] = mixed
        gatt = dot(mixed.reshape(CH * COLS, C), wo[...], 1, 1).reshape(CH, COLS, C)
        gext[pl.ds(CH * c + 3, CH)] = gatt.astype(BF)
        for m in range(CH // 2):
            pkg[(CH // 2) * c + m] = jnp.concatenate(
                [gatt[2 * m, 40:48], gatt[2 * m + 1, 40:48]], axis=0
            ).astype(BF)
        return carry

    lax.fori_loop(0, NCH, merge_backward, 0)

    halos[2].start(
        [pkg, gext.at[pl.ds(24, 3)], pkg.at[pl.ds(10, 2)]],
        [gw.at[pl.ds(2, 12)], gext.at[pl.ds(0, 3)], gw.at[pl.ds(0, 2)]],
    )
    flat = gmix[...].reshape(ROWS * COLS, C)
    att = attx[pl.ds(3, ROWS)].reshape(ROWS * COLS, C)
    gwo = dot(att, flat, 0, 0).astype(BF)
    for n in range(4):
        qo[C * n : C * (n + 1), 0:128] = gwo[:, 128 * n : 128 * (n + 1)]
    early[3].step(0)
    halos[2].arrived()
    advance(early, 1)

    def backward_row(w, carry):
        load_frame(fr, w, gext, gw)
        to_windows(fr, s2)

        def window(v, carry):
            masks = head_masks(1.0)
            scaled = head_masks(0.125)
            n = NW * w + v
            for p in range(PAIRS):
                lanes = slice(128 * p, 128 * (p + 1))
                qs = stacked(qkv[n, :, lanes].astype(F32), scaled)
                k = qkv[n, :, C + 128 * p : C + 128 * (p + 1)]
                val = qkv[n, :, 2 * C + 128 * p : 2 * C + 128 * (p + 1)]
                gs = stacked(s2[v, :, lanes], masks)
                pr = prob[n, p]
                pf = pr.astype(F32)
                dp = dot(val, gs, 1, 1)
                delta = jnp.sum(pf * dp, axis=0, keepdims=True)
                ds = (pf * (dp - delta)).astype(BF)
                dq[v, :, lanes] = merged_heads(dot(ds, k, 0, 0)) * 0.125
                dq[v, :, C + 128 * p : C + 128 * (p + 1)] = dot(ds, qs, 1, 0)
                dq[v, :, 2 * C + 128 * p : 2 * C + 128 * (p + 1)] = dot(pr, gs, 1, 0)
            return carry

        lax.fori_loop(0, NW, window, 0)
        dall[pl.ds(pl.multiple_of(w * NWT, NWT), NWT), :] = dq[...].reshape(NWT, 3 * C).astype(BF)
        return carry

    lax.fori_loop(0, 2, backward_row, 0)
    advance(early, 2)
    lax.fori_loop(2, 3, backward_row, 0)
    advance(early, 3)
    lax.fori_loop(3, 4, backward_row, 0)
    advance(early, 4)
    for n in range(6):
        tile = dot(nrm[...], dall[:, 256 * n : 256 * (n + 1)], 0, 0).astype(BF)
        for k in range(2):
            g = 2 * n + k
            qo[C * (g // 3) : C * (g // 3 + 1), 128 * (1 + g % 3) : 128 * (2 + g % 3)] = tile[:, 128 * k : 128 * (k + 1)]
    advance(late, 0)
    advance(early, 5)
    gga[...] = jnp.zeros_like(gga)

    def dgrad_row(w, carry):
        rows = pl.ds(pl.multiple_of(w * NWT, NWT), NWT)
        s2[...] = dot(dall[rows, :], wq[...], 1, 1).astype(BF).astype(F32).reshape(NW, WIN, C)
        load_frame(fr, w, text, hw)
        xhat, rstd = moments(fr[...])
        fr[:, 0:8, :] = jnp.zeros((WLAT, 8, C), F32)
        fr[:, FR - 8 : FR, :] = jnp.zeros((WLAT, 8, C), F32)
        to_frame(s2, fr)
        g = fr[...]
        gga[...] += jnp.sum(g * xhat, axis=(0, 1)).reshape(1, C)
        dx = g * ga_ref[...].reshape(1, 1, C)
        m1 = jnp.mean(dx, axis=-1, keepdims=True)
        m2 = jnp.mean(dx * xhat, axis=-1, keepdims=True)
        fr[...] = rstd * (dx - m1 - xhat * m2)
        pack_rows(fr, bw2, w)
        for r in range(3):
            bn2[WLAT * w + r] = fr[r, 8:FR, :].astype(BF)
        for r in range(3):
            gtok_ref[WLAT * w + r] = fr[3 + r, 8:FR, :] + gmix[WLAT * w + r].astype(F32)

        @pl.when(w > 0)
        def _():
            for r in range(3):
                gtok_ref[WLAT * w - 3 + r] = fr[r, 8:FR, :] + gmix[WLAT * w - 3 + r].astype(F32)

        return carry

    lax.fori_loop(0, 1, dgrad_row, 0)
    advance(late, 1)
    lax.fori_loop(1, 2, dgrad_row, 0)
    advance(early, 6)
    advance(late, 2)
    lax.fori_loop(2, 4, dgrad_row, 0)
    halos[3].start(
        [bw2, bn2.at[pl.ds(0, 3)], bw2.at[pl.ds(0, 2)]],
        [he2.at[pl.ds(0, 12)], hs2, he2.at[pl.ds(12, 2)]],
    )
    small[0] = jnp.zeros_like(small[0])
    small[0, 0:1, :] = gga[...]
    for n in range(4):
        small[0, 1 + n : 2 + n, :] = ggm[:, C * n : C * (n + 1)]
    gains = SmallSum(at, small, slots, ssend, srecv)
    gains.begin(0)
    advance(late, 3)
    gains.end(0)
    gains.begin(1)
    advance(late, 4)
    halos[3].arrived()
    for r in range(3):
        gtok_ref[21 + r] = hs2[r].astype(F32) + gmix[21 + r].astype(F32)
    for r in range(ROWS):
        edge = pair_half(he2, (r + 3) // 2, (r + 3) % 2) + gmix[r, 32:48, :].astype(F32)[8:16]
        gtok_ref[r, 40:48, :] = jnp.where(lower, gtok_ref[r, 40:48, :], edge)
    gains.end(1)
    gains.begin(2)
    advance(late, 5)
    gains.end(2)
    gains.begin(3)
    advance(early, 7)
    advance(late, 6)
    gains.end(3)
    outs_ref[...] = small[4]
    advance(late, 7)
    advance(early, 8)
    advance(late, 8)
    gains.finish()
    for halo in halos:
        halo.left()


def step_kernel(tokens, bias, gain_a, w_qkv, w_out, grad_merged, w_merge, gain_m):
    vmem = pl.BlockSpec(memory_space=pltpu.VMEM)
    hbm = pl.BlockSpec(memory_space=pl.ANY)
    lanes = (384, 384, 256, 128, 128, 128, 128)
    sums = []
    for n in lanes:
        sums += sum_scratch(TALL, n)
    return pl.pallas_call(
        step_body,
        in_specs=[hbm, vmem, vmem, hbm, hbm, hbm, hbm, vmem],
        out_specs=[vmem] * 5,
        out_shape=[
            jax.ShapeDtypeStruct((ROWS // 2, COLS // 2, C2), BF),
            jax.ShapeDtypeStruct((ROWS, COLS, C), F32),
            jax.ShapeDtypeStruct((C4, C2), BF),
            jax.ShapeDtypeStruct((TALL, C), BF),
            jax.ShapeDtypeStruct((8, C), F32),
        ],
        scratch_shapes=[
            pltpu.VMEM((27, COLS, C), BF),
            pltpu.VMEM((14, 16, C), BF),
            pltpu.VMEM((12, 16, C), BF),
            pltpu.VMEM((C, 3 * C), BF),
            pltpu.VMEM((C, C), BF),
            pltpu.VMEM((ROWS // 2, COLS // 2, C2), BF),
            pltpu.VMEM((C4, C2), BF),
            pltpu.VMEM((WROWS * NW, WIN, 3 * C), BF),
            pltpu.VMEM((WROWS * NW, PAIRS, WIN, 2 * WIN), BF),
            pltpu.VMEM((ROWS * COLS, C), BF),
            pltpu.VMEM((NW, WIN, C), F32),
            pltpu.VMEM((NW, WIN, C), F32),
            pltpu.VMEM((WLAT, FR, C), F32),
            pltpu.VMEM((27, COLS, C), BF),
            pltpu.VMEM((14, 16, C), BF),
            pltpu.VMEM((12, 16, C), BF),
            pltpu.VMEM((4, CH, COLS, 128), F32),
            pltpu.VMEM((MALL, C4), F32),
            pltpu.VMEM((MALL, 1), F32),
            pltpu.VMEM((MALL, C4), BF),
            pltpu.VMEM((C4, C2), BF),
            pltpu.VMEM((TALL, C), BF),
            pltpu.VMEM((ROWS, COLS, C), BF),
            pltpu.VMEM((27, COLS, C), BF),
            pltpu.VMEM((14, 16, C), BF),
            pltpu.VMEM((12, 16, C), BF),
            pltpu.VMEM((NW, WIN, 3 * C), F32),
            pltpu.VMEM((ROWS * COLS, 3 * C), BF),
            pltpu.VMEM((21, COLS, C), BF),
            pltpu.VMEM((12, 16, C), BF),
            pltpu.VMEM((3, COLS, C), BF),
            pltpu.VMEM((14, 16, C), BF),
            pltpu.VMEM((5, 8, C), F32),
            pltpu.VMEM((10, 8, C), F32),
            pltpu.VMEM((1, C4), F32),
            pltpu.VMEM((1, C), F32),
            pltpu.SemaphoreType.DMA((5,)),
            pltpu.SemaphoreType.DMA((4, 3)),
            pltpu.SemaphoreType.DMA((4, 3)),
            pltpu.SemaphoreType.DMA((7, SUM_COPIES)),
            pltpu.SemaphoreType.DMA((7, SUM_COPIES)),
            pltpu.SemaphoreType.DMA((10,)),
            pltpu.SemaphoreType.DMA((10,)),
        ]
        + sums,
        compiler_params=pltpu.CompilerParams(
            vmem_limit_bytes=62 * MIB, collective_id=0, has_side_effects=True
        ),
        name="step",
    )(tokens, bias, gain_a, w_qkv, w_out, grad_merged, w_merge, gain_m)


def on_device(tokens, lat_band, gain_attn, w_qkv, w_out, gain_merge, w_merge, grad_merged):
    half_lat = WLAT // 2
    band_count = lat_band.shape[0]
    extended = jnp.concatenate([lat_band[band_count - half_lat :], lat_band])
    band_rows = lax.dynamic_slice_in_dim(extended, lax.axis_index("lat") * ROWS, ROWS)
    labels = jnp.repeat(band_rows.reshape(-1, WLAT), WLON, axis=1)
    bias = jnp.where(labels[:, :, None] == jnp.tile(labels, (1, 2))[:, None, :], 0.0, -1e30).astype(F32)
    merged, grad_tokens, sum_merge, sum_qo, sum_gain = step_kernel(
        tokens, bias, gain_attn.reshape(1, C), w_qkv, w_out, grad_merged, w_merge, gain_merge.reshape(1, C4)
    )
    groups = [sum_qo[C * (g // 3) : C * (g // 3 + 1), 128 * (1 + g % 3) : 128 * (2 + g % 3)] for g in range(12)]
    outs = [sum_qo[C * n : C * (n + 1), 0:128] for n in range(4)]
    return (
        merged,
        grad_tokens,
        sum_gain[0],
        jnp.concatenate(groups, axis=1).astype(F32),
        jnp.concatenate(outs, axis=1).astype(F32),
        sum_gain[1:5].reshape(C4),
        sum_merge.astype(F32),
    )


def solution(mesh):
    return jax.shard_map(
        on_device,
        mesh=mesh,
        in_specs=(P("lat", "lon", None), P(), P(), P(), P(), P(), P(), P("lat", "lon", None)),
        out_specs=(P("lat", "lon", None), P("lat", "lon", None), P(), P(), P(), P(), P()),
        check_vma=False,
    )
```

time: 432 us -> 151 us (0.35); the launches traced: 427 us -> 151 us
  local copies, waits for them, and re-layouts: 141 us -> 8.67 us
  Pallas kernels: 0 us -> 132 us
  waiting for transfers between devices: 96.2 us -> 0 us
  blocking collectives: 67.9 us -> 0 us
  matrix products: 61.2 us -> 0 us
  other arithmetic: 33.7 us -> 9.12 us
  between operations: 14.8 us -> 0.67 us
  starting transfers between devices: 12.5 us -> 0 us
    pallas_call x0 -> x1, Pallas kernels: none -> 132 us  [step_kernel(): pl.pallas_call(step_body, in_specs=[hbm, vmem, vmem, hbm, hbm, hbm, hbm,...]
    psum x1 -> x0, waiting for transfers between devices: 77.6 us -> none  [on_device(): lax.psum((grad_gain_attn, grad_w_qkv, grad_w_out, grad_gain_merge, grad_w...]
    psum x1 -> x0, blocking collectives: 67.9 us -> none  [on_device(): lax.psum((grad_gain_attn, grad_w_qkv, grad_w_out, grad_gain_merge, grad_w...]
    dot_general x14 -> x0, matrix products: 54.7 us -> none  [the longest x3 13.1 us: windows_attend(): jnp.einsum('abhqk,abkhd->abqhd', attn_weights, value_rows, preferred_elem...]
    reshape x11 -> x1, local copies, waits for them, and re-layouts: 42.9 us -> 0.08 us  [on_device(): labels = jnp.repeat(band_rows.reshape(-1, WLAT), WLON, axis=1)]
    convert_element_type x9 -> x0, local copies, waits for them, and re-layouts: 34.1 us -> none  [the longest x5 17.6 us: section_three(): merge_groups(values).astype(jnp.float32)]
    slice x10 -> x3, local copies, waits for them, and re-layouts: 22.6 us -> 3.95 us  [the longest x1 1.51 us: on_device(): sum_qo[C * (g // 3):C * (g // 3 + 1), 128 * (1 + g % 3):128 * (2 + g % 3)]]
    ppermute x8 -> x0, waiting for transfers between devices: 18.6 us -> none  [shifted_2(): return lax.ppermute(value, axis, pairs)]
  transfers between devices with their start and end apart: 9 -> 0, of which waited for: 6 -> 0; matrix products, arithmetic and copies ran while one was open for 10% -> 0% of each run, Pallas kernels for 0% -> 0%
where the time goes in v3:
time: 151 us
  Pallas kernels  132 us (87%)
  other arithmetic  9.12 us (6%)
  local copies, waits for them, and re-layouts  8.67 us (6%)
    pallas_call x1, Pallas kernels, step_kernel(): pl.pallas_call(step_body, in_specs=[hbm, vmem, vmem, hbm, hbm, hbm, hbm,...  132 us
    convert_element_type x1, other arithmetic, on_device(): sum_merge.astype(F32)  4.44 us
    unnamed x10, local copies, waits for them, and re-layouts  3.55 us

profile of v3, /device:TPU:1, one launch (start us, length us, event | category | flops | bytes accessed | tf_op | source)
XLA Modules:
  0.0 150.9 jit_solution(4777397877440889045)
XLA Ops:
  0.6 0.8 slice.45
  1.4 0.8 pad_add_fusion
  2.1 0.1 dynamic_slice.3
  2.2 0.1 reshape.33
  2.3 0.1 broadcast_in_dim.11
  2.4 0.1 eq.15
  2.5 0.1 tile.8
  2.6 0.8 compare_select_fusion.bias_ref
  3.4 132.5 %step.1 = (bf16[12,24,1024]{2,1,0:T(8,128)(2,1)}, f32[24,48,512]{2,1,0:T(8,128)}, bf16[2048,1024]{1,0:T(8,128)(2,1)}, bf16[2048,512]{1,0:T(8,128)(2,1)}, f32[8,512]{1,0:T(8,128)}) custom-call(bf16[24,48,512]{2,1,0:T(8,128)(2,1)} %tok_hbm.1, f32[4,72,144]{2,1,0:T(8,128)} %compare_select_fusion.bias_ref, f32[1,512]{1,0:T(1,128)} %bitcast.9, ...), custom_call_target="tpu_custom_call" | custom-call | tf_op jit(solution)/shard_map/step/pallas_call | solution.py:595
  135.9 1.3 slice.46
  137.2 0.7 slice_bitcast_fusion
  137.9 0.6 copy.15
  138.5 1.1 fusion
  139.6 1.5 %fusion.1 = (bf16[512,384]{1,0:T(8,128)(2,1)S(1)}, bf16[512,384]{1,0:T(8,128)(2,1)S(1)}, bf16[512,384]{1,0:T(8,128)(2,1)S(1)}, bf16[512,384]{1,0:T(8,128)(2,1)S(1)}) fusion(bf16[2048,512]{1,0:T(8,128)(2,1)} %get-tuple-element.15), kind=kLoop, calls=%fused_computation.6 | loop fusion | bytes 3145728 | tf_op jit(solution)/shard_map/slice | solution.py:669
  141.2 0.0 copy-start
  141.2 1.0 maximum_convert_fusion.1
  142.2 2.1 %maximum_convert_fusion = f32[512,1536]{1,0:T(8,128)} fusion(bf16[512,384]{1,0:T(8,128)(2,1)S(1)} %get-tuple-element.22, bf16[512,384]{1,0:T(8,128)(2,1)S(1)} %get-tuple-element.23, bf16[512,384]{1,0:T(8,128)(2,1)S(1)} %get-tuple-element.24, bf16[512,384]{1,0:T(8,128)(2,1)S(1)} %get-tuple-element.21), kind=kLoop, calls=%fused_computation | loop fusion | flops 6291456 | bytes 4718592 | tf_op jit(solution)/shard_map/convert_element_type | solution.py:675
  144.3 0.0 copy-done
  144.3 0.0 copy-start.2
  144.3 0.0 copy-start.1
  144.3 4.4 %convert_element_type.11 = f32[2048,1024]{1,0:T(8,128)} convert(bf16[2048,1024]{1,0:T(8,128)(2,1)S(1)} %copy-done) | non-fusion elementwise | flops 2097152 | bytes 12582912 | tf_op jit(solution)/shard_map/convert_element_type | solution.py:678
  148.7 0.0 copy-done.2
  148.7 0.8 copy.18
  149.5 0.0 copy-done.1
  149.5 1.4 copy.19
  (1 shorter events, 0.0 us)
Async XLA Ops:
  141.2 3.1 %copy-start = (bf16[2048,1024]{1,0:T(8,128)(2,1)S(1)}, bf16[2048,1024]{1,0:T(8,128)(2,1)}, u32[]{:S(2)}) copy-start(bf16[2048,1024]{1,0:T(8,128)(2,1)} %get-tuple-element.16) | copy-start | bytes 12582916
  144.3 4.4 %copy-start.2 = (bf16[12,24,1024]{2,1,0:T(8,128)(2,1)S(1)}, bf16[12,24,1024]{2,1,0:T(8,128)(2,1)}, u32[]{:S(2)}) copy-start(bf16[12,24,1024]{2,1,0:T(8,128)(2,1)} %get-tuple-element.32) | copy-start | bytes 1769476
  144.3 5.3 %copy-start.1 = (f32[24,48,512]{2,1,0:T(8,128)S(1)}, f32[24,48,512]{2,1,0:T(8,128)}, u32[]{:S(2)}) copy-start(f32[24,48,512]{2,1,0:T(8,128)} %get-tuple-element.33) | copy-start | bytes 7077892

commit v4 on v3

--- a/solution.py
+++ b/solution.py
@@ -240,24 +240,39 @@
 
 
 class Halo:
-    def __init__(self, sign, send, recv):
-        self.sign, self.send, self.recv = sign, send, recv
-
-    def start(self, sources, targets):
-        self.copies = []
-        for n, (r, c) in enumerate(EDGES):
-            copy = remote(sources[n], targets[n], self.send.at[n], self.recv.at[n],
-                          neighbour(self.sign * r, self.sign * c))
-            copy.start()
-            self.copies.append(copy)
-
-    def arrived(self):
-        for copy in self.copies:
-            copy.wait_recv()
+    def __init__(self, send, recv):
+        self.send, self.recv, self.copies = send, recv, []
+
+    def start(self, src, dst, rows, cols):
+        n = len(self.copies)
+        copy = remote(src, dst, self.send.at[n], self.recv.at[n], neighbour(rows, cols))
+        copy.start()
+        self.copies.append(copy)
+        return copy
 
     def left(self):
         for copy in self.copies:
             copy.wait_send()
+
+
+def band_bias(band_ref, bias):
+    band = band_ref[...].astype(F32)
+    total = band.shape[1]
+
+    def grid_row(place, first):
+        row = first + jnp.floor((place.astype(F32) + 0.5) * (1.0 / WLON)).astype(jnp.int32)
+        return jnp.where(row >= total, row - total, row)
+
+    for w in range(WROWS):
+        first = (lax.axis_index("lat") * ROWS + WLAT * w - 3 + total) % total
+        key = lax.broadcasted_iota(jnp.int32, (WIN, total), 0)
+        hit = grid_row(key, first) == lax.broadcasted_iota(jnp.int32, (WIN, total), 1)
+        keys = jnp.sum(jnp.where(hit, band, 0.0), axis=1, keepdims=True)
+        query = lax.broadcasted_iota(jnp.int32, (total, 2 * WIN), 1)
+        query = jnp.where(query >= WIN, query - WIN, query)
+        hit = grid_row(query, first) == lax.broadcasted_iota(jnp.int32, (total, 2 * WIN), 0)
+        queries = dot(jnp.broadcast_to(band, (8, total)).astype(BF), jnp.where(hit, 1.0, 0.0).astype(BF), 1, 0)
+        bias[w] = jnp.where(keys == queries[0:1], 0.0, -1e30)
 
 
 def pair_half(ref, pair, half):
@@ -287,11 +302,11 @@
         edge_ref[3 * w + r // 2] = jnp.concatenate([fr[r, 0:8, :], fr[r + 1, 0:8, :]], axis=0).astype(BF)
 
 
-def step_body(tok_hbm, bias_ref, ga_ref, wq_hbm, wo_hbm, gm_hbm, wm_hbm, gmg_ref,
+def step_body(tok_hbm, band_ref, ga_ref, wq_hbm, wo_hbm, gm_hbm, wm_hbm, gmg_ref,
               merged_ref, gtok_ref, outm_ref, outq_ref, outs_ref,
               text, hw, pk, wq, wo, gmb, wm, qkv, prob, nrm, qf, s2, fr, attx, he, bw,
-              s1, xh, rs, mi, gwm, qo, gmix, gext, gw, pkg, dq, dall, bn2, bw2, hs2, he2,
-              small, slots, ggm, gga, lsem, hsend, hrecv, send, recv, ssend, srecv, *sums):
+              s1, xh, rs, mi, gi, gwm, qo, gmix, gext, gw, pkg, dq, dall, bn2, bw2, hs2, he2,
+              small, slots, ggm, gga, bias, lsem, hsend, hrecv, send, recv, ssend, srecv, *sums):
     loads = [
         pltpu.make_async_copy(src, dst, lsem.at[n])
         for n, (src, dst) in enumerate(
@@ -302,19 +317,23 @@
         load.start()
     at = coordinates()
     greet(at)
-    halos = [Halo(sign, hsend.at[n], hrecv.at[n]) for n, sign in enumerate((1, -1, 1, -1))]
+    halos = [Halo(hsend.at[n], hrecv.at[n]) for n in range(4)]
 
     loads[0].wait()
-    for m in range(ROWS // 2):
-        pk[m] = jnp.concatenate(
-            [text[3 + 2 * m + k, 32:48, :].astype(F32)[8:16] for k in range(2)], axis=0
-        ).astype(BF)
-    halos[0].start(
-        [pk, text.at[pl.ds(24, 3)], pk.at[pl.ds(10, 2)]],
-        [hw.at[pl.ds(2, 12)], text.at[pl.ds(0, 3)], hw.at[pl.ds(0, 2)]],
-    )
+
+    def pack_tokens(first, count):
+        for m in range(first, first + count):
+            pk[m] = jnp.concatenate(
+                [text[3 + 2 * m + k, 32:48, :].astype(F32)[8:16] for k in range(2)], axis=0
+            ).astype(BF)
+        return halos[0].start(pk.at[pl.ds(first, count)], hw.at[pl.ds(first + 2, count)], 0, 1)
+
+    north = [halos[0].start(text.at[pl.ds(24, 3)], text.at[pl.ds(0, 3)], 1, 0)]
+    west = [pack_tokens(1, 4), pack_tokens(5, 7)]
+    north.append(pack_tokens(0, 1))
+    north.append(halos[0].start(pk.at[pl.ds(10, 2)], hw.at[pl.ds(0, 2)], 1, 1))
+    band_bias(band_ref, bias)
     loads[1].wait()
-    halos[0].arrived()
 
     def forward_row(w, carry):
         load_frame(fr, w, text, hw)
@@ -328,7 +347,7 @@
             if t == 0:
                 qf[...] = part
             qkv[pl.ds(NW * w, NW), :, C * t : C * (t + 1)] = part.astype(BF)
-        bias = bias_ref[w]
+        mask = bias[w]
 
         def window(v, carry):
             masks = head_masks(0.125)
@@ -338,7 +357,7 @@
                 qs = stacked(qf[v, :, lanes].astype(BF).astype(F32), masks)
                 k = qkv[n, :, C + 128 * p : C + 128 * (p + 1)]
                 val = qkv[n, :, 2 * C + 128 * p : 2 * C + 128 * (p + 1)]
-                s = dot(k, qs, 1, 1) + bias
+                s = dot(k, qs, 1, 1) + mask
                 e = jnp.exp(s - jnp.max(s, axis=0, keepdims=True))
                 pr = (e * (1.0 / jnp.sum(e, axis=0, keepdims=True))).astype(BF)
                 prob[n, p] = pr
@@ -352,15 +371,28 @@
             attx[WLAT * w + r] = fr[r, 8:FR, :].astype(BF)
         return carry
 
-    lax.fori_loop(0, WROWS, forward_row, 0)
-
-    halos[1].start(
-        [bw, attx.at[pl.ds(0, 3)], bw.at[pl.ds(0, 2)]],
-        [he.at[pl.ds(0, 12)], attx.at[pl.ds(24, 3)], he.at[pl.ds(12, 2)]],
-    )
+    def send_back(w):
+        return halos[1].start(bw.at[pl.ds(3 * w, 3)], he.at[pl.ds(3 * w, 3)], 0, -1)
+
+    west[0].wait_recv()
+    lax.fori_loop(1, 2, forward_row, 0)
+    east = [send_back(1)]
+    for copy in north + west[1:]:
+        copy.wait_recv()
+    lax.fori_loop(0, 1, forward_row, 0)
+    south = [
+        halos[1].start(attx.at[pl.ds(0, 3)], attx.at[pl.ds(24, 3)], -1, 0),
+        halos[1].start(bw.at[pl.ds(0, 2)], he.at[pl.ds(12, 2)], -1, -1),
+    ]
+    east.append(send_back(0))
+    lax.fori_loop(2, 3, forward_row, 0)
+    east.append(send_back(2))
+    lax.fori_loop(3, 4, forward_row, 0)
+    south.append(send_back(3))
     for load in loads[2:]:
         load.wait()
-    halos[1].arrived()
+    for copy in east:
+        copy.wait_recv()
     gain = gmg_ref[...]
     lower = lax.broadcasted_iota(jnp.int32, (8, C), 0) < 2
 
@@ -389,7 +421,10 @@
         mi[here, :] = (xhat * gain).astype(BF)
         return carry
 
-    lax.fori_loop(0, NCH, merge_forward, 0)
+    lax.fori_loop(0, 3, merge_forward, 0)
+    for copy in south:
+        copy.wait_recv()
+    lax.fori_loop(3, NCH, merge_forward, 0)
     gm = gmb[...].astype(F32).reshape(MALL, C2).astype(BF)
 
     def merged_tile(n, carry):
@@ -398,12 +433,11 @@
         merged_ref[:, :, cols] = tile.astype(BF)
         return carry
 
-    lax.fori_loop(0, C2 // 256, merged_tile, 0)
 
     def wide_tile(n, carry):
         cols = pl.ds(pl.multiple_of(n * 256, 256), 256)
         gwm[cols, :] = dot(mi[:, cols], gm, 0, 0).astype(BF)
-        mi[:, cols] = dot(gm, wm[cols, :], 1, 1).astype(BF)
+        gi[:, cols] = dot(gm, wm[cols, :], 1, 1).astype(BF)
         return carry
 
     lax.fori_loop(0, C4 // 256, wide_tile, 0)
@@ -433,7 +467,7 @@
     def merge_backward(c, carry):
         here = pl.ds(pl.multiple_of(c * MT, MT), MT)
         xhat = xh[here, :]
-        g = mi[here, :].astype(F32)
+        g = gi[here, :].astype(F32)
         ggm[...] += jnp.sum(g * xhat, axis=0, keepdims=True)
         dx = g * gain
         m1 = jnp.mean(dx, axis=-1, keepdims=True)
@@ -457,20 +491,26 @@
             ).astype(BF)
         return carry
 
-    lax.fori_loop(0, NCH, merge_backward, 0)
-
-    halos[2].start(
-        [pkg, gext.at[pl.ds(24, 3)], pkg.at[pl.ds(10, 2)]],
-        [gw.at[pl.ds(2, 12)], gext.at[pl.ds(0, 3)], gw.at[pl.ds(0, 2)]],
-    )
+    def send_cotangents(first, count):
+        return halos[2].start(pkg.at[pl.ds(first, count)], gw.at[pl.ds(first + 2, count)], 0, 1)
+
+    lax.fori_loop(5, 6, merge_backward, 0)
+    halos[2].start(gext.at[pl.ds(24, 3)], gext.at[pl.ds(0, 3)], 1, 0)
+    halos[2].start(pkg.at[pl.ds(10, 2)], gw.at[pl.ds(0, 2)], 1, 1)
+    send_cotangents(10, 2)
+    lax.fori_loop(0, 3, merge_backward, 0)
+    send_cotangents(0, 6)
+    lax.fori_loop(3, 5, merge_backward, 0)
+    send_cotangents(6, 4)
     flat = gmix[...].reshape(ROWS * COLS, C)
     att = attx[pl.ds(3, ROWS)].reshape(ROWS * COLS, C)
     gwo = dot(att, flat, 0, 0).astype(BF)
     for n in range(4):
         qo[C * n : C * (n + 1), 0:128] = gwo[:, 128 * n : 128 * (n + 1)]
     early[3].step(0)
-    halos[2].arrived()
     advance(early, 1)
+    for copy in halos[2].copies:
+        copy.wait_recv()
 
     def backward_row(w, carry):
         load_frame(fr, w, gext, gw)
@@ -500,19 +540,17 @@
         dall[pl.ds(pl.multiple_of(w * NWT, NWT), NWT), :] = dq[...].reshape(NWT, 3 * C).astype(BF)
         return carry
 
-    lax.fori_loop(0, 2, backward_row, 0)
+    lax.fori_loop(0, 3, backward_row, 0)
     advance(early, 2)
-    lax.fori_loop(2, 3, backward_row, 0)
+    lax.fori_loop(3, 4, backward_row, 0)
     advance(early, 3)
-    lax.fori_loop(3, 4, backward_row, 0)
-    advance(early, 4)
     for n in range(6):
         tile = dot(nrm[...], dall[:, 256 * n : 256 * (n + 1)], 0, 0).astype(BF)
         for k in range(2):
             g = 2 * n + k
             qo[C * (g // 3) : C * (g // 3 + 1), 128 * (1 + g % 3) : 128 * (2 + g % 3)] = tile[:, 128 * k : 128 * (k + 1)]
     advance(late, 0)
-    advance(early, 5)
+    advance(early, 4)
     gga[...] = jnp.zeros_like(gga)
 
     def dgrad_row(w, carry):
@@ -543,15 +581,17 @@
         return carry
 
     lax.fori_loop(0, 1, dgrad_row, 0)
+    halos[3].start(bn2.at[pl.ds(0, 3)], hs2, -1, 0)
+    halos[3].start(bw2.at[pl.ds(0, 2)], he2.at[pl.ds(12, 2)], -1, -1)
     advance(late, 1)
     lax.fori_loop(1, 2, dgrad_row, 0)
+    halos[3].start(bw2.at[pl.ds(0, 6)], he2.at[pl.ds(0, 6)], 0, -1)
+    advance(early, 5)
+    lax.fori_loop(2, 4, dgrad_row, 0)
+    halos[3].start(bw2.at[pl.ds(6, 6)], he2.at[pl.ds(6, 6)], 0, -1)
+    advance(late, 2)
     advance(early, 6)
-    advance(late, 2)
-    lax.fori_loop(2, 4, dgrad_row, 0)
-    halos[3].start(
-        [bw2, bn2.at[pl.ds(0, 3)], bw2.at[pl.ds(0, 2)]],
-        [he2.at[pl.ds(0, 12)], hs2, he2.at[pl.ds(12, 2)]],
-    )
+    lax.fori_loop(0, C2 // 256, merged_tile, 0)
     small[0] = jnp.zeros_like(small[0])
     small[0, 0:1, :] = gga[...]
     for n in range(4):
@@ -562,7 +602,8 @@
     gains.end(0)
     gains.begin(1)
     advance(late, 4)
-    halos[3].arrived()
+    for copy in halos[3].copies:
+        copy.wait_recv()
     for r in range(3):
         gtok_ref[21 + r] = hs2[r].astype(F32) + gmix[21 + r].astype(F32)
     for r in range(ROWS):
@@ -585,7 +626,7 @@
         halo.left()
 
 
-def step_kernel(tokens, bias, gain_a, w_qkv, w_out, grad_merged, w_merge, gain_m):
+def step_kernel(tokens, band, gain_a, w_qkv, w_out, grad_merged, w_merge, gain_m):
     vmem = pl.BlockSpec(memory_space=pltpu.VMEM)
     hbm = pl.BlockSpec(memory_space=pl.ANY)
     lanes = (384, 384, 256, 128, 128, 128, 128)
@@ -624,6 +665,7 @@
             pltpu.VMEM((MALL, C4), F32),
             pltpu.VMEM((MALL, 1), F32),
             pltpu.VMEM((MALL, C4), BF),
+            pltpu.VMEM((MALL, C4), BF),
             pltpu.VMEM((C4, C2), BF),
             pltpu.VMEM((TALL, C), BF),
             pltpu.VMEM((ROWS, COLS, C), BF),
@@ -640,9 +682,10 @@
             pltpu.VMEM((10, 8, C), F32),
             pltpu.VMEM((1, C4), F32),
             pltpu.VMEM((1, C), F32),
+            pltpu.VMEM((WROWS, WIN, 2 * WIN), F32),
             pltpu.SemaphoreType.DMA((5,)),
-            pltpu.SemaphoreType.DMA((4, 3)),
-            pltpu.SemaphoreType.DMA((4, 3)),
+            pltpu.SemaphoreType.DMA((4, 6)),
+            pltpu.SemaphoreType.DMA((4, 6)),
             pltpu.SemaphoreType.DMA((7, SUM_COPIES)),
             pltpu.SemaphoreType.DMA((7, SUM_COPIES)),
             pltpu.SemaphoreType.DMA((10,)),
@@ -653,30 +696,53 @@
             vmem_limit_bytes=62 * MIB, collective_id=0, has_side_effects=True
         ),
         name="step",
-    )(tokens, bias, gain_a, w_qkv, w_out, grad_merged, w_merge, gain_m)
+    )(tokens, band, gain_a, w_qkv, w_out, grad_merged, w_merge, gain_m)
+
+
+def widen_body(m_ref, q_ref, s_ref, gm_ref, gq_ref, go_ref, ga_ref, gg_ref):
+    gm_ref[...] = m_ref[...].astype(F32)
+    go_ref[...] = q_ref[:, 0:128].astype(F32)
+    gq_ref[...] = q_ref[:, 128:].astype(F32)
+    ga_ref[...] = s_ref[0:1, :]
+    for n in range(4):
+        gg_ref[:, C * n : C * (n + 1)] = s_ref[1 + n : 2 + n, :]
+
+
+def widen(sum_merge, sum_qo, sum_gain):
+    return pl.pallas_call(
+        widen_body,
+        grid=(4,),
+        in_specs=[
+            pl.BlockSpec((C, C2), lambda i: (i, 0)),
+            pl.BlockSpec((C, C), lambda i: (i, 0)),
+            pl.BlockSpec((8, C), lambda i: (0, 0)),
+        ],
+        out_specs=[
+            pl.BlockSpec((C, C2), lambda i: (i, 0)),
+            pl.BlockSpec((C, 384), lambda i: (0, i)),
+            pl.BlockSpec((C, 128), lambda i: (0, i)),
+            pl.BlockSpec((1, C), lambda i: (0, 0)),
+            pl.BlockSpec((1, C4), lambda i: (0, 0)),
+        ],
+        out_shape=[
+            jax.ShapeDtypeStruct((C4, C2), F32),
+            jax.ShapeDtypeStruct((C, 3 * C), F32),
+            jax.ShapeDtypeStruct((C, C), F32),
+            jax.ShapeDtypeStruct((1, C), F32),
+            jax.ShapeDtypeStruct((1, C4), F32),
+        ],
+        compiler_params=pltpu.CompilerParams(vmem_limit_bytes=32 * MIB),
+        name="widen",
+    )(sum_merge, sum_qo, sum_gain)
 
 
 def on_device(tokens, lat_band, gain_attn, w_qkv, w_out, gain_merge, w_merge, grad_merged):
-    half_lat = WLAT // 2
-    band_count = lat_band.shape[0]
-    extended = jnp.concatenate([lat_band[band_count - half_lat :], lat_band])
-    band_rows = lax.dynamic_slice_in_dim(extended, lax.axis_index("lat") * ROWS, ROWS)
-    labels = jnp.repeat(band_rows.reshape(-1, WLAT), WLON, axis=1)
-    bias = jnp.where(labels[:, :, None] == jnp.tile(labels, (1, 2))[:, None, :], 0.0, -1e30).astype(F32)
     merged, grad_tokens, sum_merge, sum_qo, sum_gain = step_kernel(
-        tokens, bias, gain_attn.reshape(1, C), w_qkv, w_out, grad_merged, w_merge, gain_merge.reshape(1, C4)
+        tokens, lat_band.reshape(1, -1), gain_attn.reshape(1, C), w_qkv, w_out, grad_merged, w_merge,
+        gain_merge.reshape(1, C4)
     )
-    groups = [sum_qo[C * (g // 3) : C * (g // 3 + 1), 128 * (1 + g % 3) : 128 * (2 + g % 3)] for g in range(12)]
-    outs = [sum_qo[C * n : C * (n + 1), 0:128] for n in range(4)]
-    return (
-        merged,
-        grad_tokens,
-        sum_gain[0],
-        jnp.concatenate(groups, axis=1).astype(F32),
-        jnp.concatenate(outs, axis=1).astype(F32),
-        sum_gain[1:5].reshape(C4),
-        sum_merge.astype(F32),
-    )
+    gw_merge, gw_qkv, gw_out, gg_attn, gg_merge = widen(sum_merge, sum_qo, sum_gain)
+    return merged, grad_tokens, gg_attn.reshape(C), gw_qkv, gw_out, gg_merge.reshape(C4), gw_merge
 
 
 def solution(mesh):

time: 151 us -> 131 us (0.87)
  other arithmetic: 9.12 us -> 0 us
  Pallas kernels: 132 us -> 123 us
  local copies, waits for them, and re-layouts: 8.67 us -> 6.72 us
    pallas_call x1, Pallas kernels: 132 us -> 118 us  [step_kernel(): pl.pallas_call(step_body, in_specs=[hbm, vmem, vmem, hbm, hbm, hbm, hbm,...]
    convert_element_type x3 -> x0, other arithmetic: 7.54 us -> none  [the longest x1 4.44 us: on_device(): sum_merge.astype(F32)]
    pallas_call x0 -> x1, Pallas kernels: none -> 5.01 us  [widen(): pl.pallas_call(widen_body, grid=(4,), in_specs=[pl.BlockSpec((C, C2), lam...]
    slice x4 -> x0, local copies, waits for them, and re-layouts: 4.71 us -> none  [the longest x1 1.51 us: on_device(): sum_qo[C * (g // 3):C * (g // 3 + 1), 128 * (1 + g % 3):128 * (2 + g % 3)]]
    unnamed x10 -> x12, local copies, waits for them, and re-layouts: 3.55 us -> 6.72 us
where the time goes in v4:
time: 131 us; the launch traced here: 130 us
  Pallas kernels  123 us (94%)
  local copies, waits for them, and re-layouts  6.72 us (5%)
    pallas_call x1, Pallas kernels, step_kernel(): pl.pallas_call(step_body, in_specs=[hbm, vmem, vmem, hbm, hbm, hbm, hbm,...  118 us
    unnamed x12, local copies, waits for them, and re-layouts  6.72 us
    pallas_call x1, Pallas kernels, widen(): pl.pallas_call(widen_body, grid=(4,), in_specs=[pl.BlockSpec((C, C2), lam...  5.01 us

profile of v4, /device:TPU:1, one launch (start us, length us, event | category | flops | bytes accessed | tf_op | source)
XLA Modules:
  0.0 130.2 jit_solution(17288289913988443887)
XLA Ops:
  0.6 117.8 %step.1 = (bf16[12,24,1024]{2,1,0:T(8,128)(2,1)}, f32[24,48,512]{2,1,0:T(8,128)}, bf16[2048,1024]{1,0:T(8,128)(2,1)}, bf16[2048,512]{1,0:T(8,128)(2,1)}, f32[8,512]{1,0:T(8,128)}) custom-call(bf16[24,48,512]{2,1,0:T(8,128)(2,1)} %tok_hbm.1, s32[1,192]{1,0:T(1,128)} %bitcast.7, f32[1,512]{1,0:T(1,128)} %bitcast.6, bf16[512,1536]{1,0:T(8,128)(2,1)} %wq_hbm.1, ...), custom_call_target="tpu_custom_call" | custom-call | tf_op jit(solution)/shard_map/step/pallas_call | solution.py:636
  118.5 0.0 copy-start
  118.5 2.2 %copy-done = bf16[2048,1024]{1,0:T(8,128)(2,1)S(1)} copy-done((bf16[2048,1024]{1,0:T(8,128)(2,1)S(1)}, bf16[2048,1024]{1,0:T(8,128)(2,1)}, u32[]{:S(2)}) %copy-start) | copy-done | bytes 4194328
  120.7 0.0 copy-start.1
  120.7 1.6 %copy-done.1 = bf16[2048,512]{1,0:T(8,128)(2,1)S(1)} copy-done((bf16[2048,512]{1,0:T(8,128)(2,1)S(1)}, bf16[2048,512]{1,0:T(8,128)(2,1)}, u32[]{:S(2)}) %copy-start.1) | copy-done | bytes 2097176
  122.3 0.0 copy-start.2
  122.3 0.7 copy-done.2
  123.0 0.0 copy-start.4
  123.0 0.0 copy-start.3
  123.0 5.0 %widen.1 = (f32[2048,1024]{1,0:T(8,128)}, f32[512,1536]{1,0:T(8,128)}, f32[512,512]{1,0:T(8,128)}, f32[1,512]{1,0:T(1,128)}, f32[1,2048]{1,0:T(1,128)}) custom-call(bf16[2048,1024]{1,0:T(8,128)(2,1)S(1)} %copy-done, bf16[2048,512]{1,0:T(8,128)(2,1)S(1)} %copy-done.1, f32[8,512]{1,0:T(8,128)S(1)} %copy-done.2), custom_call_target="tpu_custom_call" | custom-call | tf_op jit(solution)/shard_map/widen/pallas_call | solution.py:712
  128.0 0.0 copy-done.4
  128.0 0.8 copy.17
  128.8 0.0 copy-done.3
  128.8 1.4 %copy.18 = f32[24,48,512]{2,1,0:T(8,128)} copy(f32[24,48,512]{2,1,0:T(8,128)S(1)} %copy-done.3) | data formatting | bytes 4718592
Async XLA Ops:
  118.5 2.2 %copy-start = (bf16[2048,1024]{1,0:T(8,128)(2,1)S(1)}, bf16[2048,1024]{1,0:T(8,128)(2,1)}, u32[]{:S(2)}) copy-start(bf16[2048,1024]{1,0:T(8,128)(2,1)} %get-tuple-element.19.m_ref) | copy-start | bytes 12582916
  120.7 1.6 %copy-start.1 = (bf16[2048,512]{1,0:T(8,128)(2,1)S(1)}, bf16[2048,512]{1,0:T(8,128)(2,1)}, u32[]{:S(2)}) copy-start(bf16[2048,512]{1,0:T(8,128)(2,1)} %get-tuple-element.20.q_ref) | copy-start | bytes 6291460
  122.3 0.7 copy-start.2
  123.0 5.0 %copy-start.4 = (bf16[12,24,1024]{2,1,0:T(8,128)(2,1)S(1)}, bf16[12,24,1024]{2,1,0:T(8,128)(2,1)}, u32[]{:S(2)}) copy-start(bf16[12,24,1024]{2,1,0:T(8,128)(2,1)} %get-tuple-element.34) | copy-start | bytes 1769476
  123.0 5.8 %copy-start.3 = (f32[24,48,512]{2,1,0:T(8,128)S(1)}, f32[24,48,512]{2,1,0:T(8,128)}, u32[]{:S(2)}) copy-start(f32[24,48,512]{2,1,0:T(8,128)} %get-tuple-element.35) | copy-start | bytes 7077892

commit v5 on v4

--- a/solution.py
+++ b/solution.py
@@ -303,8 +303,9 @@
 
 
 def step_body(tok_hbm, band_ref, ga_ref, wq_hbm, wo_hbm, gm_hbm, wm_hbm, gmg_ref,
-              merged_ref, gtok_ref, outm_ref, outq_ref, outs_ref,
-              text, hw, pk, wq, wo, gmb, wm, qkv, prob, nrm, qf, s2, fr, attx, he, bw,
+              merged_out, gtok_out, outm_out, outq_out, outs_ref,
+              merged_ref, gtok_ref, outm_ref, outq_ref,
+              text, hw, pk, wq, wo, gmb, wm, qkv, prob, qst, nrm, qf, s2, fr, attx, he, bw,
               s1, xh, rs, mi, gi, gwm, qo, gmix, gext, gw, pkg, dq, dall, bn2, bw2, hs2, he2,
               small, slots, ggm, gga, bias, lsem, hsend, hrecv, send, recv, ssend, srecv, *sums):
     loads = [
@@ -352,16 +353,21 @@
         def window(v, carry):
             masks = head_masks(0.125)
             n = NW * w + v
+            scores = []
             for p in range(PAIRS):
-                lanes = slice(128 * p, 128 * (p + 1))
-                qs = stacked(qf[v, :, lanes].astype(BF).astype(F32), masks)
-                k = qkv[n, :, C + 128 * p : C + 128 * (p + 1)]
-                val = qkv[n, :, 2 * C + 128 * p : 2 * C + 128 * (p + 1)]
-                s = dot(k, qs, 1, 1) + mask
+                qs = stacked(qf[v, :, 128 * p : 128 * (p + 1)].astype(BF).astype(F32), masks)
+                qst[n, p] = qs
+                scores.append(dot(qkv[n, :, C + 128 * p : C + 128 * (p + 1)], qs, 1, 1))
+            probs = []
+            for p in range(PAIRS):
+                s = scores[p] + mask
                 e = jnp.exp(s - jnp.max(s, axis=0, keepdims=True))
                 pr = (e * (1.0 / jnp.sum(e, axis=0, keepdims=True))).astype(BF)
                 prob[n, p] = pr
-                s2[v, :, lanes] = merged_heads(dot(pr, val, 0, 0))
+                probs.append(pr)
+            for p in range(PAIRS):
+                val = qkv[n, :, 2 * C + 128 * p : 2 * C + 128 * (p + 1)]
+                s2[v, :, 128 * p : 128 * (p + 1)] = merged_heads(dot(probs[p], val, 0, 0))
             return carry
 
         lax.fori_loop(0, NW, window, 0)
@@ -434,13 +440,12 @@
         return carry
 
 
-    def wide_tile(n, carry):
+    def weight_tile(n, carry):
         cols = pl.ds(pl.multiple_of(n * 256, 256), 256)
         gwm[cols, :] = dot(mi[:, cols], gm, 0, 0).astype(BF)
-        gi[:, cols] = dot(gm, wm[cols, :], 1, 1).astype(BF)
-        return carry
-
-    lax.fori_loop(0, C4 // 256, wide_tile, 0)
+        return carry
+
+    lax.fori_loop(0, C4 // 256, weight_tile, 0)
 
     def summed(src, out, turn, n):
         order = AXES[turn:] + AXES[:turn]
@@ -462,6 +467,13 @@
             part.step(n)
 
     advance(wide, 0)
+
+    def cotangent_tile(n, carry):
+        cols = pl.ds(pl.multiple_of(n * 256, 256), 256)
+        gi[:, cols] = dot(gm, wm[cols, :], 1, 1).astype(BF)
+        return carry
+
+    lax.fori_loop(0, C4 // 256, cotangent_tile, 0)
     ggm[...] = jnp.zeros_like(ggm)
 
     def merge_backward(c, carry):
@@ -518,22 +530,24 @@
 
         def window(v, carry):
             masks = head_masks(1.0)
-            scaled = head_masks(0.125)
             n = NW * w + v
+            cots, dps = [], []
             for p in range(PAIRS):
-                lanes = slice(128 * p, 128 * (p + 1))
-                qs = stacked(qkv[n, :, lanes].astype(F32), scaled)
+                gs = stacked(s2[v, :, 128 * p : 128 * (p + 1)], masks)
+                cots.append(gs)
+                dps.append(dot(qkv[n, :, 2 * C + 128 * p : 2 * C + 128 * (p + 1)], gs, 1, 1))
+            for p in range(PAIRS):
+                dq[v, :, 2 * C + 128 * p : 2 * C + 128 * (p + 1)] = dot(prob[n, p], cots[p], 1, 0)
+            dss = []
+            for p in range(PAIRS):
+                pf = prob[n, p].astype(F32)
+                delta = jnp.sum(pf * dps[p], axis=0, keepdims=True)
+                dss.append((pf * (dps[p] - delta)).astype(BF))
+            for p in range(PAIRS):
+                dq[v, :, C + 128 * p : C + 128 * (p + 1)] = dot(dss[p], qst[n, p], 1, 0)
+            for p in range(PAIRS):
                 k = qkv[n, :, C + 128 * p : C + 128 * (p + 1)]
-                val = qkv[n, :, 2 * C + 128 * p : 2 * C + 128 * (p + 1)]
-                gs = stacked(s2[v, :, lanes], masks)
-                pr = prob[n, p]
-                pf = pr.astype(F32)
-                dp = dot(val, gs, 1, 1)
-                delta = jnp.sum(pf * dp, axis=0, keepdims=True)
-                ds = (pf * (dp - delta)).astype(BF)
-                dq[v, :, lanes] = merged_heads(dot(ds, k, 0, 0)) * 0.125
-                dq[v, :, C + 128 * p : C + 128 * (p + 1)] = dot(ds, qs, 1, 0)
-                dq[v, :, 2 * C + 128 * p : 2 * C + 128 * (p + 1)] = dot(pr, gs, 1, 0)
+                dq[v, :, 128 * p : 128 * (p + 1)] = merged_heads(dot(dss[p], k, 0, 0)) * 0.125
             return carry
 
         lax.fori_loop(0, NW, window, 0)
@@ -592,6 +606,13 @@
     advance(late, 2)
     advance(early, 6)
     lax.fori_loop(0, C2 // 256, merged_tile, 0)
+    stores = [
+        pltpu.make_async_copy(src, dst, lsem.at[5 + n])
+        for n, (src, dst) in enumerate(
+            [(merged_ref, merged_out), (gtok_ref, gtok_out), (outm_ref, outm_out), (outq_ref, outq_out)]
+        )
+    ]
+    stores[0].start()
     small[0] = jnp.zeros_like(small[0])
     small[0, 0:1, :] = gga[...]
     for n in range(4):
@@ -609,6 +630,7 @@
     for r in range(ROWS):
         edge = pair_half(he2, (r + 3) // 2, (r + 3) % 2) + gmix[r, 32:48, :].astype(F32)[8:16]
         gtok_ref[r, 40:48, :] = jnp.where(lower, gtok_ref[r, 40:48, :], edge)
+    stores[1].start()
     gains.end(1)
     gains.begin(2)
     advance(late, 5)
@@ -618,12 +640,16 @@
     advance(late, 6)
     gains.end(3)
     outs_ref[...] = small[4]
+    advance(early, 8)
+    stores[2].start()
     advance(late, 7)
-    advance(early, 8)
     advance(late, 8)
+    stores[3].start()
     gains.finish()
     for halo in halos:
         halo.left()
+    for store in stores:
+        store.wait()
 
 
 def step_kernel(tokens, band, gain_a, w_qkv, w_out, grad_merged, w_merge, gain_m):
@@ -636,7 +662,7 @@
     return pl.pallas_call(
         step_body,
         in_specs=[hbm, vmem, vmem, hbm, hbm, hbm, hbm, vmem],
-        out_specs=[vmem] * 5,
+        out_specs=[hbm] * 4 + [vmem],
         out_shape=[
             jax.ShapeDtypeStruct((ROWS // 2, COLS // 2, C2), BF),
             jax.ShapeDtypeStruct((ROWS, COLS, C), F32),
@@ -645,6 +671,10 @@
             jax.ShapeDtypeStruct((8, C), F32),
         ],
         scratch_shapes=[
+            pltpu.VMEM((ROWS // 2, COLS // 2, C2), BF),
+            pltpu.VMEM((ROWS, COLS, C), F32),
+            pltpu.VMEM((C4, C2), BF),
+            pltpu.VMEM((TALL, C), BF),
             pltpu.VMEM((27, COLS, C), BF),
             pltpu.VMEM((14, 16, C), BF),
             pltpu.VMEM((12, 16, C), BF),
@@ -654,6 +684,7 @@
             pltpu.VMEM((C4, C2), BF),
             pltpu.VMEM((WROWS * NW, WIN, 3 * C), BF),
             pltpu.VMEM((WROWS * NW, PAIRS, WIN, 2 * WIN), BF),
+            pltpu.VMEM((WROWS * NW, PAIRS, 2 * WIN, 128), BF),
             pltpu.VMEM((ROWS * COLS, C), BF),
             pltpu.VMEM((NW, WIN, C), F32),
             pltpu.VMEM((NW, WIN, C), F32),
@@ -683,7 +714,7 @@
             pltpu.VMEM((1, C4), F32),
             pltpu.VMEM((1, C), F32),
             pltpu.VMEM((WROWS, WIN, 2 * WIN), F32),
-            pltpu.SemaphoreType.DMA((5,)),
+            pltpu.SemaphoreType.DMA((9,)),
             pltpu.SemaphoreType.DMA((4, 6)),
             pltpu.SemaphoreType.DMA((4, 6)),
             pltpu.SemaphoreType.DMA((7, SUM_COPIES)),
@@ -731,7 +762,7 @@
             jax.ShapeDtypeStruct((1, C), F32),
             jax.ShapeDtypeStruct((1, C4), F32),
         ],
-        compiler_params=pltpu.CompilerParams(vmem_limit_bytes=32 * MIB),
+        compiler_params=pltpu.CompilerParams(vmem_limit_bytes=60 * MIB),
         name="widen",
     )(sum_merge, sum_qo, sum_gain)
 

time: 131 us -> 117 us (0.89)
  Pallas kernels: 123 us -> 114 us
  local copies, waits for them, and re-layouts: 6.72 us -> 2.23 us
    pallas_call x1, Pallas kernels: 118 us -> 106 us  [step_kernel(): pl.pallas_call(step_body, in_specs=[hbm, vmem, vmem, hbm, hbm, hbm, hbm,...]
    unnamed x12 -> x6, local copies, waits for them, and re-layouts: 6.72 us -> 2.23 us
    pallas_call x1, Pallas kernels: 5.01 us -> 8 us  [widen(): pl.pallas_call(widen_body, grid=(4,), in_specs=[pl.BlockSpec((C, C2), lam...]
where the time goes in v5:
time: 117 us
  Pallas kernels  114 us (97%)
  local copies, waits for them, and re-layouts  2.23 us (2%)
    pallas_call x1, Pallas kernels, step_kernel(): pl.pallas_call(step_body, in_specs=[hbm, vmem, vmem, hbm, hbm, hbm, hbm,...  106 us
    pallas_call x1, Pallas kernels, widen(): pl.pallas_call(widen_body, grid=(4,), in_specs=[pl.BlockSpec((C, C2), lam...  8 us

profile of v5, /device:TPU:1, one launch (start us, length us, event | category | flops | bytes accessed | tf_op | source)
XLA Modules:
  0.0 117.1 jit_solution(6902524577013003260)
XLA Ops:
  0.6 106.2 %step.1 = (bf16[12,24,1024]{2,1,0:T(8,128)(2,1)}, f32[24,48,512]{2,1,0:T(8,128)}, bf16[2048,1024]{1,0:T(8,128)(2,1)}, bf16[2048,512]{1,0:T(8,128)(2,1)}, f32[8,512]{1,0:T(8,128)}) custom-call(bf16[24,48,512]{2,1,0:T(8,128)(2,1)} %tok_hbm.1, s32[1,192]{1,0:T(1,128)} %bitcast.7, f32[1,512]{1,0:T(1,128)} %bitcast.6, bf16[512,1536]{1,0:T(8,128)(2,1)} %wq_hbm.1, ...), custom_call_target="tpu_custom_call" | custom-call | tf_op jit(solution)/shard_map/step/pallas_call | solution.py:662
  106.9 0.0 copy-start.1
  106.9 0.0 copy-start
  106.9 8.0 %widen.1 = (f32[2048,1024]{1,0:T(8,128)}, f32[512,1536]{1,0:T(8,128)}, f32[512,512]{1,0:T(8,128)}, f32[1,512]{1,0:T(1,128)}, f32[1,2048]{1,0:T(1,128)}) custom-call(bf16[2048,1024]{1,0:T(8,128)(2,1)} %get-tuple-element.19.m_ref, bf16[2048,512]{1,0:T(8,128)(2,1)} %get-tuple-element.20.q_ref, f32[8,512]{1,0:T(8,128)} %get-tuple-element.21.s_ref), custom_call_target="tpu_custom_call" | custom-call | tf_op jit(solution)/shard_map/widen/pallas_call | solution.py:743
  114.9 0.0 copy-done.1
  114.9 0.8 copy.17
  115.7 0.0 copy-done
  115.7 1.4 %copy.18 = f32[24,48,512]{2,1,0:T(8,128)} copy(f32[24,48,512]{2,1,0:T(8,128)S(1)} %copy-done) | data formatting | bytes 4718592
Async XLA Ops:
  106.9 8.0 %copy-start.1 = (bf16[12,24,1024]{2,1,0:T(8,128)(2,1)S(1)}, bf16[12,24,1024]{2,1,0:T(8,128)(2,1)}, u32[]{:S(2)}) copy-start(bf16[12,24,1024]{2,1,0:T(8,128)(2,1)} %get-tuple-element.34) | copy-start | bytes 1769476
  106.9 8.8 %copy-start = (f32[24,48,512]{2,1,0:T(8,128)S(1)}, f32[24,48,512]{2,1,0:T(8,128)}, u32[]{:S(2)}) copy-start(f32[24,48,512]{2,1,0:T(8,128)} %get-tuple-element.35) | copy-start | bytes 7077892

commit v6 on v5

--- a/solution.py
+++ b/solution.py
@@ -111,10 +111,10 @@
 
 
 class Sum:
-    def __init__(self, at, src, out, order, recvs, send, recv):
+    def __init__(self, at, src, out, order, recvs, send, recv, ring):
         self.at, self.src, self.out, self.order = at, src, out, order
         self.recvs, self.send, self.recv = recvs, send, recv
-        self.rows = src.shape[0]
+        self.rows, self.ring = src.shape[0], ring
         self.sent = []
 
     def start(self, src, dst, index, target):
@@ -147,7 +147,12 @@
             add_rows(self.out, first, terms, count)
             self.gather(3)
             return
+        if level == 1 and self.ring:
+            terms = [(self.src, first), (self.recvs[1].at[1], 0), (self.recvs[1].at[2], 0)]
         add_rows(self.src, first, terms, count)
+        if level == 0 and self.ring:
+            self.ring_start()
+            return
         axis = self.order[level]
         block = self.block(level + 1)
         self.last = []
@@ -160,12 +165,49 @@
                 )
             )
 
+    def part(self, step, half):
+        block = self.block(1)
+        return pl.multiple_of(self.first(0) + (self.at[self.order[0]] + step) % 4 * block + half * (block // 2), 16)
+
+    def ring_send(self, step, half, slot, index, towards):
+        size = self.block(1) // 2
+        return self.start(
+            self.src.at[pl.ds(self.part(step, half), size), :],
+            self.recvs[1].at[slot, pl.ds(half * size, size), :],
+            index, peer(self.at, self.order[0], towards),
+        )
+
+    def ring_start(self):
+        self.relayed = [self.ring_send(2, 0, 0, 20, 1), self.ring_send(2, 1, 0, 21, 3)]
+        self.last = [self.ring_send(1, 1, 1, 22, 1), self.ring_send(3, 0, 1, 23, 3)]
+
+    def ring_relay(self):
+        for copy in self.relayed:
+            copy.wait_recv()
+        size = self.block(1) // 2
+        for step, half, index in ((1, 0, 24), (3, 1, 25)):
+            first = self.part(step, half)
+            add_rows(self.src, first, [(self.src, first), (self.recvs[1].at[0], half * size)], size)
+            self.last.append(self.ring_send(step, half, 2, index, step))
+
+    def ring_forward(self):
+        for copy in self.last:
+            copy.wait_recv()
+        size = self.block(1) // 2
+        self.last = []
+        for step, half, index in ((3, 0, 28), (1, 1, 29)):
+            rows = self.out.at[pl.ds(self.part(step, half), size), :]
+            self.last.append(self.start(rows, rows, index, peer(self.at, self.order[0], 4 - step)))
+
     def gather(self, level):
         mine = self.out.at[pl.ds(self.first(level), self.block(level)), :]
         if level == 0:
             self.last = [self.start(mine, mine, 19, peer(self.at, "core", 1))]
             return
         axis = self.order[level - 1]
+        if level == 1 and self.ring:
+            self.last = [self.start(mine, mine, 26 + n, peer(self.at, axis, step)) for n, step in enumerate((1, 3))]
+            return
         self.last = [
             self.start(mine, mine, 10 + 3 * (level - 1) + step - 1, peer(self.at, axis, step)) for step in range(1, 4)
         ]
@@ -181,6 +223,14 @@
             copy.wait_send()
 
     def step(self, n):
+        if self.ring:
+            if n == 2:
+                self.ring_relay()
+                return
+            if n == 8:
+                self.ring_forward()
+                return
+            n = n - (n > 2) - (n > 8)
         if n == 0:
             self.begin()
         elif n < 5:
@@ -191,7 +241,7 @@
             self.finish()
 
 
-SUM_COPIES = 20
+SUM_COPIES = 30
 
 
 def sum_scratch(rows, lanes):
@@ -447,18 +497,18 @@
 
     lax.fori_loop(0, C4 // 256, weight_tile, 0)
 
-    def summed(src, out, turn, n):
+    def summed(src, out, turn, n, ring):
         order = AXES[turn:] + AXES[:turn]
-        return Sum(at, src, out, order, sums[4 * n : 4 * n + 4], send.at[n], recv.at[n])
+        return Sum(at, src, out, order, sums[4 * n : 4 * n + 4], send.at[n], recv.at[n], ring)
 
     wide = [
-        summed(gwm.at[:, 0:384], outm_ref.at[:, 0:384], 0, 0),
-        summed(gwm.at[:, 384:768], outm_ref.at[:, 384:768], 1, 1),
-        summed(gwm.at[:, 768:1024], outm_ref.at[:, 768:1024], 2, 2),
+        summed(gwm.at[:, 0:384], outm_ref.at[:, 0:384], 0, 0, True),
+        summed(gwm.at[:, 384:768], outm_ref.at[:, 384:768], 1, 1, True),
+        summed(gwm.at[:, 768:1024], outm_ref.at[:, 768:1024], 2, 2, True),
     ]
-    early = wide + [summed(qo.at[:, 0:128], outq_ref.at[:, 0:128], 2, 3)]
+    early = wide + [summed(qo.at[:, 0:128], outq_ref.at[:, 0:128], 2, 3, True)]
     late = [
-        summed(qo.at[:, 128 * (t + 1) : 128 * (t + 2)], outq_ref.at[:, 128 * (t + 1) : 128 * (t + 2)], t, 4 + t)
+        summed(qo.at[:, 128 * (t + 1) : 128 * (t + 2)], outq_ref.at[:, 128 * (t + 1) : 128 * (t + 2)], t, 4 + t, False)
         for t in range(3)
     ]
 
@@ -554,9 +604,9 @@
         dall[pl.ds(pl.multiple_of(w * NWT, NWT), NWT), :] = dq[...].reshape(NWT, 3 * C).astype(BF)
         return carry
 
-    lax.fori_loop(0, 3, backward_row, 0)
+    lax.fori_loop(0, 2, backward_row, 0)
     advance(early, 2)
-    lax.fori_loop(3, 4, backward_row, 0)
+    lax.fori_loop(2, 4, backward_row, 0)
     advance(early, 3)
     for n in range(6):
         tile = dot(nrm[...], dall[:, 256 * n : 256 * (n + 1)], 0, 0).astype(BF)
@@ -564,7 +614,6 @@
             g = 2 * n + k
             qo[C * (g // 3) : C * (g // 3 + 1), 128 * (1 + g % 3) : 128 * (2 + g % 3)] = tile[:, 128 * k : 128 * (k + 1)]
     advance(late, 0)
-    advance(early, 4)
     gga[...] = jnp.zeros_like(gga)
 
     def dgrad_row(w, carry):
@@ -598,13 +647,12 @@
     halos[3].start(bn2.at[pl.ds(0, 3)], hs2, -1, 0)
     halos[3].start(bw2.at[pl.ds(0, 2)], he2.at[pl.ds(12, 2)], -1, -1)
     advance(late, 1)
+    advance(early, 4)
     lax.fori_loop(1, 2, dgrad_row, 0)
     halos[3].start(bw2.at[pl.ds(0, 6)], he2.at[pl.ds(0, 6)], 0, -1)
-    advance(early, 5)
     lax.fori_loop(2, 4, dgrad_row, 0)
     halos[3].start(bw2.at[pl.ds(6, 6)], he2.at[pl.ds(6, 6)], 0, -1)
-    advance(late, 2)
-    advance(early, 6)
+    advance(early, 5)
     lax.fori_loop(0, C2 // 256, merged_tile, 0)
     stores = [
         pltpu.make_async_copy(src, dst, lsem.at[5 + n])
@@ -619,10 +667,7 @@
         small[0, 1 + n : 2 + n, :] = ggm[:, C * n : C * (n + 1)]
     gains = SmallSum(at, small, slots, ssend, srecv)
     gains.begin(0)
-    advance(late, 3)
-    gains.end(0)
-    gains.begin(1)
-    advance(late, 4)
+    advance(early, 6)
     for copy in halos[3].copies:
         copy.wait_recv()
     for r in range(3):
@@ -631,18 +676,25 @@
         edge = pair_half(he2, (r + 3) // 2, (r + 3) % 2) + gmix[r, 32:48, :].astype(F32)[8:16]
         gtok_ref[r, 40:48, :] = jnp.where(lower, gtok_ref[r, 40:48, :], edge)
     stores[1].start()
+    gains.end(0)
+    gains.begin(1)
+    advance(late, 2)
     gains.end(1)
     gains.begin(2)
-    advance(late, 5)
+    advance(early, 7)
+    advance(late, 3)
     gains.end(2)
     gains.begin(3)
-    advance(early, 7)
-    advance(late, 6)
+    advance(late, 4)
     gains.end(3)
     outs_ref[...] = small[4]
+    advance(late, 5)
     advance(early, 8)
+    advance(late, 6)
+    advance(early, 9)
+    advance(late, 7)
+    advance(early, 10)
     stores[2].start()
-    advance(late, 7)
     advance(late, 8)
     stores[3].start()
     gains.finish()
@@ -742,18 +794,18 @@
 def widen(sum_merge, sum_qo, sum_gain):
     return pl.pallas_call(
         widen_body,
-        grid=(4,),
+        grid=(4, 2),
         in_specs=[
-            pl.BlockSpec((C, C2), lambda i: (i, 0)),
-            pl.BlockSpec((C, C), lambda i: (i, 0)),
-            pl.BlockSpec((8, C), lambda i: (0, 0)),
+            pl.BlockSpec((C // 2, C2), lambda i, j: (2 * i + j, 0)),
+            pl.BlockSpec((C // 2, C), lambda i, j: (2 * i + j, 0)),
+            pl.BlockSpec((8, C), lambda i, j: (0, 0)),
         ],
         out_specs=[
-            pl.BlockSpec((C, C2), lambda i: (i, 0)),
-            pl.BlockSpec((C, 384), lambda i: (0, i)),
-            pl.BlockSpec((C, 128), lambda i: (0, i)),
-            pl.BlockSpec((1, C), lambda i: (0, 0)),
-            pl.BlockSpec((1, C4), lambda i: (0, 0)),
+            pl.BlockSpec((C // 2, C2), lambda i, j: (2 * i + j, 0)),
+            pl.BlockSpec((C // 2, 384), lambda i, j: (j, i)),
+            pl.BlockSpec((C // 2, 128), lambda i, j: (j, i)),
+            pl.BlockSpec((1, C), lambda i, j: (0, 0)),
+            pl.BlockSpec((1, C4), lambda i, j: (0, 0)),
         ],
         out_shape=[
             jax.ShapeDtypeStruct((C4, C2), F32),

time: 117 us -> 118 us (level)
  no operation moved by 1% of the time
where the time goes in v6:
time: 118 us
  Pallas kernels  115 us (97%)
  local copies, waits for them, and re-layouts  2.23 us (2%)
    pallas_call x1, Pallas kernels, step_kernel(): pl.pallas_call(step_body, in_specs=[hbm, vmem, vmem, hbm, hbm, hbm, hbm,...  106 us
    pallas_call x1, Pallas kernels, widen(): pl.pallas_call(widen_body, grid=(4, 2), in_specs=[pl.BlockSpec((C // 2, C...  8.85 us

profile of v6, /device:TPU:1, one launch (start us, length us, event | category | flops | bytes accessed | tf_op | source)
XLA Modules:
  0.0 117.6 jit_solution(11133356063750100570)
XLA Ops:
  0.6 105.9 %step.1 = (bf16[12,24,1024]{2,1,0:T(8,128)(2,1)}, f32[24,48,512]{2,1,0:T(8,128)}, bf16[2048,1024]{1,0:T(8,128)(2,1)}, bf16[2048,512]{1,0:T(8,128)(2,1)}, f32[8,512]{1,0:T(8,128)}) custom-call(bf16[24,48,512]{2,1,0:T(8,128)(2,1)} %tok_hbm.1, s32[1,192]{1,0:T(1,128)} %bitcast.7, f32[1,512]{1,0:T(1,128)} %bitcast.6, bf16[512,1536]{1,0:T(8,128)(2,1)} %wq_hbm.1, ...), custom_call_target="tpu_custom_call" | custom-call | tf_op jit(solution)/shard_map/step/pallas_call | solution.py:714
  106.6 0.0 copy-start.1
  106.6 0.0 copy-start
  106.6 8.8 %widen.1 = (f32[2048,1024]{1,0:T(8,128)}, f32[512,1536]{1,0:T(8,128)}, f32[512,512]{1,0:T(8,128)}, f32[1,512]{1,0:T(1,128)}, f32[1,2048]{1,0:T(1,128)}) custom-call(bf16[2048,1024]{1,0:T(8,128)(2,1)} %get-tuple-element.19.m_ref, bf16[2048,512]{1,0:T(8,128)(2,1)} %get-tuple-element.20.q_ref, f32[8,512]{1,0:T(8,128)} %get-tuple-element.21.s_ref), custom_call_target="tpu_custom_call" | custom-call | tf_op jit(solution)/shard_map/widen/pallas_call | solution.py:795
  115.4 0.0 copy-done.1
  115.4 0.8 copy.17
  116.2 0.0 copy-done
  116.2 1.4 %copy.18 = f32[24,48,512]{2,1,0:T(8,128)} copy(f32[24,48,512]{2,1,0:T(8,128)S(1)} %copy-done) | data formatting | bytes 4718592
Async XLA Ops:
  106.6 8.9 %copy-start.1 = (bf16[12,24,1024]{2,1,0:T(8,128)(2,1)S(1)}, bf16[12,24,1024]{2,1,0:T(8,128)(2,1)}, u32[]{:S(2)}) copy-start(bf16[12,24,1024]{2,1,0:T(8,128)(2,1)} %get-tuple-element.34) | copy-start | bytes 1769476
  106.6 9.7 %copy-start = (f32[24,48,512]{2,1,0:T(8,128)S(1)}, f32[24,48,512]{2,1,0:T(8,128)}, u32[]{:S(2)}) copy-start(f32[24,48,512]{2,1,0:T(8,128)} %get-tuple-element.35) | copy-start | bytes 7077892

commit v7 on v6

--- a/solution.py
+++ b/solution.py
@@ -354,9 +354,9 @@
 
 def step_body(tok_hbm, band_ref, ga_ref, wq_hbm, wo_hbm, gm_hbm, wm_hbm, gmg_ref,
               merged_out, gtok_out, outm_out, outq_out, outs_ref,
-              merged_ref, gtok_ref, outm_ref, outq_ref,
+              merged_ref, gtok_ref, om0, om1, om2, oq0, oq1, oq2, oq3,
               text, hw, pk, wq, wo, gmb, wm, qkv, prob, qst, nrm, qf, s2, fr, attx, he, bw,
-              s1, xh, rs, mi, gi, gwm, qo, gmix, gext, gw, pkg, dq, dall, bn2, bw2, hs2, he2,
+              s1, xh, rs, mi, gi, gw0, gw1, gw2, qo0, qo1, qo2, qo3, gmix, gext, gw, pkg, dq, dall, bn2, bw2, hs2, he2,
               small, slots, ggm, gga, bias, lsem, hsend, hrecv, send, recv, ssend, srecv, *sums):
     loads = [
         pltpu.make_async_copy(src, dst, lsem.at[n])
@@ -492,7 +492,10 @@
 
     def weight_tile(n, carry):
         cols = pl.ds(pl.multiple_of(n * 256, 256), 256)
-        gwm[cols, :] = dot(mi[:, cols], gm, 0, 0).astype(BF)
+        tile = dot(mi[:, cols], gm, 0, 0).astype(BF)
+        gw0[cols, :] = tile[:, 0:384]
+        gw1[cols, :] = tile[:, 384:768]
+        gw2[cols, :] = tile[:, 768:1024]
         return carry
 
     lax.fori_loop(0, C4 // 256, weight_tile, 0)
@@ -502,13 +505,13 @@
         return Sum(at, src, out, order, sums[4 * n : 4 * n + 4], send.at[n], recv.at[n], ring)
 
     wide = [
-        summed(gwm.at[:, 0:384], outm_ref.at[:, 0:384], 0, 0, True),
-        summed(gwm.at[:, 384:768], outm_ref.at[:, 384:768], 1, 1, True),
-        summed(gwm.at[:, 768:1024], outm_ref.at[:, 768:1024], 2, 2, True),
+        summed(gw0, om0, 0, 0, True),
+        summed(gw1, om1, 1, 1, True),
+        summed(gw2, om2, 2, 2, True),
     ]
-    early = wide + [summed(qo.at[:, 0:128], outq_ref.at[:, 0:128], 2, 3, True)]
+    early = wide + [summed(qo0, oq0, 2, 3, True)]
     late = [
-        summed(qo.at[:, 128 * (t + 1) : 128 * (t + 2)], outq_ref.at[:, 128 * (t + 1) : 128 * (t + 2)], t, 4 + t, False)
+        summed((qo1, qo2, qo3)[t], (oq1, oq2, oq3)[t], t, 4 + t, False)
         for t in range(3)
     ]
 
@@ -568,7 +571,7 @@
     att = attx[pl.ds(3, ROWS)].reshape(ROWS * COLS, C)
     gwo = dot(att, flat, 0, 0).astype(BF)
     for n in range(4):
-        qo[C * n : C * (n + 1), 0:128] = gwo[:, 128 * n : 128 * (n + 1)]
+        qo0[C * n : C * (n + 1), :] = gwo[:, 128 * n : 128 * (n + 1)]
     early[3].step(0)
     advance(early, 1)
     for copy in halos[2].copies:
@@ -612,7 +615,7 @@
         tile = dot(nrm[...], dall[:, 256 * n : 256 * (n + 1)], 0, 0).astype(BF)
         for k in range(2):
             g = 2 * n + k
-            qo[C * (g // 3) : C * (g // 3 + 1), 128 * (1 + g % 3) : 128 * (2 + g % 3)] = tile[:, 128 * k : 128 * (k + 1)]
+            (qo1, qo2, qo3)[g % 3][C * (g // 3) : C * (g // 3 + 1), :] = tile[:, 128 * k : 128 * (k + 1)]
     advance(late, 0)
     gga[...] = jnp.zeros_like(gga)
 
@@ -657,7 +660,9 @@
     stores = [
         pltpu.make_async_copy(src, dst, lsem.at[5 + n])
         for n, (src, dst) in enumerate(
-            [(merged_ref, merged_out), (gtok_ref, gtok_out), (outm_ref, outm_out), (outq_ref, outq_out)]
+            [(merged_ref, merged_out), (gtok_ref, gtok_out)]
+            + [(om, outm_out.at[:, 384 * k : 384 * k + om.shape[1]]) for k, om in enumerate((om0, om1, om2))]
+            + [(oq, outq_out.at[:, 128 * k : 128 * (k + 1)]) for k, oq in enumerate((oq0, oq1, oq2, oq3))]
         )
     ]
     stores[0].start()
@@ -694,9 +699,11 @@
     advance(early, 9)
     advance(late, 7)
     advance(early, 10)
-    stores[2].start()
+    for store in stores[2:6]:
+        store.start()
     advance(late, 8)
-    stores[3].start()
+    for store in stores[6:]:
+        store.start()
     gains.finish()
     for halo in halos:
         halo.left()
@@ -711,6 +718,7 @@
     sums = []
     for n in lanes:
         sums += sum_scratch(TALL, n)
+    wide = [pltpu.VMEM((TALL, n), BF) for n in lanes]
     return pl.pallas_call(
         step_body,
         in_specs=[hbm, vmem, vmem, hbm, hbm, hbm, hbm, vmem],
@@ -725,8 +733,7 @@
         scratch_shapes=[
             pltpu.VMEM((ROWS // 2, COLS // 2, C2), BF),
             pltpu.VMEM((ROWS, COLS, C), F32),
-            pltpu.VMEM((C4, C2), BF),
-            pltpu.VMEM((TALL, C), BF),
+            *wide,
             pltpu.VMEM((27, COLS, C), BF),
             pltpu.VMEM((14, 16, C), BF),
             pltpu.VMEM((12, 16, C), BF),
@@ -749,8 +756,7 @@
             pltpu.VMEM((MALL, 1), F32),
             pltpu.VMEM((MALL, C4), BF),
             pltpu.VMEM((MALL, C4), BF),
-            pltpu.VMEM((C4, C2), BF),
-            pltpu.VMEM((TALL, C), BF),
+            *wide,
             pltpu.VMEM((ROWS, COLS, C), BF),
             pltpu.VMEM((27, COLS, C), BF),
             pltpu.VMEM((14, 16, C), BF),
@@ -766,7 +772,7 @@
             pltpu.VMEM((1, C4), F32),
             pltpu.VMEM((1, C), F32),
             pltpu.VMEM((WROWS, WIN, 2 * WIN), F32),
-            pltpu.SemaphoreType.DMA((9,)),
+            pltpu.SemaphoreType.DMA((14,)),
             pltpu.SemaphoreType.DMA((4, 6)),
             pltpu.SemaphoreType.DMA((4, 6)),
             pltpu.SemaphoreType.DMA((7, SUM_COPIES)),
@@ -794,18 +800,18 @@
 def widen(sum_merge, sum_qo, sum_gain):
     return pl.pallas_call(
         widen_body,
-        grid=(4, 2),
+        grid=(4,),
         in_specs=[
-            pl.BlockSpec((C // 2, C2), lambda i, j: (2 * i + j, 0)),
-            pl.BlockSpec((C // 2, C), lambda i, j: (2 * i + j, 0)),
-            pl.BlockSpec((8, C), lambda i, j: (0, 0)),
+            pl.BlockSpec((C, C2), lambda i: (i, 0)),
+            pl.BlockSpec((C, C), lambda i: (i, 0)),
+            pl.BlockSpec((8, C), lambda i: (0, 0)),
         ],
         out_specs=[
-            pl.BlockSpec((C // 2, C2), lambda i, j: (2 * i + j, 0)),
-            pl.BlockSpec((C // 2, 384), lambda i, j: (j, i)),
-            pl.BlockSpec((C // 2, 128), lambda i, j: (j, i)),
-            pl.BlockSpec((1, C), lambda i, j: (0, 0)),
-            pl.BlockSpec((1, C4), lambda i, j: (0, 0)),
+            pl.BlockSpec((C, C2), lambda i: (i, 0)),
+            pl.BlockSpec((C, 384), lambda i: (0, i)),
+            pl.BlockSpec((C, 128), lambda i: (0, i)),
+            pl.BlockSpec((1, C), lambda i: (0, 0)),
+            pl.BlockSpec((1, C4), lambda i: (0, 0)),
         ],
         out_shape=[
             jax.ShapeDtypeStruct((C4, C2), F32),

time: 118 us -> 117 us (level)
  no operation moved by 1% of the time
where the time goes in v7:
time: 117 us
  Pallas kernels  114 us (97%)
  local copies, waits for them, and re-layouts  2.23 us (2%)
    pallas_call x1, Pallas kernels, step_kernel(): pl.pallas_call(step_body, in_specs=[hbm, vmem, vmem, hbm, hbm, hbm, hbm,...  106 us
    pallas_call x1, Pallas kernels, widen(): pl.pallas_call(widen_body, grid=(4,), in_specs=[pl.BlockSpec((C, C2), lam...  8 us

profile of v7, /device:TPU:1, one launch (start us, length us, event | category | flops | bytes accessed | tf_op | source)
XLA Modules:
  0.0 116.7 jit_solution(14342786799889552170)
XLA Ops:
  0.6 105.9 %step.1 = (bf16[12,24,1024]{2,1,0:T(8,128)(2,1)}, f32[24,48,512]{2,1,0:T(8,128)}, bf16[2048,1024]{1,0:T(8,128)(2,1)}, bf16[2048,512]{1,0:T(8,128)(2,1)}, f32[8,512]{1,0:T(8,128)}) custom-call(bf16[24,48,512]{2,1,0:T(8,128)(2,1)} %tok_hbm.1, s32[1,192]{1,0:T(1,128)} %bitcast.7, f32[1,512]{1,0:T(1,128)} %bitcast.6, bf16[512,1536]{1,0:T(8,128)(2,1)} %wq_hbm.1, ...), custom_call_target="tpu_custom_call" | custom-call | tf_op jit(solution)/shard_map/step/pallas_call | solution.py:722
  106.5 0.0 copy-start.1
  106.5 0.0 copy-start
  106.5 8.0 %widen.1 = (f32[2048,1024]{1,0:T(8,128)}, f32[512,1536]{1,0:T(8,128)}, f32[512,512]{1,0:T(8,128)}, f32[1,512]{1,0:T(1,128)}, f32[1,2048]{1,0:T(1,128)}) custom-call(bf16[2048,1024]{1,0:T(8,128)(2,1)} %get-tuple-element.19.m_ref, bf16[2048,512]{1,0:T(8,128)(2,1)} %get-tuple-element.20.q_ref, f32[8,512]{1,0:T(8,128)} %get-tuple-element.21.s_ref), custom_call_target="tpu_custom_call" | custom-call | tf_op jit(solution)/shard_map/widen/pallas_call | solution.py:801
  114.5 0.0 copy-done.1
  114.5 0.8 copy.17
  115.3 0.0 copy-done
  115.3 1.4 %copy.18 = f32[24,48,512]{2,1,0:T(8,128)} copy(f32[24,48,512]{2,1,0:T(8,128)S(1)} %copy-done) | data formatting | bytes 4718592
Async XLA Ops:
  106.5 8.0 %copy-start.1 = (bf16[12,24,1024]{2,1,0:T(8,128)(2,1)S(1)}, bf16[12,24,1024]{2,1,0:T(8,128)(2,1)}, u32[]{:S(2)}) copy-start(bf16[12,24,1024]{2,1,0:T(8,128)(2,1)} %get-tuple-element.34) | copy-start | bytes 1769476
  106.5 8.8 %copy-start = (f32[24,48,512]{2,1,0:T(8,128)S(1)}, f32[24,48,512]{2,1,0:T(8,128)}, u32[]{:S(2)}) copy-start(f32[24,48,512]{2,1,0:T(8,128)} %get-tuple-element.35) | copy-start | bytes 7077892

commit v8 on v5

--- a/solution.py
+++ b/solution.py
@@ -133,9 +133,45 @@
         return pl.multiple_of(first, 16)
 
     def begin(self):
-        half = self.rows // 2
-        theirs = pl.ds(pl.multiple_of((1 - self.at["core"]) * half, 16), half)
-        self.last = [self.start(self.src.at[theirs, :], self.recvs[0].at[0], 0, peer(self.at, "core", 1))]
+        block = self.block(1)
+        self.last = []
+        for n, step in enumerate((1, 2, 3, 0)):
+            place = (self.at[self.order[0]] + step) % 4 * block
+            theirs = pl.multiple_of((1 - self.at["core"]) * (self.rows // 2) + place, 16)
+            self.last.append(
+                self.start(
+                    self.src.at[pl.ds(theirs, block), :],
+                    self.recvs[0].at[0, pl.ds(pl.multiple_of(place, 16), block), :],
+                    (0, 23, 24, 25)[n], peer(self.at, "core", 1),
+                )
+            )
+
+    def pass_on(self):
+        block = self.block(1)
+        arriving, self.last = self.last, []
+        for copy, step in zip(arriving, (1, 2, 3, 0)):
+            copy.wait_recv()
+            place = (self.at[self.order[0]] + step) % 4 * block
+            first = pl.multiple_of(self.first(0) + place, 16)
+            add_rows(self.src, first, [(self.src, first), (self.recvs[0].at[0], place)], block)
+            if step:
+                self.last.append(
+                    self.start(
+                        self.src.at[pl.ds(first, block), :], self.recvs[1].at[step - 1],
+                        step, peer(self.at, self.order[0], step),
+                    )
+                )
+
+    def to_partner(self, step, index):
+        block = self.block(1)
+        place = (self.at[self.order[0]] + step) % 4 * block
+        rows = self.out.at[pl.ds(pl.multiple_of(self.first(0) + place, 16), block), :]
+        self.crossed.append(self.start(rows, rows, index, peer(self.at, "core", 1)))
+
+    def cross(self):
+        for copy, step in zip(self.last, (3, 2, 1)):
+            copy.wait_recv()
+            self.to_partner(step, 19 + step)
 
     def combine(self, level):
         for copy in self.last:
@@ -162,13 +198,13 @@
 
     def gather(self, level):
         mine = self.out.at[pl.ds(self.first(level), self.block(level)), :]
-        if level == 0:
-            self.last = [self.start(mine, mine, 19, peer(self.at, "core", 1))]
-            return
         axis = self.order[level - 1]
         self.last = [
             self.start(mine, mine, 10 + 3 * (level - 1) + step - 1, peer(self.at, axis, step)) for step in range(1, 4)
         ]
+        if level == 1:
+            self.crossed = []
+            self.to_partner(0, 19)
 
     def gathered(self, level):
         for copy in self.last:
@@ -176,22 +212,27 @@
         self.gather(level - 1)
 
     def finish(self):
-        self.last[0].wait_recv()
+        for copy in self.crossed:
+            copy.wait_recv()
         for copy in self.sent:
             copy.wait_send()
 
     def step(self, n):
         if n == 0:
             self.begin()
+        elif n == 1:
+            self.pass_on()
         elif n < 5:
             self.combine(n - 1)
-        elif n < 8:
+        elif n < 7:
             self.gathered(8 - n)
+        elif n == 7:
+            self.cross()
         else:
             self.finish()
 
 
-SUM_COPIES = 20
+SUM_COPIES = 30
 
 
 def sum_scratch(rows, lanes):
@@ -304,9 +345,9 @@
 
 def step_body(tok_hbm, band_ref, ga_ref, wq_hbm, wo_hbm, gm_hbm, wm_hbm, gmg_ref,
               merged_out, gtok_out, outm_out, outq_out, outs_ref,
-              merged_ref, gtok_ref, outm_ref, outq_ref,
+              merged_ref, gtok_ref, om0, om1, om2, oq0, oq1, oq2, oq3,
               text, hw, pk, wq, wo, gmb, wm, qkv, prob, qst, nrm, qf, s2, fr, attx, he, bw,
-              s1, xh, rs, mi, gi, gwm, qo, gmix, gext, gw, pkg, dq, dall, bn2, bw2, hs2, he2,
+              s1, xh, rs, mi, gi, gw0, gw1, gw2, qo0, qo1, qo2, qo3, gmix, gext, gw, pkg, dq, dall, bn2, bw2, hs2, he2,
               small, slots, ggm, gga, bias, lsem, hsend, hrecv, send, recv, ssend, srecv, *sums):
     loads = [
         pltpu.make_async_copy(src, dst, lsem.at[n])
@@ -442,7 +483,10 @@
 
     def weight_tile(n, carry):
         cols = pl.ds(pl.multiple_of(n * 256, 256), 256)
-        gwm[cols, :] = dot(mi[:, cols], gm, 0, 0).astype(BF)
+        tile = dot(mi[:, cols], gm, 0, 0).astype(BF)
+        gw0[cols, :] = tile[:, 0:384]
+        gw1[cols, :] = tile[:, 384:768]
+        gw2[cols, :] = tile[:, 768:1024]
         return carry
 
     lax.fori_loop(0, C4 // 256, weight_tile, 0)
@@ -452,13 +496,13 @@
         return Sum(at, src, out, order, sums[4 * n : 4 * n + 4], send.at[n], recv.at[n])
 
     wide = [
-        summed(gwm.at[:, 0:384], outm_ref.at[:, 0:384], 0, 0),
-        summed(gwm.at[:, 384:768], outm_ref.at[:, 384:768], 1, 1),
-        summed(gwm.at[:, 768:1024], outm_ref.at[:, 768:1024], 2, 2),
+        summed(gw0, om0, 0, 0),
+        summed(gw1, om1, 1, 1),
+        summed(gw2, om2, 2, 2),
     ]
-    early = wide + [summed(qo.at[:, 0:128], outq_ref.at[:, 0:128], 2, 3)]
+    early = wide + [summed(qo0, oq0, 2, 3)]
     late = [
-        summed(qo.at[:, 128 * (t + 1) : 128 * (t + 2)], outq_ref.at[:, 128 * (t + 1) : 128 * (t + 2)], t, 4 + t)
+        summed((qo1, qo2, qo3)[t], (oq1, oq2, oq3)[t], t, 4 + t)
         for t in range(3)
     ]
 
@@ -518,7 +562,7 @@
     att = attx[pl.ds(3, ROWS)].reshape(ROWS * COLS, C)
     gwo = dot(att, flat, 0, 0).astype(BF)
     for n in range(4):
-        qo[C * n : C * (n + 1), 0:128] = gwo[:, 128 * n : 128 * (n + 1)]
+        qo0[C * n : C * (n + 1), :] = gwo[:, 128 * n : 128 * (n + 1)]
     early[3].step(0)
     advance(early, 1)
     for copy in halos[2].copies:
@@ -554,15 +598,15 @@
         dall[pl.ds(pl.multiple_of(w * NWT, NWT), NWT), :] = dq[...].reshape(NWT, 3 * C).astype(BF)
         return carry
 
-    lax.fori_loop(0, 3, backward_row, 0)
+    lax.fori_loop(0, 2, backward_row, 0)
     advance(early, 2)
-    lax.fori_loop(3, 4, backward_row, 0)
+    lax.fori_loop(2, 4, backward_row, 0)
     advance(early, 3)
     for n in range(6):
         tile = dot(nrm[...], dall[:, 256 * n : 256 * (n + 1)], 0, 0).astype(BF)
         for k in range(2):
             g = 2 * n + k
-            qo[C * (g // 3) : C * (g // 3 + 1), 128 * (1 + g % 3) : 128 * (2 + g % 3)] = tile[:, 128 * k : 128 * (k + 1)]
+            (qo1, qo2, qo3)[g % 3][C * (g // 3) : C * (g // 3 + 1), :] = tile[:, 128 * k : 128 * (k + 1)]
     advance(late, 0)
     advance(early, 4)
     gga[...] = jnp.zeros_like(gga)
@@ -600,16 +644,16 @@
     advance(late, 1)
     lax.fori_loop(1, 2, dgrad_row, 0)
     halos[3].start(bw2.at[pl.ds(0, 6)], he2.at[pl.ds(0, 6)], 0, -1)
-    advance(early, 5)
     lax.fori_loop(2, 4, dgrad_row, 0)
     halos[3].start(bw2.at[pl.ds(6, 6)], he2.at[pl.ds(6, 6)], 0, -1)
-    advance(late, 2)
-    advance(early, 6)
+    advance(early, 5)
     lax.fori_loop(0, C2 // 256, merged_tile, 0)
     stores = [
         pltpu.make_async_copy(src, dst, lsem.at[5 + n])
         for n, (src, dst) in enumerate(
-            [(merged_ref, merged_out), (gtok_ref, gtok_out), (outm_ref, outm_out), (outq_ref, outq_out)]
+            [(merged_ref, merged_out), (gtok_ref, gtok_out)]
+            + [(om, outm_out.at[:, 384 * k : 384 * k + om.shape[1]]) for k, om in enumerate((om0, om1, om2))]
+            + [(oq, outq_out.at[:, 128 * k : 128 * (k + 1)]) for k, oq in enumerate((oq0, oq1, oq2, oq3))]
         )
     ]
     stores[0].start()
@@ -619,10 +663,7 @@
         small[0, 1 + n : 2 + n, :] = ggm[:, C * n : C * (n + 1)]
     gains = SmallSum(at, small, slots, ssend, srecv)
     gains.begin(0)
-    advance(late, 3)
-    gains.end(0)
-    gains.begin(1)
-    advance(late, 4)
+    advance(early, 6)
     for copy in halos[3].copies:
         copy.wait_recv()
     for r in range(3):
@@ -631,20 +672,27 @@
         edge = pair_half(he2, (r + 3) // 2, (r + 3) % 2) + gmix[r, 32:48, :].astype(F32)[8:16]
         gtok_ref[r, 40:48, :] = jnp.where(lower, gtok_ref[r, 40:48, :], edge)
     stores[1].start()
+    gains.end(0)
+    gains.begin(1)
+    advance(late, 2)
     gains.end(1)
     gains.begin(2)
-    advance(late, 5)
+    advance(late, 3)
     gains.end(2)
     gains.begin(3)
+    advance(late, 4)
+    gains.end(3)
+    outs_ref[...] = small[4]
+    advance(late, 5)
     advance(early, 7)
     advance(late, 6)
-    gains.end(3)
-    outs_ref[...] = small[4]
+    advance(late, 7)
     advance(early, 8)
-    stores[2].start()
-    advance(late, 7)
+    for store in stores[2:6]:
+        store.start()
     advance(late, 8)
-    stores[3].start()
+    for store in stores[6:]:
+        store.start()
     gains.finish()
     for halo in halos:
         halo.left()
@@ -659,6 +707,7 @@
     sums = []
     for n in lanes:
         sums += sum_scratch(TALL, n)
+    wide = [pltpu.VMEM((TALL, n), BF) for n in lanes]
     return pl.pallas_call(
         step_body,
         in_specs=[hbm, vmem, vmem, hbm, hbm, hbm, hbm, vmem],
@@ -673,8 +722,7 @@
         scratch_shapes=[
             pltpu.VMEM((ROWS // 2, COLS // 2, C2), BF),
             pltpu.VMEM((ROWS, COLS, C), F32),
-            pltpu.VMEM((C4, C2), BF),
-            pltpu.VMEM((TALL, C), BF),
+            *wide,
             pltpu.VMEM((27, COLS, C), BF),
             pltpu.VMEM((14, 16, C), BF),
             pltpu.VMEM((12, 16, C), BF),
@@ -697,8 +745,7 @@
             pltpu.VMEM((MALL, 1), F32),
             pltpu.VMEM((MALL, C4), BF),
             pltpu.VMEM((MALL, C4), BF),
-            pltpu.VMEM((C4, C2), BF),
-            pltpu.VMEM((TALL, C), BF),
+            *wide,
             pltpu.VMEM((ROWS, COLS, C), BF),
             pltpu.VMEM((27, COLS, C), BF),
             pltpu.VMEM((14, 16, C), BF),
@@ -714,7 +761,7 @@
             pltpu.VMEM((1, C4), F32),
             pltpu.VMEM((1, C), F32),
             pltpu.VMEM((WROWS, WIN, 2 * WIN), F32),
-            pltpu.SemaphoreType.DMA((9,)),
+            pltpu.SemaphoreType.DMA((14,)),
             pltpu.SemaphoreType.DMA((4, 6)),
             pltpu.SemaphoreType.DMA((4, 6)),
             pltpu.SemaphoreType.DMA((7, SUM_COPIES)),

time: 117 us -> 124 us (1.060)
  Pallas kernels: 114 us -> 121 us
    pallas_call x1, Pallas kernels: 106 us -> 113 us  [step_kernel(): pl.pallas_call(step_body, in_specs=[hbm, vmem, vmem, hbm, hbm, hbm, hbm,...]
where the time goes in v8:
time: 124 us
  Pallas kernels  121 us (98%)
  local copies, waits for them, and re-layouts  2.23 us (2%)
    pallas_call x1, Pallas kernels, step_kernel(): pl.pallas_call(step_body, in_specs=[hbm, vmem, vmem, hbm, hbm, hbm, hbm,...  113 us
    pallas_call x1, Pallas kernels, widen(): pl.pallas_call(widen_body, grid=(4,), in_specs=[pl.BlockSpec((C, C2), lam...  8 us

profile of v8, /device:TPU:1, one launch (start us, length us, event | category | flops | bytes accessed | tf_op | source)
XLA Modules:
  0.0 123.5 jit_solution(16812075284823393284)
XLA Ops:
  0.6 112.6 %step.1 = (bf16[12,24,1024]{2,1,0:T(8,128)(2,1)}, f32[24,48,512]{2,1,0:T(8,128)}, bf16[2048,1024]{1,0:T(8,128)(2,1)}, bf16[2048,512]{1,0:T(8,128)(2,1)}, f32[8,512]{1,0:T(8,128)}) custom-call(bf16[24,48,512]{2,1,0:T(8,128)(2,1)} %tok_hbm.1, s32[1,192]{1,0:T(1,128)} %bitcast.7, f32[1,512]{1,0:T(1,128)} %bitcast.6, bf16[512,1536]{1,0:T(8,128)(2,1)} %wq_hbm.1, ...), custom_call_target="tpu_custom_call" | custom-call | tf_op jit(solution)/shard_map/step/pallas_call | solution.py:711
  113.3 0.0 copy-start.1
  113.3 0.0 copy-start
  113.3 8.0 %widen.1 = (f32[2048,1024]{1,0:T(8,128)}, f32[512,1536]{1,0:T(8,128)}, f32[512,512]{1,0:T(8,128)}, f32[1,512]{1,0:T(1,128)}, f32[1,2048]{1,0:T(1,128)}) custom-call(bf16[2048,1024]{1,0:T(8,128)(2,1)} %get-tuple-element.19.m_ref, bf16[2048,512]{1,0:T(8,128)(2,1)} %get-tuple-element.20.q_ref, f32[8,512]{1,0:T(8,128)} %get-tuple-element.21.s_ref), custom_call_target="tpu_custom_call" | custom-call | tf_op jit(solution)/shard_map/widen/pallas_call | solution.py:790
  121.3 0.0 copy-done.1
  121.3 0.8 copy.17
  122.1 0.0 copy-done
  122.1 1.4 %copy.18 = f32[24,48,512]{2,1,0:T(8,128)} copy(f32[24,48,512]{2,1,0:T(8,128)S(1)} %copy-done) | data formatting | bytes 4718592
Async XLA Ops:
  113.3 8.0 %copy-start.1 = (bf16[12,24,1024]{2,1,0:T(8,128)(2,1)S(1)}, bf16[12,24,1024]{2,1,0:T(8,128)(2,1)}, u32[]{:S(2)}) copy-start(bf16[12,24,1024]{2,1,0:T(8,128)(2,1)} %get-tuple-element.34) | copy-start | bytes 1769476
  113.3 8.8 %copy-start = (f32[24,48,512]{2,1,0:T(8,128)S(1)}, f32[24,48,512]{2,1,0:T(8,128)}, u32[]{:S(2)}) copy-start(f32[24,48,512]{2,1,0:T(8,128)} %get-tuple-element.35) | copy-start | bytes 7077892
